TPU v7x, 256 devices: a whole 4x4x8 slice. The times are simulated.
256 devices in a mesh: dp: 16 (over z, core), mp: 16 (over x, y).
Axes of the slice: x: 4, y: 4, z: 8, core: 2. Of those that a mesh axis runs over, the one named last changes fastest.
Arguments:
- grad_parts: bfloat16 [16, 512, 256, 256], P('dp', 'mp'), may hold values from -0.25 to 0.25
- left_stats: float32 [16, 16, 4, 256, 256], P('dp', 'mp'), may hold values from -6 to 6
- right_stats: float32 [16, 16, 4, 256, 256], P('dp', 'mp'), may hold values from -6 to 6
- left_root: bfloat16 [16, 16, 4, 256, 256], P('dp', 'mp'), may hold values from -4 to 4
- right_root: bfloat16 [16, 16, 4, 256, 256], P('dp', 'mp'), may hold values from -4 to 4
- owners: int32 [512], replicated, may hold values from 0 to 15, as said below
Outputs:
- direction: bfloat16 [512, 256, 256], P('mp')
- left_updated: float32 [16, 16, 4, 256, 256], P('dp', 'mp')
- right_updated: float32 [16, 16, 4, 256, 256], P('dp', 'mp')
Inputs may be any that keep to these rules, and one draw needn't show every extreme that they name: The blocks b with the same b // 2 have distinct owners. Among the blocks of one row, no owner is named more than 4 times, and in every row some owner is named exactly 4 times.
All inputs are finite; a program needn't handle non-finite values.
Results may differ from a plain program's by a relative error of at most 0.02.
Values may be sent and summed in bfloat16 or wider, within the bound.
No kernel may reach another device: no remote copies, remote signals or barrier semaphores. Data moves between devices by JAX's collectives and lax.ppermute only.
A program may use at most 64 MiB of HBM per device.

v0:
```python
import jax
import jax.numpy as jnp
from jax import lax
from jax.sharding import Mesh
from jax.sharding import PartitionSpec as P

DP = ("dp_0", "dp_1")


def in_blocks(value, dim, peers):
    before, after = (value.shape[:dim], value.shape[dim + 1 :])
    return jnp.moveaxis(value.reshape(*before, peers, -1, *after), dim, 0)


def sum_by_chip(value, chips, core, dim):
    sizes = (lax.axis_size(chips), lax.axis_size(core))
    tiles = in_blocks(value, dim, sizes[0] * sizes[1])
    inside = tiles.shape[1:]
    tiles = tiles.reshape(*sizes, *inside).swapaxes(0, 1).reshape(-1, *inside)
    tiles = lax.psum_scatter(tiles, core, scatter_dimension=0, tiled=True)
    return lax.psum_scatter(tiles, chips, scatter_dimension=0, tiled=True)[0]


def per_device(grad_parts, left_stats, right_stats, left_root, right_root, owners):
    dp_count = lax.axis_size(DP)
    mp_count = lax.axis_size("mp")
    dp_index = lax.axis_index(DP)
    mp_index = lax.axis_index("mp")
    per_shard = grad_parts.shape[1]
    held_count = per_shard // dp_count
    slots_count = left_stats.shape[2]
    total_blocks = owners.shape[0]
    block_ids = jnp.arange(total_blocks, dtype=jnp.int32)
    row_of = block_ids % per_shard // held_count
    same_owner = owners[:, None] == owners[None, :]
    before = block_ids[None, :] < block_ids[:, None]
    slot_of = jnp.sum(
        ((row_of[:, None] == row_of[None, :]) & same_owner & before).astype(jnp.int32), axis=1
    )
    row_pos = jnp.arange(mp_count * held_count, dtype=jnp.int32)
    row_ids = row_pos // held_count * per_shard + dp_index * held_count + row_pos % held_count
    row_owner = jnp.take(owners, row_ids)
    row_slot = jnp.take(slot_of, row_ids)
    slot_ids = jnp.arange(slots_count, dtype=jnp.int32)
    mine_in = (row_owner[None, :] == mp_index) & (row_slot[None, :] == slot_ids[:, None])
    local_ids = (
        mp_index * per_shard + dp_index * held_count + jnp.arange(held_count, dtype=jnp.int32)
    )
    local_owner = jnp.take(owners, local_ids)
    shares = sum_by_chip(grad_parts[0], "dp_0", "dp_1", 0).astype(jnp.float32)
    held_blocks = shares.astype(jnp.bfloat16)
    targets = jnp.arange(mp_count, dtype=jnp.int32)
    send_map = (local_owner[None, :] == targets[:, None]).astype(jnp.bfloat16)
    row_holder = row_pos // held_count
    receive_map = jnp.any(
        mine_in[:, :, None] & (row_holder[None, :, None] == targets[None, None, :]), axis=1
    ).astype(jnp.bfloat16)
    packed = jnp.einsum(
        "qj,jxy->qxy", send_map, held_blocks, preferred_element_type=jnp.float32
    ).astype(jnp.bfloat16)
    arrived = lax.all_to_all(packed, "mp", split_axis=0, concat_axis=0, tiled=True)
    owned_grad = jnp.einsum(
        "sq,qxy->sxy", receive_map, arrived, preferred_element_type=jnp.float32
    ).astype(jnp.bfloat16)
    left_updated = left_stats[0, 0] + jnp.einsum(
        "sik,sjk->sij", owned_grad, owned_grad, preferred_element_type=jnp.float32
    )
    right_updated = right_stats[0, 0] + jnp.einsum(
        "ski,skj->sij", owned_grad, owned_grad, preferred_element_type=jnp.float32
    )
    half_step = jnp.einsum(
        "sik,skj->sij", left_root[0, 0], owned_grad, preferred_element_type=jnp.float32
    ).astype(jnp.bfloat16)
    precond = jnp.einsum(
        "sik,skj->sij", half_step, right_root[0, 0], preferred_element_type=jnp.float32
    ).astype(jnp.bfloat16)
    out_packed = jnp.einsum(
        "sq,sxy->qxy", receive_map, precond, preferred_element_type=jnp.float32
    ).astype(jnp.bfloat16)
    came_back = lax.all_to_all(out_packed, "mp", split_axis=0, concat_axis=0, tiled=True)
    returned = jnp.einsum(
        "qj,qxy->jxy", send_map, came_back, preferred_element_type=jnp.float32
    ).astype(jnp.bfloat16)
    direction = lax.all_gather(returned, DP, axis=0, tiled=True)
    return (direction, left_updated[None, None], right_updated[None, None])


def solution(mesh):
    split = Mesh(mesh.devices.reshape(8, 2, mesh.shape["mp"]), ("dp_0", "dp_1", "mp"))
    in_specs = (
        P(DP, "mp", None, None),
        P(DP, "mp", None, None, None),
        P(DP, "mp", None, None, None),
        P(DP, "mp", None, None, None),
        P(DP, "mp", None, None, None),
        P(),
    )
    out_specs = (P("mp", None, None), P(DP, "mp", None, None, None), P(DP, "mp", None, None, None))
    return jax.shard_map(
        per_device, mesh=split, in_specs=in_specs, out_specs=out_specs, check_vma=False
    )
```

profile of v0, /device:TPU:1, one launch (start us, length us, event | category | flops | bytes accessed | tf_op | source)
XLA Modules:
  0.0 201.7 jit_solution(8462344840040544123)
XLA Ops:
  7.2 0.0 copy-start
  7.2 0.0 reduce-scatter.3.cloned.1.call-start
  7.2 4.7 %copy.43 = bf16[2,8,2,256,256]{4,3,2,1,0:T(8,128)(2,1)} copy(bf16[2,8,2,256,256]{4,3,2,0,1:T(8,128)(2,1)} %bitcast.35) | data formatting | bytes 8388608 | tf_op jit(solution)/shard_map/transpose | solution.py:19
  11.9 0.0 reduce-scatter.3.cloned.1.call-update
  11.9 0.0 copy-start.1
  11.9 0.0 reduce-scatter.5.cloned.1.call-start
  12.0 21.8 %reduce-scatter.3.cloned.1.call-done = bf16[8,2,256,256]{3,2,1,0:T(8,128)(2,1)} async-done(((bf16[16,2,256,256]{3,2,1,0:T(8,128)(2,1)}), bf16[8,2,256,256]{3,2,1,0:T(8,128)(2,1)}) %reduce-scatter.3.cloned.1.call-update) | async-done | bytes 2097168 | tf_op jit(solution)/shard_map/reduce_scatter | solution.py:20
  33.8 0.0 reduce-scatter.5.cloned.1.call-update
  33.9 0.0 copy-done.1
  33.9 0.6 gather_fusion
  34.5 40.7 %reduce-scatter.5.cloned.1.call-done = bf16[1,2,256,256]{3,2,1,0:T(8,128)(2,1)} async-done(((bf16[8,2,256,256]{3,2,1,0:T(8,128)(2,1)}), bf16[1,2,256,256]{3,2,1,0:T(8,128)(2,1)}) %reduce-scatter.5.cloned.1.call-update) | async-done | bytes 262160 | tf_op jit(solution)/shard_map/reduce_scatter | solution.py:21
  75.3 1.8 convolution_convert_fusion.1
  77.1 2.0 %copy.45 = bf16[16,256,256]{2,1,0:T(8,128)(2,1)} copy(bf16[16,256,256]{2,0,1:T(8,128)(2,1)S(1)} %convolution_convert_fusion.1) | data formatting | bytes 4194304 | tf_op jit(solution)/shard_map/convert_element_type | solution.py:60
  79.1 6.7 %all-to-all-start = ((bf16[16,256,256]{2,1,0:T(8,128)(2,1)}), bf16[16,256,256]{2,1,0:T(8,128)(2,1)S(1)}, u32[]{:S(2)}, u32[]{:S(2)}) async-start(bf16[16,256,256]{2,1,0:T(8,128)(2,1)} %copy.45), calls=%async_computation.2 | async-start | bytes 4194304 | tf_op jit(solution)/shard_map/all_to_all | solution.py:61
  85.8 0.0 all-gather.2.cloned.1.call-start
  85.9 0.7 gather_fusion.1
  86.6 0.3 convert_reduce_fusion
  87.0 0.7 gather_fusion.2
  87.7 0.2 and_reduce_fusion
  87.9 21.4 %all-to-all-done = bf16[16,256,256]{2,1,0:T(8,128)(2,1)S(1)} async-done(((bf16[16,256,256]{2,1,0:T(8,128)(2,1)}), bf16[16,256,256]{2,1,0:T(8,128)(2,1)S(1)}, u32[]{:S(2)}, u32[]{:S(2)}) %all-to-all-start) | async-done | bytes 2097184 | tf_op jit(solution)/shard_map/all_to_all | solution.py:61
  109.3 1.3 fusion.6
  110.6 0.3 copy.47
  110.9 0.0 copy-done
  111.0 1.6 convolution_convert_fusion.2
  112.6 0.8 convolution_convert_fusion
  113.4 0.7 copy.50
  114.1 31.6 %all_to_all.10 = bf16[16,256,256]{2,1,0:T(8,128)(2,1)S(1)} all-to-all(bf16[16,256,256]{2,1,0:T(8,128)(2,1)S(1)} %copy.50), channel_id=1, replica_groups=mesh['dp_0'=8,'dp_1'=2,'mp'=16] {'mp'}, dimensions={0} | all-to-all | bytes 4194304 | tf_op jit(solution)/shard_map/all_to_all | solution.py:80
  145.7 1.3 fusion.9
  147.0 0.0 copy-start.2
  147.0 0.7 copy.52
  147.8 0.0 all-gather.2.cloned.1.call-update
  147.8 2.5 %fusion.5 = f32[1,1,4,256,256]{4,3,2,1,0:T(8,128)} fusion(f32[1,1,4,256,256]{4,3,2,1,0:T(8,128)} %param.9, bf16[4,256,256]{2,0,1:T(4,128)(2,1)S(1)} %fusion.6), kind=kOutput, calls=%fused_computation.12 | convolution fusion | flops 134479872 | bytes 2621440 | tf_op jit(solution)/shard_map/sik,sjk->sij/dot_general | solution.py:65
  150.3 0.0 copy-done.2
  150.3 1.3 fusion.4
  151.6 38.9 %all-gather.2.cloned.1.call-done = bf16[32,256,256]{2,1,0:T(8,128)(2,1)} async-done(((bf16[2,256,256]{2,1,0:T(8,128)(2,1)}), bf16[32,256,256]{2,1,0:T(8,128)(2,1)}) %all-gather.2.cloned.1.call-update) | async-done | bytes 4194320 | tf_op jit(solution)/shard_map/all_gather | solution.py:84
  190.6 4.6 %copy.75 = bf16[32,256,256]{2,1,0:T(8,128)(2,1)} copy(bf16[32,256,256]{2,1,0:T(8,128)(2,1)} %all-gather.2.cloned.1.call-done) | data formatting | bytes 8388608
  (11 shorter events, 0.1 us)
Async XLA Ops:
  7.2 103.8 %copy-start = (bf16[1,1,4,256,256]{4,3,2,1,0:T(8,128)(2,1)S(1)}, bf16[1,1,4,256,256]{4,3,2,1,0:T(8,128)(2,1)}, u32[]{:S(2)}) copy-start(bf16[1,1,4,256,256]{4,3,2,1,0:T(8,128)(2,1)} %param.12) | copy-start | bytes 1572868
  7.2 26.6 %reduce-scatter.3.cloned.1.call-start = ((), (), s32[]{:S(2)}) async-start(), calls=%async_computation.4 | async-start | bytes 6291456 | tf_op jit(solution)/shard_map/reduce_scatter | solution.py:20
  11.9 21.9 %copy-start.1 = (s32[512]{0:T(512)S(1)}, s32[512]{0:T(512)}, u32[]{:S(2)}) copy-start(s32[512]{0:T(512)} %param.13) | copy-start | bytes 6148
  11.9 63.3 %reduce-scatter.5.cloned.1.call-start = ((), (), s32[]{:S(2)}) async-start(), calls=%async_computation.5 | async-start | bytes 2359296 | tf_op jit(solution)/shard_map/reduce_scatter | solution.py:21
  79.1 30.2 %all-to-all-start = ((bf16[16,256,256]{2,1,0:T(8,128)(2,1)}), bf16[16,256,256]{2,1,0:T(8,128)(2,1)S(1)}, u32[]{:S(2)}, u32[]{:S(2)}) async-start(bf16[16,256,256]{2,1,0:T(8,128)(2,1)} %copy.45), calls=%async_computation.2 | async-start | bytes 4194304 | tf_op jit(solution)/shard_map/all_to_all | solution.py:61
  85.8 104.7 %all-gather.2.cloned.1.call-start = ((), (), s32[]{:S(2)}) async-start(), calls=%async_computation.6 | async-start | bytes 4456448 | tf_op jit(solution)/shard_map/all_gather | solution.py:84
  147.0 3.3 %copy-start.2 = (f32[1,1,4,256,256]{4,3,2,1,0:T(8,128)S(1)}, f32[1,1,4,256,256]{4,3,2,1,0:T(8,128)}, u32[]{:S(2)}) copy-start(f32[1,1,4,256,256]{4,3,2,1,0:T(8,128)} %param.10) | copy-start | bytes 3145732
Sparse Core Ops, SparseCore 0:
  12.1 21.7 reduce-scatter.2
  36.5 38.6 reduce-scatter.4
  147.9 42.6 all-gather.1
where the time goes:
time: 202 us
  waiting for transfers between devices  123 us (61%)
  blocking collectives  31.6 us (16%)
  local copies, waits for them, and re-layouts  15.2 us (8%)
  between operations  13.9 us (7%)
  matrix products  10.6 us (5%)
  starting transfers between devices  6.84 us (3%)
    reduce_scatter x1, waiting for transfers between devices, sum_by_chip(): return lax.psum_scatter(tiles, chips, scatter_dimension=0, tiled=True)[0]  40.7 us
    all_gather x1, waiting for transfers between devices, per_device(): direction = lax.all_gather(returned, DP, axis=0, tiled=True)  38.9 us
    all_to_all x1, blocking collectives, per_device(): lax.all_to_all(out_packed, 'mp', split_axis=0, concat_axis=0, tiled=True)  31.6 us
    reduce_scatter x1, waiting for transfers between devices, sum_by_chip(): tiles = lax.psum_scatter(tiles, core, scatter_dimension=0, tiled=True)  21.8 us
    all_to_all x1, waiting for transfers between devices, per_device(): lax.all_to_all(packed, 'mp', split_axis=0, concat_axis=0, tiled=True)  21.4 us
    all_to_all x1, starting transfers between devices, per_device(): lax.all_to_all(packed, 'mp', split_axis=0, concat_axis=0, tiled=True)  6.72 us
    transpose x1, local copies, waits for them, and re-layouts, sum_by_chip(): tiles = tiles.reshape(*sizes, *inside).swapaxes(0, 1).reshape(-1, *inside)  4.69 us
    unnamed x7, local copies, waits for them, and re-layouts  4.66 us
  transfers between devices with their start and end apart: 4, of which 4 were waited for; matrix products, arithmetic and copies ran while one was open for 3% of the time, Pallas kernels for 0%

commit v1 on v0

v1 whole, which is shorter than its diff:
```python
import jax
import jax.numpy as jnp
from jax import lax
from jax.experimental import pallas as pl
from jax.experimental.pallas import tpu as pltpu
from jax.sharding import Mesh
from jax.sharding import PartitionSpec as P

DP = ("z", "core")
F32 = jnp.float32
BF16 = jnp.bfloat16


def pick_kernel(src_ref, val_ref, out_ref):
    def one(i, carry):
        src = src_ref[i]
        piece = val_ref[jnp.maximum(src, 0)]
        out_ref[i] = jnp.where(src >= 0, piece, jnp.zeros_like(piece))
        return carry

    lax.fori_loop(0, out_ref.shape[0], one, 0, unroll=8)


def pick(src, values, count):
    return pl.pallas_call(
        pick_kernel,
        out_shape=jax.ShapeDtypeStruct((count, *values.shape[1:]), values.dtype),
        in_specs=[
            pl.BlockSpec(memory_space=pltpu.SMEM),
            pl.BlockSpec(memory_space=pltpu.VMEM),
        ],
        out_specs=pl.BlockSpec(memory_space=pltpu.VMEM),
        name="pick",
    )(src, values)


def precond_kernel(own_ref, left_ref, right_ref, out_ref):
    peers, _, rows, cols = own_ref.shape
    for s in range(own_ref.shape[1]):
        own = own_ref[:, s].reshape(peers * rows, cols)
        half = jnp.dot(left_ref[s], own, preferred_element_type=F32).astype(BF16)
        full = jnp.dot(half, right_ref[s], preferred_element_type=F32).astype(BF16)
        out_ref[:, s] = full.reshape(peers, rows, cols)


def precondition(own, left_root, right_root):
    vmem = pl.BlockSpec(memory_space=pltpu.VMEM)
    return pl.pallas_call(
        precond_kernel,
        out_shape=jax.ShapeDtypeStruct(own.shape, BF16),
        in_specs=[vmem, vmem, vmem],
        out_specs=vmem,
        name="precond",
    )(own, left_root, right_root)


def per_device(grad_parts, left_stats, right_stats, left_root, right_root, owners):
    zs = lax.axis_size("z")
    mp = lax.axis_size("mp")
    z = lax.axis_index("z")
    core = lax.axis_index("core")
    dp = z * 2 + core
    _, per_shard, rows, cols = grad_parts.shape
    held = per_shard // (2 * zs)
    slots = left_stats.shape[2]
    piece = rows // mp
    up = [(i, (i + 1) % zs) for i in range(zs)]
    down = [(i, (i - 1) % zs) for i in range(zs)]
    swap = [(0, 1), (1, 0)]
    grads = grad_parts.reshape(zs, 2, held, rows, cols)

    row_owner = lax.dynamic_index_in_dim(
        owners.reshape(mp, 2 * zs, held), dp, 1, keepdims=False
    ).reshape(mp * held)
    pos = jnp.arange(mp * held, dtype=jnp.int32)
    same = (row_owner[:, None] == row_owner[None, :]) & (pos[None, :] < pos[:, None])
    row_slot = jnp.sum(same.astype(jnp.int32), axis=1)
    key = row_owner * slots + row_slot
    keys = jnp.arange(mp * slots, dtype=jnp.int32)
    hit = keys[:, None] == key[None, :]
    source = jnp.sum(jnp.where(hit, pos[None, :] + 1, 0), axis=1) - 1

    other = [
        lax.ppermute(
            lax.dynamic_slice(
                grads, (0, 1 - core, j, 0, 0), (zs, 1, 1, rows, cols)
            ).reshape(zs, rows, cols),
            "core",
            swap,
        )
        for j in range(held)
    ]

    def base(step, j):
        at = (z + step) % zs
        mine = lax.dynamic_slice(grads, (at, core, j, 0, 0), (1, 1, 1, rows, cols))
        theirs = lax.dynamic_slice(other[j], (at, 0, 0), (1, rows, cols))
        return mine.reshape(rows, cols).astype(F32) + theirs.reshape(rows, cols).astype(F32)

    far = zs // 2
    left = [[far - (j % 2 == 1), far - (j % 2 == 0)] for j in range(held)]
    moving = [
        [base(left[j][0], j).astype(BF16), base(-left[j][1], j).astype(BF16)] for j in range(held)
    ]
    ended = [[None, None] for _ in range(held)]
    for _ in range(far):
        for j in range(held):
            for way in range(2):
                if left[j][way] == 0:
                    continue
                came = lax.ppermute(moving[j][way], "z", up if way == 0 else down)
                left[j][way] -= 1
                if left[j][way] == 0:
                    ended[j][way] = came
                else:
                    step = left[j][way] if way == 0 else -left[j][way]
                    moving[j][way] = (came.astype(F32) + base(step, j)).astype(BF16)
    blocks = jnp.stack(
        [
            (ended[j][0].astype(F32) + ended[j][1].astype(F32) + base(0, j))
            .astype(BF16)
            .reshape(mp, piece, cols)
            for j in range(held)
        ],
        axis=1,
    )

    sliced = lax.all_to_all(blocks, "mp", 0, 0, tiled=True)
    to_owner = pick(source, sliced.reshape(mp * held, piece, cols), mp * slots)
    own = lax.all_to_all(to_owner.reshape(mp, slots, piece, cols), "mp", 0, 0, tiled=True)
    result = precondition(own, left_root[0, 0], right_root[0, 0])
    back = lax.all_to_all(result, "mp", 0, 0, tiled=True)
    to_holder = pick(key, back.reshape(mp * slots, piece, cols), mp * held)
    home = lax.all_to_all(to_holder.reshape(mp, held, piece, cols), "mp", 0, 0, tiled=True)

    owned = own.swapaxes(0, 1).reshape(slots, rows, cols)
    left_updated = left_stats[0, 0] + jnp.einsum(
        "sik,sjk->sij", owned, owned, preferred_element_type=F32
    )
    right_updated = right_stats[0, 0] + jnp.einsum(
        "ski,skj->sij", owned, owned, preferred_element_type=F32
    )

    direction = jnp.zeros((zs, 2, held, rows, cols), BF16)

    def place(direction, value, other_value, step, j):
        at = (z + step) % zs
        for where, val in ((core, value), (1 - core, other_value)):
            direction = lax.dynamic_update_slice(
                direction, val.reshape(1, 1, 1, rows, cols), (at, where, j, 0, 0)
            )
        return direction

    mine = [home[:, j].reshape(rows, cols) for j in range(held)]
    moving = [[mine[j], mine[j]] for j in range(held)]
    for j in range(held):
        direction = place(direction, mine[j], lax.ppermute(mine[j], "core", swap), 0, j)
    for step in range(1, far + 1):
        for j in range(held):
            for way in range(2):
                if step == far and way != j % 2:
                    continue
                moving[j][way] = lax.ppermute(moving[j][way], "z", up if way == 0 else down)
                direction = place(
                    direction,
                    moving[j][way],
                    lax.ppermute(moving[j][way], "core", swap),
                    -step if way == 0 else step,
                    j,
                )
    return (
        direction.reshape(per_shard, rows, cols),
        left_updated[None, None],
        right_updated[None, None],
    )


def solution(mesh):
    split = Mesh(mesh.devices.reshape(-1, 2, mesh.shape["mp"]), ("z", "core", "mp"))
    held = P(DP, "mp", None, None, None)
    in_specs = (P(DP, "mp", None, None), held, held, held, held, P())
    out_specs = (P("mp", None, None), held, held)
    return jax.shard_map(
        per_device, mesh=split, in_specs=in_specs, out_specs=out_specs, check_vma=False
    )
```

time: 202 us -> 179 us (0.89)
  waiting for transfers between devices: 123 us -> 51 us
  starting transfers between devices: 6.84 us -> 72.4 us
  between operations: 13.9 us -> 1.18 us
  other arithmetic: 0.55 us -> 12.4 us
  local copies, waits for them, and re-layouts: 15.2 us -> 5.72 us
  matrix products: 10.6 us -> 2.62 us
  Pallas kernels: 0 us -> 6.61 us
  blocking collectives: 31.6 us -> 26.4 us
    reduce_scatter x2 -> x0, waiting for transfers between devices: 62.6 us -> none  [the longest x1 40.7 us: sum_by_chip(): return lax.psum_scatter(tiles, chips, scatter_dimension=0, tiled=True)[0]]
    ppermute x0 -> x46, starting transfers between devices: none -> 62.1 us  [the longest x14 19.1 us: per_device(): came = lax.ppermute(moving[j][way], 'z', up if way == 0 else down)]
    all_gather x1 -> x0, waiting for transfers between devices: 38.9 us -> none  [per_device(): direction = lax.all_gather(returned, DP, axis=0, tiled=True)]
    ppermute x0 -> x46, waiting for transfers between devices: none -> 38.3 us  [the longest x14 29 us: per_device(): came = lax.ppermute(moving[j][way], 'z', up if way == 0 else down)]
    convert_element_type x0 -> x9, other arithmetic: none -> 10.8 us  [the longest x5 6.75 us: per_device(): moving[j][way] = (came.astype(F32) + base(step, j)).astype(BF16)]
    all_to_all x1 -> x2, waiting for transfers between devices: 21.4 us -> 12.7 us  [the longest x1 6.65 us: per_device(): sliced = lax.all_to_all(blocks, 'mp', 0, 0, tiled=True)]
    dot_general x7 -> x2, matrix products: 10.6 us -> 2.62 us  [the longest x1 1.32 us: per_device(): jnp.einsum('ski,skj->sij', owned, owned, preferred_element_type=F32)]
    pallas_call x0 -> x3, Pallas kernels: none -> 6.61 us  [the longest x2 3.8 us: pick(): pl.pallas_call(pick_kernel, out_shape=jax.ShapeDtypeStruct((count, *value...]
  transfers between devices with their start and end apart: 4 -> 48, of which waited for: 4 -> 17; matrix products, arithmetic and copies ran while one was open for 3% -> 5% of each run, Pallas kernels for 0% -> 0%
where the time goes in v1:
time: 179 us; the launch traced here: 178 us
  starting transfers between devices  72.4 us (40%)
  waiting for transfers between devices  51 us (28%)
  blocking collectives  26.4 us (15%)
  other arithmetic  12.4 us (7%)
  Pallas kernels  6.61 us (4%)
  local copies, waits for them, and re-layouts  5.72 us (3%)
  matrix products  2.62 us (1%)
    ppermute x14, waiting for transfers between devices, per_device(): came = lax.ppermute(moving[j][way], 'z', up if way == 0 else down)  29 us
    ppermute x14, starting transfers between devices, per_device(): came = lax.ppermute(moving[j][way], 'z', up if way == 0 else down)  19.1 us
    ppermute x14, starting transfers between devices, per_device(): moving[j][way] = lax.ppermute(moving[j][way], 'z', up if way == 0 else down)  17.2 us
    ppermute x2, starting transfers between devices, per_device(): lax.ppermute(mine[j], 'core', swap)  14 us
    all_to_all x1, blocking collectives, per_device(): back = lax.all_to_all(result, 'mp', 0, 0, tiled=True)  13.2 us
    all_to_all x1, blocking collectives, per_device(): lax.all_to_all(to_owner.reshape(mp, slots, piece, cols), 'mp', 0, 0, tile...  13.2 us
    ppermute x14, starting transfers between devices, per_device(): lax.ppermute(moving[j][way], 'core', swap)  8 us
    all_to_all x1, starting transfers between devices, per_device(): sliced = lax.all_to_all(blocks, 'mp', 0, 0, tiled=True)  6.75 us
  transfers between devices with their start and end apart: 48, of which 17 were waited for; matrix products, arithmetic and copies ran while one was open for 5% of the time, Pallas kernels for 0%

profile of v1, /device:TPU:1, one launch (start us, length us, event | category | flops | bytes accessed | tf_op | source)
XLA Modules:
  0.0 178.2 jit_solution(12853326248885748784)
XLA Ops:
  0.6 1.7 dynamic-slice_bitcast_fusion.1
  2.3 3.3 %collective-permute-start = (bf16[8,256,256]{2,1,0:T(8,128)(2,1)S(1)}, bf16[8,256,256]{2,1,0:T(8,128)(2,1)S(1)}, u32[]{:S(2)}, u32[]{:S(2)}) collective-permute-start(bf16[8,256,256]{2,1,0:T(8,128)(2,1)S(1)} %get-tuple-element.17), channel_id=1, source_target_pairs={{0,16},{16,0},{1,17},{17,1},{2,18},{18,2},{3,19},{19,3},{4,20},{20... | collective-permute-start | bytes 3145736 | tf_op jit(solution)/shard_map/ppermute | solution.py:84
  5.7 2.3 %collective-permute-done = bf16[8,256,256]{2,1,0:T(8,128)(2,1)S(1)} collective-permute-done((bf16[8,256,256]{2,1,0:T(8,128)(2,1)S(1)}, bf16[8,256,256]{2,1,0:T(8,128)(2,1)S(1)}, u32[]{:S(2)}, u32[]{:S(2)}) %collective-permute-start) | collective-permute-done | bytes 1048608 | tf_op jit(solution)/shard_map/ppermute | solution.py:84
  8.0 0.9 fusion.29
  9.5 6.9 %collective-permute-done.1 = bf16[256,256]{1,0:T(8,128)(2,1)S(1)} collective-permute-done((bf16[256,256]{1,0:T(8,128)(2,1)S(1)}, bf16[256,256]{1,0:T(8,128)(2,1)S(1)}, u32[]{:S(2)}, u32[]{:S(2)}) %collective-permute-start.1) | collective-permute-done | bytes 131104 | tf_op jit(solution)/shard_map/ppermute | solution.py:111
  16.4 1.7 fusion.28
  18.1 2.7 %collective-permute-start.5 = (bf16[256,256]{1,0:T(8,128)(2,1)S(1)}, bf16[256,256]{1,0:T(8,128)(2,1)}, u32[]{:S(2)}, u32[]{:S(2)}) collective-permute-start(bf16[256,256]{1,0:T(8,128)(2,1)S(1)} %get-tuple-element.8), channel_id=1, source_target_pairs={{0,224},{32,0},{64,32},{96,64},{128,96},{160,128},{192,160},{224,1... | collective-permute-start | bytes 393224 | tf_op jit(solution)/shard_map/ppermute | solution.py:111
  20.8 2.9 %collective-permute-done.2 = bf16[256,256]{1,0:T(8,128)(2,1)S(1)} collective-permute-done((bf16[256,256]{1,0:T(8,128)(2,1)}, bf16[256,256]{1,0:T(8,128)(2,1)S(1)}, u32[]{:S(2)}, u32[]{:S(2)}) %collective-permute-start.2) | collective-permute-done | bytes 131104 | tf_op jit(solution)/shard_map/ppermute | solution.py:111
  23.6 1.1 fusion.26
  24.9 2.7 %collective-permute-start.6 = (bf16[256,256]{1,0:T(8,128)(2,1)S(1)}, bf16[256,256]{1,0:T(8,128)(2,1)}, u32[]{:S(2)}, u32[]{:S(2)}) collective-permute-start(bf16[256,256]{1,0:T(8,128)(2,1)S(1)} %get-tuple-element.6), channel_id=1, source_target_pairs={{0,224},{32,0},{64,32},{96,64},{128,96},{160,128},{192,160},{224,1... | collective-permute-start | bytes 393224 | tf_op jit(solution)/shard_map/ppermute | solution.py:111
  27.5 2.4 %collective-permute-done.3 = bf16[256,256]{1,0:T(8,128)(2,1)S(1)} collective-permute-done((bf16[256,256]{1,0:T(8,128)(2,1)S(1)}, bf16[256,256]{1,0:T(8,128)(2,1)S(1)}, u32[]{:S(2)}, u32[]{:S(2)}) %collective-permute-start.3) | collective-permute-done | bytes 131104 | tf_op jit(solution)/shard_map/ppermute | solution.py:111
  29.9 1.8 %fusion.24 = (bf16[256,256]{1,0:T(8,128)(2,1)}, bf16[256,256]{1,0:T(8,128)(2,1)S(1)}) fusion(bf16[256,256]{1,0:T(8,128)(2,1)S(1)} %collective-permute-done.3, bf16[8,256,256]{2,1,0:T(8,128)(2,1)S(1)} %collective-permute-done, s32[]{:T(128)S(6)} %select_n.240, bf16[8,2,2,256,256]{4,3,2,1,0:T(8,128)(2,1)} %bitcast.195, s32[]{:T(128)S(6)} %select_n.119, ...), kind=kLoop, calls=%fused_computation.42 | loop fusion | flops 786432 | bytes 1048588 | tf_op jit(solution)/shard_map/convert_element_type | solution.py:117
  31.7 1.5 collective-permute-start.4
  33.2 1.2 collective-permute-start.7
  34.4 2.6 %collective-permute-done.4 = bf16[256,256]{1,0:T(8,128)(2,1)S(1)} collective-permute-done((bf16[256,256]{1,0:T(8,128)(2,1)}, bf16[256,256]{1,0:T(8,128)(2,1)S(1)}, u32[]{:S(2)}, u32[]{:S(2)}) %collective-permute-start.4) | collective-permute-done | bytes 131104 | tf_op jit(solution)/shard_map/ppermute | solution.py:111
  37.2 1.1 fusion.17
  38.3 2.3 %collective-permute-start.12 = (bf16[256,256]{1,0:T(8,128)(2,1)S(1)}, bf16[256,256]{1,0:T(8,128)(2,1)S(1)}, u32[]{:S(2)}, u32[]{:S(2)}) collective-permute-start(bf16[256,256]{1,0:T(8,128)(2,1)S(1)} %get-tuple-element.16), channel_id=1, source_target_pairs={{0,224},{32,0},{64,32},{96,64},{128,96},{160,128},{192,160},{224,1... | collective-permute-start | bytes 393224 | tf_op jit(solution)/shard_map/ppermute | solution.py:111
  40.6 2.3 %collective-permute-done.12 = bf16[256,256]{1,0:T(8,128)(2,1)S(1)} collective-permute-done((bf16[256,256]{1,0:T(8,128)(2,1)S(1)}, bf16[256,256]{1,0:T(8,128)(2,1)S(1)}, u32[]{:S(2)}, u32[]{:S(2)}) %collective-permute-start.12) | collective-permute-done | bytes 131104 | tf_op jit(solution)/shard_map/ppermute | solution.py:111
  43.0 1.0 fusion.15
  44.0 2.8 %collective-permute-start.13 = (bf16[256,256]{1,0:T(8,128)(2,1)S(1)}, bf16[256,256]{1,0:T(8,128)(2,1)S(1)}, u32[]{:S(2)}, u32[]{:S(2)}) collective-permute-start(bf16[256,256]{1,0:T(8,128)(2,1)S(1)} %get-tuple-element.14), channel_id=1, source_target_pairs={{0,224},{32,0},{64,32},{96,64},{128,96},{160,128},{192,160},{224,1... | collective-permute-start | bytes 393224 | tf_op jit(solution)/shard_map/ppermute | solution.py:111
  46.8 2.6 %collective-permute-done.13 = bf16[256,256]{1,0:T(8,128)(2,1)S(1)} collective-permute-done((bf16[256,256]{1,0:T(8,128)(2,1)S(1)}, bf16[256,256]{1,0:T(8,128)(2,1)S(1)}, u32[]{:S(2)}, u32[]{:S(2)}) %collective-permute-start.13) | collective-permute-done | bytes 131104 | tf_op jit(solution)/shard_map/ppermute | solution.py:111
  49.4 2.4 %collective-permute-done.9 = bf16[256,256]{1,0:T(8,128)(2,1)S(1)} collective-permute-done((bf16[256,256]{1,0:T(8,128)(2,1)S(1)}, bf16[256,256]{1,0:T(8,128)(2,1)S(1)}, u32[]{:S(2)}, u32[]{:S(2)}) %collective-permute-start.9) | collective-permute-done | bytes 131104 | tf_op jit(solution)/shard_map/ppermute | solution.py:111
  51.8 1.1 fusion.14
  53.0 2.7 %collective-permute-start.14 = (bf16[256,256]{1,0:T(8,128)(2,1)S(1)}, bf16[256,256]{1,0:T(8,128)(2,1)S(1)}, u32[]{:S(2)}, u32[]{:S(2)}) collective-permute-start(bf16[256,256]{1,0:T(8,128)(2,1)S(1)} %get-tuple-element.12), channel_id=1, source_target_pairs={{0,224},{32,0},{64,32},{96,64},{128,96},{160,128},{192,160},{224,1... | collective-permute-start | bytes 393224 | tf_op jit(solution)/shard_map/ppermute | solution.py:111
  56.1 3.5 %collective-permute-done.10 = bf16[256,256]{1,0:T(8,128)(2,1)S(1)} collective-permute-done((bf16[256,256]{1,0:T(8,128)(2,1)S(1)}, bf16[256,256]{1,0:T(8,128)(2,1)S(1)}, u32[]{:S(2)}, u32[]{:S(2)}) %collective-permute-start.10) | collective-permute-done | bytes 131104 | tf_op jit(solution)/shard_map/ppermute | solution.py:111
  59.6 1.1 fusion.12
  60.9 2.7 %collective-permute-start.15 = (bf16[256,256]{1,0:T(8,128)(2,1)S(1)}, bf16[256,256]{1,0:T(8,128)(2,1)S(1)}, u32[]{:S(2)}, u32[]{:S(2)}) collective-permute-start(bf16[256,256]{1,0:T(8,128)(2,1)S(1)} %get-tuple-element.10), channel_id=1, source_target_pairs={{0,224},{32,0},{64,32},{96,64},{128,96},{160,128},{192,160},{224,1... | collective-permute-start | bytes 393224 | tf_op jit(solution)/shard_map/ppermute | solution.py:111
  63.6 3.3 %collective-permute-done.11 = bf16[256,256]{1,0:T(8,128)(2,1)S(1)} collective-permute-done((bf16[256,256]{1,0:T(8,128)(2,1)S(1)}, bf16[256,256]{1,0:T(8,128)(2,1)S(1)}, u32[]{:S(2)}, u32[]{:S(2)}) %collective-permute-start.11) | collective-permute-done | bytes 131104 | tf_op jit(solution)/shard_map/ppermute | solution.py:111
  66.9 1.0 fusion.3
  67.9 0.7 pad_maximum_fusion
  68.6 6.8 %all-to-all-start = ((bf16[16,2,16,256]{3,2,1,0:T(8,128)(2,1)}), bf16[16,2,16,256]{3,2,1,0:T(8,128)(2,1)S(1)}, u32[]{:S(2)}, u32[]{:S(2)}) async-start(bf16[16,2,16,256]{3,2,1,0:T(8,128)(2,1)} %pad_maximum_fusion), calls=%async_computation | async-start | bytes 524288 | tf_op jit(solution)/shard_map/all_to_all | solution.py:128
  76.1 6.6 %all-to-all-done = bf16[16,2,16,256]{3,2,1,0:T(8,128)(2,1)S(1)} async-done(((bf16[16,2,16,256]{3,2,1,0:T(8,128)(2,1)}), bf16[16,2,16,256]{3,2,1,0:T(8,128)(2,1)S(1)}, u32[]{:S(2)}, u32[]{:S(2)}) %all-to-all-start) | async-done | bytes 262176 | tf_op jit(solution)/shard_map/all_to_all | solution.py:128
  82.7 0.7 copy-done.4
  83.4 2.0 %pick.2 = bf16[64,16,256]{2,1,0:T(8,128)(2,1)} custom-call(s32[64]{0:T(128)} %broadcast_add_fusion.src_ref, bf16[32,16,256]{2,1,0:T(8,128)(2,1)} %bitcast.204), custom_call_target="tpu_custom_call" | custom-call | tf_op jit(solution)/shard_map/pick/pallas_call | solution.py:25
  85.4 13.2 %all_to_all.20.own_ref = bf16[16,4,16,256]{3,2,1,0:T(8,128)(2,1)} all-to-all(bf16[16,4,16,256]{3,2,1,0:T(8,128)(2,1)} %bitcast.202), channel_id=1, replica_groups=mesh['z'=8,'core'=2,'mp'=16] {'mp'}, dimensions={0} | all-to-all | bytes 1048576 | tf_op jit(solution)/shard_map/all_to_all | solution.py:130
  98.5 2.8 %precond.1 = bf16[16,4,16,256]{3,2,1,0:T(8,128)(2,1)} custom-call(bf16[16,4,16,256]{3,2,1,0:T(8,128)(2,1)} %all_to_all.20.own_ref, bf16[4,256,256]{2,1,0:T(8,128)(2,1)} %bitcast.216, bf16[4,256,256]{2,1,0:T(8,128)(2,1)} %bitcast.217), custom_call_target="tpu_custom_call" | custom-call | tf_op jit(solution)/shard_map/precond/pallas_call | solution.py:48
  101.3 13.2 %all_to_all.21 = bf16[16,4,16,256]{3,2,1,0:T(8,128)(2,1)} all-to-all(bf16[16,4,16,256]{3,2,1,0:T(8,128)(2,1)} %precond.1), channel_id=1, replica_groups=mesh['z'=8,'core'=2,'mp'=16] {'mp'}, dimensions={0} | all-to-all | bytes 1048576 | tf_op jit(solution)/shard_map/all_to_all | solution.py:132
  114.5 1.9 %pick.3 = bf16[32,16,256]{2,1,0:T(8,128)(2,1)} custom-call(s32[32]{0:T(128)} %copy-done.6, bf16[64,16,256]{2,1,0:T(8,128)(2,1)} %bitcast.203), custom_call_target="tpu_custom_call" | custom-call | tf_op jit(solution)/shard_map/pick/pallas_call | solution.py:25
  116.4 3.5 %all-to-all-start.3 = ((bf16[16,2,16,256]{3,2,1,0:T(8,128)(2,1)}), bf16[16,2,16,256]{3,2,1,0:T(8,128)(2,1)S(1)}, u32[]{:S(2)}, u32[]{:S(2)}) async-start(bf16[16,2,16,256]{3,2,1,0:T(8,128)(2,1)} %bitcast.205), calls=%async_computation.3 | async-start | bytes 524288 | tf_op jit(solution)/shard_map/all_to_all | solution.py:134
  120.0 1.3 fusion
  121.3 6.0 %all-to-all-done.3 = bf16[16,2,16,256]{3,2,1,0:T(8,128)(2,1)S(1)} async-done(((bf16[16,2,16,256]{3,2,1,0:T(8,128)(2,1)}), bf16[16,2,16,256]{3,2,1,0:T(8,128)(2,1)S(1)}, u32[]{:S(2)}, u32[]{:S(2)}) %all-to-all-start.3) | async-done | bytes 262176 | tf_op jit(solution)/shard_map/all_to_all | solution.py:134
  127.3 13.6 %collective-permute-start.16 = (bf16[256,256]{1,0:T(8,128)(2,1)S(1)}, bf16[256,256]{1,0:T(8,128)(2,1)S(1)}, u32[]{:S(2)}, u32[]{:S(2)}) collective-permute-start(bf16[256,256]{1,0:T(8,128)(2,1)S(1)} %bitcast.212), channel_id=1, source_target_pairs={{0,16},{16,0},{1,17},{17,1},{2,18},{18,2},{3,19},{19,3},{4,20},{20... | collective-permute-start | bytes 393224 | tf_op jit(solution)/shard_map/ppermute | solution.py:157
  141.0 2.5 %collective-permute-start.18 = (bf16[256,256]{1,0:T(8,128)(2,1)S(1)}, bf16[256,256]{1,0:T(8,128)(2,1)S(1)}, u32[]{:S(2)}, u32[]{:S(2)}) collective-permute-start(bf16[256,256]{1,0:T(8,128)(2,1)S(1)} %bitcast.213), channel_id=1, source_target_pairs={{0,32},{32,64},{64,96},{96,128},{128,160},{160,192},{192,224},{224... | collective-permute-start | bytes 393224 | tf_op jit(solution)/shard_map/ppermute | solution.py:163
  143.5 1.3 fusion.1
  144.8 1.3 collective-permute-start.20
  146.4 0.6 collective-permute-start.22
  147.5 2.2 %collective-permute-start.24 = (bf16[256,256]{1,0:T(8,128)(2,1)S(1)}, bf16[256,256]{1,0:T(8,128)(2,1)S(1)}, u32[]{:S(2)}, u32[]{:S(2)}) collective-permute-start(bf16[256,256]{1,0:T(8,128)(2,1)S(1)} %bitcast.210), channel_id=1, source_target_pairs={{0,224},{32,0},{64,32},{96,64},{128,96},{160,128},{192,160},{224,1... | collective-permute-start | bytes 393224 | tf_op jit(solution)/shard_map/ppermute | solution.py:163
  149.7 0.7 collective-permute-start.19
  150.6 0.6 collective-permute-start.21
  151.2 1.4 collective-permute-done.22
  152.6 1.1 collective-permute-start.28
  153.7 0.7 collective-permute-start.23
  154.4 1.0 collective-permute-start.30
  155.8 2.0 %collective-permute-start.32 = (bf16[256,256]{1,0:T(8,128)(2,1)S(1)}, bf16[256,256]{1,0:T(8,128)(2,1)S(1)}, u32[]{:S(2)}, u32[]{:S(2)}) collective-permute-start(bf16[256,256]{1,0:T(8,128)(2,1)S(1)} %collective-permute-done.24), channel_id=1, source_target_pairs={{0,224},{32,0},{64,32},{96,64},{128,96},{160,128},{192,160},{224,1... | collective-permute-start | bytes 393224 | tf_op jit(solution)/shard_map/ppermute | solution.py:163
  158.6 2.2 %collective-permute-done.30 = bf16[256,256]{1,0:T(8,128)(2,1)S(1)} collective-permute-done((bf16[256,256]{1,0:T(8,128)(2,1)S(1)}, bf16[256,256]{1,0:T(8,128)(2,1)S(1)}, u32[]{:S(2)}, u32[]{:S(2)}) %collective-permute-start.30) | collective-permute-done | bytes 131104 | tf_op jit(solution)/shard_map/ppermute | solution.py:163
  160.8 0.7 collective-permute-start.36
  162.1 1.4 collective-permute-start.38
  163.8 1.5 collective-permute-start.40
  166.3 2.7 %collective-permute-done.40 = bf16[256,256]{1,0:T(8,128)(2,1)S(1)} collective-permute-done((bf16[256,256]{1,0:T(8,128)(2,1)S(1)}, bf16[256,256]{1,0:T(8,128)(2,1)S(1)}, u32[]{:S(2)}, u32[]{:S(2)}) %collective-permute-start.40) | collective-permute-done | bytes 131104 | tf_op jit(solution)/shard_map/ppermute | solution.py:163
  169.0 2.3 %collective-permute-start.44 = (bf16[256,256]{1,0:T(8,128)(2,1)S(1)}, bf16[256,256]{1,0:T(8,128)(2,1)S(1)}, u32[]{:S(2)}, u32[]{:S(2)}) collective-permute-start(bf16[256,256]{1,0:T(8,128)(2,1)S(1)} %collective-permute-done.40), channel_id=1, source_target_pairs={{0,224},{32,0},{64,32},{96,64},{128,96},{160,128},{192,160},{224,1... | collective-permute-start | bytes 393224 | tf_op jit(solution)/shard_map/ppermute | solution.py:163
  171.4 1.4 collective-permute-start.41
  173.5 1.7 collective-permute-start.45
  175.5 0.7 collective-permute-done.45
  176.2 2.0 %copy-done.1 = bf16[8,2,2,256,256]{4,3,2,1,0:T(8,128)(2,1)} copy-done((bf16[8,2,2,256,256]{4,3,2,1,0:T(8,128)(2,1)}, bf16[8,2,2,256,256]{4,3,2,1,0:T(8,128)(2,1)S(1)}, u32[]{:S(2)}) %copy-start.1) | copy-done | bytes 4194328
  (107 shorter events, 7.4 us)
Async XLA Ops:
  2.3 53.3 %copy-start.5 = (s32[512]{0:T(512)S(1)}, s32[512]{0:T(512)}, u32[]{:S(2)}) copy-start(s32[512]{0:T(512)} %param.11) | copy-start | bytes 6148
  2.3 5.6 %collective-permute-start = (bf16[8,256,256]{2,1,0:T(8,128)(2,1)S(1)}, bf16[8,256,256]{2,1,0:T(8,128)(2,1)S(1)}, u32[]{:S(2)}, u32[]{:S(2)}) collective-permute-start(bf16[8,256,256]{2,1,0:T(8,128)(2,1)S(1)} %get-tuple-element.17), channel_id=1, source_target_pairs={{0,16},{16,0},{1,17},{17,1},{2,18},{18,2},{3,19},{19,3},{4,20},{20... | collective-permute-start | bytes 3145736 | tf_op jit(solution)/shard_map/ppermute | solution.py:84
  8.9 7.5 %collective-permute-start.1 = (bf16[256,256]{1,0:T(8,128)(2,1)S(1)}, bf16[256,256]{1,0:T(8,128)(2,1)S(1)}, u32[]{:S(2)}, u32[]{:S(2)}) collective-permute-start(bf16[256,256]{1,0:T(8,128)(2,1)S(1)} %fusion.29), channel_id=1, source_target_pairs={{0,32},{32,64},{64,96},{96,128},{128,160},{160,192},{192,224},{224... | collective-permute-start | bytes 393224 | tf_op jit(solution)/shard_map/ppermute | solution.py:111
  9.0 25.5 %collective-permute-start.8 = (bf16[8,256,256]{2,1,0:T(8,128)(2,1)S(1)}, bf16[8,256,256]{2,1,0:T(8,128)(2,1)S(1)}, u32[]{:S(2)}, u32[]{:S(2)}) collective-permute-start(bf16[8,256,256]{2,1,0:T(8,128)(2,1)S(1)} %get-tuple-element.18), channel_id=1, source_target_pairs={{0,16},{16,0},{1,17},{17,1},{2,18},{18,2},{3,19},{19,3},{4,20},{20... | collective-permute-start | bytes 3145736 | tf_op jit(solution)/shard_map/ppermute | solution.py:84
  18.1 5.6 %collective-permute-start.2 = (bf16[256,256]{1,0:T(8,128)(2,1)}, bf16[256,256]{1,0:T(8,128)(2,1)S(1)}, u32[]{:S(2)}, u32[]{:S(2)}) collective-permute-start(bf16[256,256]{1,0:T(8,128)(2,1)} %get-tuple-element.7), channel_id=1, source_target_pairs={{0,32},{32,64},{64,96},{96,128},{128,160},{160,192},{192,224},{224... | collective-permute-start | bytes 393224 | tf_op jit(solution)/shard_map/ppermute | solution.py:111
  18.1 5.6 %collective-permute-start.5 = (bf16[256,256]{1,0:T(8,128)(2,1)S(1)}, bf16[256,256]{1,0:T(8,128)(2,1)}, u32[]{:S(2)}, u32[]{:S(2)}) collective-permute-start(bf16[256,256]{1,0:T(8,128)(2,1)S(1)} %get-tuple-element.8), channel_id=1, source_target_pairs={{0,224},{32,0},{64,32},{96,64},{128,96},{160,128},{192,160},{224,1... | collective-permute-start | bytes 393224 | tf_op jit(solution)/shard_map/ppermute | solution.py:111
  24.8 5.1 %collective-permute-start.3 = (bf16[256,256]{1,0:T(8,128)(2,1)S(1)}, bf16[256,256]{1,0:T(8,128)(2,1)S(1)}, u32[]{:S(2)}, u32[]{:S(2)}) collective-permute-start(bf16[256,256]{1,0:T(8,128)(2,1)S(1)} %get-tuple-element.5), channel_id=1, source_target_pairs={{0,32},{32,64},{64,96},{96,128},{128,160},{160,192},{192,224},{224... | collective-permute-start | bytes 393224 | tf_op jit(solution)/shard_map/ppermute | solution.py:111
  24.9 5.0 %collective-permute-start.6 = (bf16[256,256]{1,0:T(8,128)(2,1)S(1)}, bf16[256,256]{1,0:T(8,128)(2,1)}, u32[]{:S(2)}, u32[]{:S(2)}) collective-permute-start(bf16[256,256]{1,0:T(8,128)(2,1)S(1)} %get-tuple-element.6), channel_id=1, source_target_pairs={{0,224},{32,0},{64,32},{96,64},{128,96},{160,128},{192,160},{224,1... | collective-permute-start | bytes 393224 | tf_op jit(solution)/shard_map/ppermute | solution.py:111
  31.7 5.3 %collective-permute-start.4 = (bf16[256,256]{1,0:T(8,128)(2,1)}, bf16[256,256]{1,0:T(8,128)(2,1)S(1)}, u32[]{:S(2)}, u32[]{:S(2)}) collective-permute-start(bf16[256,256]{1,0:T(8,128)(2,1)} %get-tuple-element.3), channel_id=1, source_target_pairs={{0,32},{32,64},{64,96},{96,128},{128,160},{160,192},{192,224},{224... | collective-permute-start | bytes 393224 | tf_op jit(solution)/shard_map/ppermute | solution.py:111
  33.2 4.0 %collective-permute-start.7 = (bf16[256,256]{1,0:T(8,128)(2,1)S(1)}, bf16[256,256]{1,0:T(8,128)(2,1)S(1)}, u32[]{:S(2)}, u32[]{:S(2)}) collective-permute-start(bf16[256,256]{1,0:T(8,128)(2,1)S(1)} %get-tuple-element.4), channel_id=1, source_target_pairs={{0,224},{32,0},{64,32},{96,64},{128,96},{160,128},{192,160},{224,1... | collective-permute-start | bytes 393224 | tf_op jit(solution)/shard_map/ppermute | solution.py:111
  38.3 4.7 %collective-permute-start.12 = (bf16[256,256]{1,0:T(8,128)(2,1)S(1)}, bf16[256,256]{1,0:T(8,128)(2,1)S(1)}, u32[]{:S(2)}, u32[]{:S(2)}) collective-permute-start(bf16[256,256]{1,0:T(8,128)(2,1)S(1)} %get-tuple-element.16), channel_id=1, source_target_pairs={{0,224},{32,0},{64,32},{96,64},{128,96},{160,128},{192,160},{224,1... | collective-permute-start | bytes 393224 | tf_op jit(solution)/shard_map/ppermute | solution.py:111
  44.0 5.4 %collective-permute-start.13 = (bf16[256,256]{1,0:T(8,128)(2,1)S(1)}, bf16[256,256]{1,0:T(8,128)(2,1)S(1)}, u32[]{:S(2)}, u32[]{:S(2)}) collective-permute-start(bf16[256,256]{1,0:T(8,128)(2,1)S(1)} %get-tuple-element.14), channel_id=1, source_target_pairs={{0,224},{32,0},{64,32},{96,64},{128,96},{160,128},{192,160},{224,1... | collective-permute-start | bytes 393224 | tf_op jit(solution)/shard_map/ppermute | solution.py:111
  46.8 5.0 %collective-permute-start.9 = (bf16[256,256]{1,0:T(8,128)(2,1)S(1)}, bf16[256,256]{1,0:T(8,128)(2,1)S(1)}, u32[]{:S(2)}, u32[]{:S(2)}) collective-permute-start(bf16[256,256]{1,0:T(8,128)(2,1)S(1)} %get-tuple-element.13), channel_id=1, source_target_pairs={{0,32},{32,64},{64,96},{96,128},{128,160},{160,192},{192,224},{224... | collective-permute-start | bytes 393224 | tf_op jit(solution)/shard_map/ppermute | solution.py:111
  52.9 6.7 %collective-permute-start.10 = (bf16[256,256]{1,0:T(8,128)(2,1)S(1)}, bf16[256,256]{1,0:T(8,128)(2,1)S(1)}, u32[]{:S(2)}, u32[]{:S(2)}) collective-permute-start(bf16[256,256]{1,0:T(8,128)(2,1)S(1)} %get-tuple-element.11), channel_id=1, source_target_pairs={{0,32},{32,64},{64,96},{96,128},{128,160},{160,192},{192,224},{224... | collective-permute-start | bytes 393224 | tf_op jit(solution)/shard_map/ppermute | solution.py:111
  53.0 6.6 %collective-permute-start.14 = (bf16[256,256]{1,0:T(8,128)(2,1)S(1)}, bf16[256,256]{1,0:T(8,128)(2,1)S(1)}, u32[]{:S(2)}, u32[]{:S(2)}) collective-permute-start(bf16[256,256]{1,0:T(8,128)(2,1)S(1)} %get-tuple-element.12), channel_id=1, source_target_pairs={{0,224},{32,0},{64,32},{96,64},{128,96},{160,128},{192,160},{224,1... | collective-permute-start | bytes 393224 | tf_op jit(solution)/shard_map/ppermute | solution.py:111
  60.7 6.2 %collective-permute-start.11 = (bf16[256,256]{1,0:T(8,128)(2,1)S(1)}, bf16[256,256]{1,0:T(8,128)(2,1)S(1)}, u32[]{:S(2)}, u32[]{:S(2)}) collective-permute-start(bf16[256,256]{1,0:T(8,128)(2,1)S(1)} %get-tuple-element.9), channel_id=1, source_target_pairs={{0,32},{32,64},{64,96},{96,128},{128,160},{160,192},{192,224},{224... | collective-permute-start | bytes 393224 | tf_op jit(solution)/shard_map/ppermute | solution.py:111
  60.9 6.0 %collective-permute-start.15 = (bf16[256,256]{1,0:T(8,128)(2,1)S(1)}, bf16[256,256]{1,0:T(8,128)(2,1)S(1)}, u32[]{:S(2)}, u32[]{:S(2)}) collective-permute-start(bf16[256,256]{1,0:T(8,128)(2,1)S(1)} %get-tuple-element.10), channel_id=1, source_target_pairs={{0,224},{32,0},{64,32},{96,64},{128,96},{160,128},{192,160},{224,1... | collective-permute-start | bytes 393224 | tf_op jit(solution)/shard_map/ppermute | solution.py:111
  63.6 50.9 %copy-start.6 = (s32[32]{0:T(128)}, s32[32]{0:T(128)S(1)}, u32[]{:S(2)}) copy-start(s32[32]{0:T(128)S(1)} %multiply_add_fusion.src_ref) | copy-start | bytes 388
  67.9 52.1 %copy-start.2 = (f32[1,1,4,256,256]{4,3,2,1,0:T(8,128)S(1)}, f32[1,1,4,256,256]{4,3,2,1,0:T(8,128)}, u32[]{:S(2)}) copy-start(f32[1,1,4,256,256]{4,3,2,1,0:T(8,128)} %param.8) | copy-start | bytes 3145732
  68.6 14.1 %all-to-all-start = ((bf16[16,2,16,256]{3,2,1,0:T(8,128)(2,1)}), bf16[16,2,16,256]{3,2,1,0:T(8,128)(2,1)S(1)}, u32[]{:S(2)}, u32[]{:S(2)}) async-start(bf16[16,2,16,256]{3,2,1,0:T(8,128)(2,1)} %pad_maximum_fusion), calls=%async_computation | async-start | bytes 524288 | tf_op jit(solution)/shard_map/all_to_all | solution.py:128
  82.7 0.7 copy-start.4
  98.5 21.4 %copy-start = (bf16[16,4,16,256]{3,2,1,0:T(8,128)(2,1)S(1)}, bf16[16,4,16,256]{3,2,1,0:T(8,128)(2,1)}, u32[]{:S(2)}) copy-start(bf16[16,4,16,256]{3,2,1,0:T(8,128)(2,1)} %all_to_all.20.own_ref) | copy-start | bytes 1572868
  98.5 44.9 %copy-start.3 = (f32[1,1,4,256,256]{4,3,2,1,0:T(8,128)S(1)}, f32[1,1,4,256,256]{4,3,2,1,0:T(8,128)}, u32[]{:S(2)}) copy-start(f32[1,1,4,256,256]{4,3,2,1,0:T(8,128)} %param.7) | copy-start | bytes 3145732
  116.4 10.9 %all-to-all-start.3 = ((bf16[16,2,16,256]{3,2,1,0:T(8,128)(2,1)}), bf16[16,2,16,256]{3,2,1,0:T(8,128)(2,1)S(1)}, u32[]{:S(2)}, u32[]{:S(2)}) async-start(bf16[16,2,16,256]{3,2,1,0:T(8,128)(2,1)} %bitcast.205), calls=%async_computation.3 | async-start | bytes 524288 | tf_op jit(solution)/shard_map/all_to_all | solution.py:134
  127.3 20.2 %collective-permute-start.16 = (bf16[256,256]{1,0:T(8,128)(2,1)S(1)}, bf16[256,256]{1,0:T(8,128)(2,1)S(1)}, u32[]{:S(2)}, u32[]{:S(2)}) collective-permute-start(bf16[256,256]{1,0:T(8,128)(2,1)S(1)} %bitcast.212), channel_id=1, source_target_pairs={{0,16},{16,0},{1,17},{17,1},{2,18},{18,2},{3,19},{19,3},{4,20},{20... | collective-permute-start | bytes 393224 | tf_op jit(solution)/shard_map/ppermute | solution.py:157
  141.0 8.7 %collective-permute-start.18 = (bf16[256,256]{1,0:T(8,128)(2,1)S(1)}, bf16[256,256]{1,0:T(8,128)(2,1)S(1)}, u32[]{:S(2)}, u32[]{:S(2)}) collective-permute-start(bf16[256,256]{1,0:T(8,128)(2,1)S(1)} %bitcast.213), channel_id=1, source_target_pairs={{0,32},{32,64},{64,96},{96,128},{128,160},{160,192},{192,224},{224... | collective-permute-start | bytes 393224 | tf_op jit(solution)/shard_map/ppermute | solution.py:163
  144.8 5.8 %collective-permute-start.20 = (bf16[256,256]{1,0:T(8,128)(2,1)S(1)}, bf16[256,256]{1,0:T(8,128)(2,1)S(1)}, u32[]{:S(2)}, u32[]{:S(2)}) collective-permute-start(bf16[256,256]{1,0:T(8,128)(2,1)S(1)} %bitcast.214), channel_id=1, source_target_pairs={{0,224},{32,0},{64,32},{96,64},{128,96},{160,128},{192,160},{224,1... | collective-permute-start | bytes 393224 | tf_op jit(solution)/shard_map/ppermute | solution.py:163
  146.1 4.4 %collective-permute-start.17 = (bf16[256,256]{1,0:T(8,128)(2,1)S(1)}, bf16[256,256]{1,0:T(8,128)(2,1)S(1)}, u32[]{:S(2)}, u32[]{:S(2)}) collective-permute-start(bf16[256,256]{1,0:T(8,128)(2,1)S(1)} %bitcast.208), channel_id=1, source_target_pairs={{0,16},{16,0},{1,17},{17,1},{2,18},{18,2},{3,19},{19,3},{4,20},{20... | collective-permute-start | bytes 393224 | tf_op jit(solution)/shard_map/ppermute | solution.py:157
  146.4 6.2 %collective-permute-start.22 = (bf16[256,256]{1,0:T(8,128)(2,1)S(1)}, bf16[256,256]{1,0:T(8,128)(2,1)S(1)}, u32[]{:S(2)}, u32[]{:S(2)}) collective-permute-start(bf16[256,256]{1,0:T(8,128)(2,1)S(1)} %bitcast.209), channel_id=1, source_target_pairs={{0,32},{32,64},{64,96},{96,128},{128,160},{160,192},{192,224},{224... | collective-permute-start | bytes 393224 | tf_op jit(solution)/shard_map/ppermute | solution.py:163
  147.5 6.9 %collective-permute-start.24 = (bf16[256,256]{1,0:T(8,128)(2,1)S(1)}, bf16[256,256]{1,0:T(8,128)(2,1)S(1)}, u32[]{:S(2)}, u32[]{:S(2)}) collective-permute-start(bf16[256,256]{1,0:T(8,128)(2,1)S(1)} %bitcast.210), channel_id=1, source_target_pairs={{0,224},{32,0},{64,32},{96,64},{128,96},{160,128},{192,160},{224,1... | collective-permute-start | bytes 393224 | tf_op jit(solution)/shard_map/ppermute | solution.py:163
  149.7 4.0 %collective-permute-start.19 = (bf16[256,256]{1,0:T(8,128)(2,1)S(1)}, bf16[256,256]{1,0:T(8,128)(2,1)S(1)}, u32[]{:S(2)}, u32[]{:S(2)}) collective-permute-start(bf16[256,256]{1,0:T(8,128)(2,1)S(1)} %collective-permute-done.18), channel_id=1, source_target_pairs={{0,16},{16,0},{1,17},{17,1},{2,18},{18,2},{3,19},{19,3},{4,20},{20... | collective-permute-start | bytes 393224 | tf_op jit(solution)/shard_map/ppermute | solution.py:167
  150.5 7.3 %collective-permute-start.26 = (bf16[256,256]{1,0:T(8,128)(2,1)S(1)}, bf16[256,256]{1,0:T(8,128)(2,1)S(1)}, u32[]{:S(2)}, u32[]{:S(2)}) collective-permute-start(bf16[256,256]{1,0:T(8,128)(2,1)S(1)} %collective-permute-done.18), channel_id=1, source_target_pairs={{0,32},{32,64},{64,96},{96,128},{128,160},{160,192},{192,224},{224... | collective-permute-start | bytes 393224 | tf_op jit(solution)/shard_map/ppermute | solution.py:163
  150.6 4.9 %collective-permute-start.21 = (bf16[256,256]{1,0:T(8,128)(2,1)S(1)}, bf16[256,256]{1,0:T(8,128)(2,1)S(1)}, u32[]{:S(2)}, u32[]{:S(2)}) collective-permute-start(bf16[256,256]{1,0:T(8,128)(2,1)S(1)} %collective-permute-done.20), channel_id=1, source_target_pairs={{0,16},{16,0},{1,17},{17,1},{2,18},{18,2},{3,19},{19,3},{4,20},{20... | collective-permute-start | bytes 393224 | tf_op jit(solution)/shard_map/ppermute | solution.py:167
  152.6 5.9 %collective-permute-start.28 = (bf16[256,256]{1,0:T(8,128)(2,1)S(1)}, bf16[256,256]{1,0:T(8,128)(2,1)S(1)}, u32[]{:S(2)}, u32[]{:S(2)}) collective-permute-start(bf16[256,256]{1,0:T(8,128)(2,1)S(1)} %collective-permute-done.20), channel_id=1, source_target_pairs={{0,224},{32,0},{64,32},{96,64},{128,96},{160,128},{192,160},{224,1... | collective-permute-start | bytes 393224 | tf_op jit(solution)/shard_map/ppermute | solution.py:163
  153.7 2.1 %collective-permute-start.23 = (bf16[256,256]{1,0:T(8,128)(2,1)S(1)}, bf16[256,256]{1,0:T(8,128)(2,1)S(1)}, u32[]{:S(2)}, u32[]{:S(2)}) collective-permute-start(bf16[256,256]{1,0:T(8,128)(2,1)S(1)} %collective-permute-done.22), channel_id=1, source_target_pairs={{0,16},{16,0},{1,17},{17,1},{2,18},{18,2},{3,19},{19,3},{4,20},{20... | collective-permute-start | bytes 393224 | tf_op jit(solution)/shard_map/ppermute | solution.py:167
  154.4 6.4 %collective-permute-start.30 = (bf16[256,256]{1,0:T(8,128)(2,1)S(1)}, bf16[256,256]{1,0:T(8,128)(2,1)S(1)}, u32[]{:S(2)}, u32[]{:S(2)}) collective-permute-start(bf16[256,256]{1,0:T(8,128)(2,1)S(1)} %collective-permute-done.22), channel_id=1, source_target_pairs={{0,32},{32,64},{64,96},{96,128},{128,160},{160,192},{192,224},{224... | collective-permute-start | bytes 393224 | tf_op jit(solution)/shard_map/ppermute | solution.py:163
  155.4 2.9 %collective-permute-start.25 = (bf16[256,256]{1,0:T(8,128)(2,1)S(1)}, bf16[256,256]{1,0:T(8,128)(2,1)S(1)}, u32[]{:S(2)}, u32[]{:S(2)}) collective-permute-start(bf16[256,256]{1,0:T(8,128)(2,1)S(1)} %collective-permute-done.24), channel_id=1, source_target_pairs={{0,16},{16,0},{1,17},{17,1},{2,18},{18,2},{3,19},{19,3},{4,20},{20... | collective-permute-start | bytes 393224 | tf_op jit(solution)/shard_map/ppermute | solution.py:167
  155.8 6.3 %collective-permute-start.32 = (bf16[256,256]{1,0:T(8,128)(2,1)S(1)}, bf16[256,256]{1,0:T(8,128)(2,1)S(1)}, u32[]{:S(2)}, u32[]{:S(2)}) collective-permute-start(bf16[256,256]{1,0:T(8,128)(2,1)S(1)} %collective-permute-done.24), channel_id=1, source_target_pairs={{0,224},{32,0},{64,32},{96,64},{128,96},{160,128},{192,160},{224,1... | collective-permute-start | bytes 393224 | tf_op jit(solution)/shard_map/ppermute | solution.py:163
  157.8 3.7 %collective-permute-start.27 = (bf16[256,256]{1,0:T(8,128)(2,1)S(1)}, bf16[256,256]{1,0:T(8,128)(2,1)S(1)}, u32[]{:S(2)}, u32[]{:S(2)}) collective-permute-start(bf16[256,256]{1,0:T(8,128)(2,1)S(1)} %collective-permute-done.26), channel_id=1, source_target_pairs={{0,16},{16,0},{1,17},{17,1},{2,18},{18,2},{3,19},{19,3},{4,20},{20... | collective-permute-start | bytes 393224 | tf_op jit(solution)/shard_map/ppermute | solution.py:167
  158.4 6.9 %collective-permute-start.34 = (bf16[256,256]{1,0:T(8,128)(2,1)S(1)}, bf16[256,256]{1,0:T(8,128)(2,1)S(1)}, u32[]{:S(2)}, u32[]{:S(2)}) collective-permute-start(bf16[256,256]{1,0:T(8,128)(2,1)S(1)} %collective-permute-done.26), channel_id=1, source_target_pairs={{0,32},{32,64},{64,96},{96,128},{128,160},{160,192},{192,224},{224... | collective-permute-start | bytes 393224 | tf_op jit(solution)/shard_map/ppermute | solution.py:163
  158.5 5.0 %collective-permute-start.29 = (bf16[256,256]{1,0:T(8,128)(2,1)S(1)}, bf16[256,256]{1,0:T(8,128)(2,1)S(1)}, u32[]{:S(2)}, u32[]{:S(2)}) collective-permute-start(bf16[256,256]{1,0:T(8,128)(2,1)S(1)} %collective-permute-done.28), channel_id=1, source_target_pairs={{0,16},{16,0},{1,17},{17,1},{2,18},{18,2},{3,19},{19,3},{4,20},{20... | collective-permute-start | bytes 393224 | tf_op jit(solution)/shard_map/ppermute | solution.py:167
  160.8 10.6 %collective-permute-start.36 = (bf16[256,256]{1,0:T(8,128)(2,1)S(1)}, bf16[256,256]{1,0:T(8,128)(2,1)S(1)}, u32[]{:S(2)}, u32[]{:S(2)}) collective-permute-start(bf16[256,256]{1,0:T(8,128)(2,1)S(1)} %collective-permute-done.28), channel_id=1, source_target_pairs={{0,224},{32,0},{64,32},{96,64},{128,96},{160,128},{192,160},{224,1... | collective-permute-start | bytes 393224 | tf_op jit(solution)/shard_map/ppermute | solution.py:163
  161.5 2.3 %collective-permute-start.31 = (bf16[256,256]{1,0:T(8,128)(2,1)S(1)}, bf16[256,256]{1,0:T(8,128)(2,1)S(1)}, u32[]{:S(2)}, u32[]{:S(2)}) collective-permute-start(bf16[256,256]{1,0:T(8,128)(2,1)S(1)} %collective-permute-done.30), channel_id=1, source_target_pairs={{0,16},{16,0},{1,17},{17,1},{2,18},{18,2},{3,19},{19,3},{4,20},{20... | collective-permute-start | bytes 393224 | tf_op jit(solution)/shard_map/ppermute | solution.py:167
  162.1 10.7 %collective-permute-start.38 = (bf16[256,256]{1,0:T(8,128)(2,1)S(1)}, bf16[256,256]{1,0:T(8,128)(2,1)S(1)}, u32[]{:S(2)}, u32[]{:S(2)}) collective-permute-start(bf16[256,256]{1,0:T(8,128)(2,1)S(1)} %collective-permute-done.30), channel_id=1, source_target_pairs={{0,32},{32,64},{64,96},{96,128},{128,160},{160,192},{192,224},{224... | collective-permute-start | bytes 393224 | tf_op jit(solution)/shard_map/ppermute | solution.py:163
  163.5 2.4 %collective-permute-start.33 = (bf16[256,256]{1,0:T(8,128)(2,1)S(1)}, bf16[256,256]{1,0:T(8,128)(2,1)S(1)}, u32[]{:S(2)}, u32[]{:S(2)}) collective-permute-start(bf16[256,256]{1,0:T(8,128)(2,1)S(1)} %collective-permute-done.32), channel_id=1, source_target_pairs={{0,16},{16,0},{1,17},{17,1},{2,18},{18,2},{3,19},{19,3},{4,20},{20... | collective-permute-start | bytes 393224 | tf_op jit(solution)/shard_map/ppermute | solution.py:167
  163.8 5.2 %collective-permute-start.40 = (bf16[256,256]{1,0:T(8,128)(2,1)S(1)}, bf16[256,256]{1,0:T(8,128)(2,1)S(1)}, u32[]{:S(2)}, u32[]{:S(2)}) collective-permute-start(bf16[256,256]{1,0:T(8,128)(2,1)S(1)} %collective-permute-done.32), channel_id=1, source_target_pairs={{0,224},{32,0},{64,32},{96,64},{128,96},{160,128},{192,160},{224,1... | collective-permute-start | bytes 393224 | tf_op jit(solution)/shard_map/ppermute | solution.py:163
  165.3 7.7 %collective-permute-start.35 = (bf16[256,256]{1,0:T(8,128)(2,1)S(1)}, bf16[256,256]{1,0:T(8,128)(2,1)S(1)}, u32[]{:S(2)}, u32[]{:S(2)}) collective-permute-start(bf16[256,256]{1,0:T(8,128)(2,1)S(1)} %collective-permute-done.34), channel_id=1, source_target_pairs={{0,16},{16,0},{1,17},{17,1},{2,18},{18,2},{3,19},{19,3},{4,20},{20... | collective-permute-start | bytes 393224 | tf_op jit(solution)/shard_map/ppermute | solution.py:167
  165.9 7.5 %collective-permute-start.42 = (bf16[256,256]{1,0:T(8,128)(2,1)S(1)}, bf16[256,256]{1,0:T(8,128)(2,1)S(1)}, u32[]{:S(2)}, u32[]{:S(2)}) collective-permute-start(bf16[256,256]{1,0:T(8,128)(2,1)S(1)} %collective-permute-done.34), channel_id=1, source_target_pairs={{0,32},{32,64},{64,96},{96,128},{128,160},{160,192},{192,224},{224... | collective-permute-start | bytes 393224 | tf_op jit(solution)/shard_map/ppermute | solution.py:163
  169.0 4.4 %collective-permute-start.44 = (bf16[256,256]{1,0:T(8,128)(2,1)S(1)}, bf16[256,256]{1,0:T(8,128)(2,1)S(1)}, u32[]{:S(2)}, u32[]{:S(2)}) collective-permute-start(bf16[256,256]{1,0:T(8,128)(2,1)S(1)} %collective-permute-done.40), channel_id=1, source_target_pairs={{0,224},{32,0},{64,32},{96,64},{128,96},{160,128},{192,160},{224,1... | collective-permute-start | bytes 393224 | tf_op jit(solution)/shard_map/ppermute | solution.py:163
  171.4 4.0 %collective-permute-start.41 = (bf16[256,256]{1,0:T(8,128)(2,1)S(1)}, bf16[256,256]{1,0:T(8,128)(2,1)S(1)}, u32[]{:S(2)}, u32[]{:S(2)}) collective-permute-start(bf16[256,256]{1,0:T(8,128)(2,1)S(1)} %collective-permute-done.40), channel_id=1, source_target_pairs={{0,16},{16,0},{1,17},{17,1},{2,18},{18,2},{3,19},{19,3},{4,20},{20... | collective-permute-start | bytes 393224 | tf_op jit(solution)/shard_map/ppermute | solution.py:167
  172.8 2.4 %collective-permute-start.37 = (bf16[256,256]{1,0:T(8,128)(2,1)S(1)}, bf16[256,256]{1,0:T(8,128)(2,1)S(1)}, u32[]{:S(2)}, u32[]{:S(2)}) collective-permute-start(bf16[256,256]{1,0:T(8,128)(2,1)S(1)} %collective-permute-done.36), channel_id=1, source_target_pairs={{0,16},{16,0},{1,17},{17,1},{2,18},{18,2},{3,19},{19,3},{4,20},{20... | collective-permute-start | bytes 393224 | tf_op jit(solution)/shard_map/ppermute | solution.py:167
  173.0 2.4 %collective-permute-start.39 = (bf16[256,256]{1,0:T(8,128)(2,1)S(1)}, bf16[256,256]{1,0:T(8,128)(2,1)S(1)}, u32[]{:S(2)}, u32[]{:S(2)}) collective-permute-start(bf16[256,256]{1,0:T(8,128)(2,1)S(1)} %collective-permute-done.38), channel_id=1, source_target_pairs={{0,16},{16,0},{1,17},{17,1},{2,18},{18,2},{3,19},{19,3},{4,20},{20... | collective-permute-start | bytes 393224 | tf_op jit(solution)/shard_map/ppermute | solution.py:167
  173.4 2.1 %collective-permute-start.43 = (bf16[256,256]{1,0:T(8,128)(2,1)S(1)}, bf16[256,256]{1,0:T(8,128)(2,1)S(1)}, u32[]{:S(2)}, u32[]{:S(2)}) collective-permute-start(bf16[256,256]{1,0:T(8,128)(2,1)S(1)} %collective-permute-done.42), channel_id=1, source_target_pairs={{0,16},{16,0},{1,17},{17,1},{2,18},{18,2},{3,19},{19,3},{4,20},{20... | collective-permute-start | bytes 393224 | tf_op jit(solution)/shard_map/ppermute | solution.py:167
  173.5 2.7 %collective-permute-start.45 = (bf16[256,256]{1,0:T(8,128)(2,1)S(1)}, bf16[256,256]{1,0:T(8,128)(2,1)S(1)}, u32[]{:S(2)}, u32[]{:S(2)}) collective-permute-start(bf16[256,256]{1,0:T(8,128)(2,1)S(1)} %collective-permute-done.44), channel_id=1, source_target_pairs={{0,16},{16,0},{1,17},{17,1},{2,18},{18,2},{3,19},{19,3},{4,20},{20... | collective-permute-start | bytes 393224 | tf_op jit(solution)/shard_map/ppermute | solution.py:167
  176.2 2.0 %copy-start.1 = (bf16[8,2,2,256,256]{4,3,2,1,0:T(8,128)(2,1)}, bf16[8,2,2,256,256]{4,3,2,1,0:T(8,128)(2,1)S(1)}, u32[]{:S(2)}) copy-start(bf16[8,2,2,256,256]{4,3,2,1,0:T(8,128)(2,1)S(1)} %bitcast_dynamic-update-slice_fusion) | copy-start | bytes 12582916

commit v2 on v1

v2 whole, which is shorter than its diff:
```python
import jax
import jax.numpy as jnp
from jax import lax
from jax.experimental import pallas as pl
from jax.experimental.pallas import tpu as pltpu
from jax.sharding import Mesh
from jax.sharding import PartitionSpec as P

DP = ("z", "core")
F32 = jnp.float32
BF16 = jnp.bfloat16
SMEM = pl.BlockSpec(memory_space=pltpu.SMEM)
VMEM = pl.BlockSpec(memory_space=pltpu.VMEM)
ANYWHERE = pl.BlockSpec(memory_space=pl.ANY)


def tie(value, *others):
    return lax.optimization_barrier((value, others))[0]


def pick_kernel(source_ref, value_ref, out_ref):
    def one(i, carry):
        source = source_ref[i]
        piece = value_ref[jnp.maximum(source, 0)]
        out_ref[i] = jnp.where(source >= 0, piece, jnp.zeros_like(piece))
        return carry

    lax.fori_loop(0, out_ref.shape[0], one, 0, unroll=8)


def pick(source, values):
    return pl.pallas_call(
        pick_kernel,
        out_shape=jax.ShapeDtypeStruct((*source.shape, *values.shape[1:]), values.dtype),
        in_specs=[SMEM, VMEM],
        out_specs=VMEM,
        name="pick",
    )(source, values)


def precond_kernel(grad_ref, root_ref, out_ref):
    held, rows, cols = grad_ref.shape
    for j in range(held):
        left = root_ref[:, j, 0].reshape(rows, rows)
        right = root_ref[:, j, 1].reshape(cols, cols)
        half = jnp.dot(left, grad_ref[j], preferred_element_type=F32).astype(BF16)
        out_ref[j] = jnp.dot(half, right, preferred_element_type=F32).astype(BF16)


def precondition(grads, roots):
    return pl.pallas_call(
        precond_kernel,
        out_shape=jax.ShapeDtypeStruct(grads.shape, BF16),
        in_specs=[VMEM, VMEM],
        out_specs=VMEM,
        name="precondition",
    )(grads, roots)


def statistics_kernel(own_ref, left_ref, right_ref, left_out_ref, right_out_ref):
    peers, _, piece, cols = own_ref.shape
    own = own_ref[:, 0].reshape(peers * piece, cols)
    left_out_ref[0] = left_ref[0] + lax.dot_general(
        own, own, (((1,), (1,)), ((), ())), preferred_element_type=F32
    )
    right_out_ref[0] = right_ref[0] + lax.dot_general(
        own, own, (((0,), (0,)), ((), ())), preferred_element_type=F32
    )


def statistics(own, left, right):
    peers, slots, piece, cols = own.shape
    one = pl.BlockSpec((1, *left.shape[1:]), lambda s: (s, 0, 0))
    return pl.pallas_call(
        statistics_kernel,
        grid=(slots,),
        out_shape=(
            jax.ShapeDtypeStruct(left.shape, F32),
            jax.ShapeDtypeStruct(right.shape, F32),
        ),
        in_specs=[pl.BlockSpec((peers, 1, piece, cols), lambda s: (0, s, 0, 0)), one, one],
        out_specs=(one, one),
        name="statistics",
    )(own, left, right)


def place(where, pieces, direction, shape):
    zs = shape[0]
    fresh = direction is None

    def kernel(where_ref, *refs):
        refs = list(refs)
        sem = refs.pop()
        out_ref = refs.pop()
        if not fresh:
            refs.pop(0)
        z, core = where_ref[0], where_ref[1]
        way = 1 - 2 * core
        copies = []
        for ref, (places, value) in zip(refs, pieces):
            for i, (step, cross, part) in enumerate(places):
                at = lax.rem(z + way * step + zs, zs)
                side = 1 - core if cross else core
                target = out_ref.at[at, side]
                if part is not None:
                    target = target.at[pl.ds(1 - core if part else core, 1)]
                copies.append(pltpu.make_async_copy(ref.at[i], target, sem.at[len(copies)]))
        for copy in copies:
            copy.start()
        for copy in copies:
            copy.wait()

    operands = ([] if fresh else [direction]) + [value for _, value in pieces]
    return pl.pallas_call(
        kernel,
        out_shape=jax.ShapeDtypeStruct(shape, BF16),
        in_specs=[SMEM] + ([] if fresh else [ANYWHERE]) + [VMEM] * len(pieces),
        out_specs=ANYWHERE,
        scratch_shapes=[pltpu.SemaphoreType.DMA((sum(len(p) for p, _ in pieces),))],
        input_output_aliases={} if fresh else {1: 0},
        name="place",
    )(where, *operands)


def per_device(grad_parts, left_stats, right_stats, left_root, right_root, owners):
    zs = lax.axis_size("z")
    mp = lax.axis_size("mp")
    z = lax.axis_index("z")
    core = lax.axis_index("core")
    way = 1 - 2 * core
    dp = z * 2 + core
    _, per_shard, rows, cols = grad_parts.shape
    held = per_shard // (2 * zs)
    slots = left_stats.shape[2]
    piece = rows // mp
    far = zs // 2
    grads = grad_parts.reshape(zs, 2, held, rows, cols)
    ring = [(2 * i, 2 * ((i + 1) % zs)) for i in range(zs)]
    ring += [(2 * i + 1, 2 * ((i - 1) % zs) + 1) for i in range(zs)]

    def hop(value):
        return lax.ppermute(value, DP, ring)

    def swap(value):
        return lax.ppermute(value, "core", [(0, 1), (1, 0)])

    row_owner = lax.dynamic_slice(
        owners.reshape(mp, 2 * zs, held), (0, dp, 0), (mp, 1, held)
    ).reshape(mp * held)
    pos = jnp.arange(mp * held, dtype=jnp.int32)
    same = (row_owner[:, None] == row_owner[None, :]) & (pos[None, :] < pos[:, None])
    key = row_owner * slots + jnp.sum(same.astype(jnp.int32), axis=1)
    keys = jnp.arange(mp * slots, dtype=jnp.int32)
    hit = keys[:, None] == key[None, :]
    source = jnp.sum(jnp.where(hit, pos[None, :] + 1, 0), axis=1) - 1

    def rows_for(step, part):
        at = (z + step + zs) % zs
        if part is None:
            return lax.dynamic_slice(
                grads, (at, 0, 0, 0, 0), (1, 2, held, rows, cols)
            ).reshape(2, held, rows, cols)
        return lax.dynamic_slice(
            grads, (at, 0, part, 0, 0), (1, 2, 1, rows, cols)
        ).reshape(2, 1, rows, cols)

    def base(step, theirs, part=None):
        return rows_for(way * step, part).astype(F32) + theirs.astype(F32)

    theirs = swap(rows_for(-way * far, 1 - core))
    theirs3 = swap(rows_for(-way * (far - 1), None))
    moving = base(far, theirs, core).astype(BF16)
    came = hop(moving)

    spread = jnp.stack([left_root[0, 0], right_root[0, 0]], axis=1).reshape(
        slots, 2, mp, piece, cols
    )
    spread = tie(jnp.moveaxis(spread, 2, 0), moving)
    spread = lax.all_to_all(spread, "mp", 0, 0, tiled=True)
    wanted = pick(key, spread.reshape(mp * slots, 2, piece, cols))
    roots = lax.all_to_all(wanted.reshape(mp, held, 2, piece, cols), "mp", 0, 0, tiled=True)

    nearer = base(far - 1, tie(theirs3, moving))
    mine = jnp.where(
        jnp.arange(held)[None, :, None, None] == core,
        jnp.broadcast_to(came, nearer.shape).astype(F32),
        0,
    )
    for step in range(far - 1, 0, -1):
        before = moving
        moving = (mine + nearer).astype(BF16)
        came = hop(moving)
        if step > 1:
            theirs = swap(tie(rows_for(-way * (step - 1), None), before))
            nearer = lax.optimization_barrier(base(step - 1, tie(theirs, moving)))
            mine = came.astype(F32)

    def side(value, which):
        return lax.dynamic_slice(value, (which, 0, 0, 0), (1, held, rows, cols))[0]

    here = lax.dynamic_slice(grads, (z, 0, 0, 0, 0), (1, 2, held, rows, cols))[0]
    give = (side(came, 1 - core).astype(F32) + side(here, 1 - core).astype(F32)).astype(BF16)
    taken = swap(give)
    blocks = (
        side(came, core).astype(F32) + side(here, core).astype(F32) + taken.astype(F32)
    ).astype(BF16)

    result = precondition(blocks, roots)

    sliced = jnp.moveaxis(tie(blocks, result).reshape(held, mp, piece, cols), 1, 0)
    sliced = lax.all_to_all(sliced, "mp", 0, 0, tiled=True)
    to_owner = pick(source, sliced.reshape(mp * held, piece, cols))
    own = lax.all_to_all(to_owner.reshape(mp, slots, piece, cols), "mp", 0, 0, tiled=True)
    left_updated, right_updated = statistics(own, left_stats[0, 0], right_stats[0, 0])

    shape = (zs, 2, held, rows, cols)
    where = jnp.stack([z, core])
    beside = swap(result)
    pieces = [([(0, False, None)], result[None]), ([(0, True, None)], beside[None])]
    flow = [result, beside]
    for step in range(1, far):
        flow = [hop(value) for value in flow]
        pair = jnp.stack(flow)
        got = swap(pair)
        pieces.append(([(-step, False, None), (-step, True, None)], pair))
        pieces.append(([(step, True, None), (step, False, None)], got))
    flow = [
        hop(lax.dynamic_slice(value, (core, 0, 0), (1, rows, cols))) for value in flow
    ]
    pair = jnp.stack(flow)
    got = swap(pair)
    late = [([(far, False, 0), (far, True, 0)], pair), ([(far, True, 1), (far, False, 1)], got)]
    direction = place(where, pieces, None, shape)
    direction = place(where, late, direction, shape)
    return (
        direction.reshape(per_shard, rows, cols),
        left_updated[None, None],
        right_updated[None, None],
    )


def solution(mesh):
    split = Mesh(mesh.devices.reshape(-1, 2, mesh.shape["mp"]), ("z", "core", "mp"))
    held = P(DP, "mp", None, None, None)
    in_specs = (P(DP, "mp", None, None), held, held, held, held, P())
    out_specs = (P("mp", None, None), held, held)
    return jax.shard_map(
        per_device, mesh=split, in_specs=in_specs, out_specs=out_specs, check_vma=False
    )
```

time: 179 us -> 145 us (0.81)
  the two profiles are of different devices: /device:TPU:1 before, /device:TPU:64 now
where the time goes in v2:
time: 145 us; the launch traced here: 143 us
  starting transfers between devices  56.6 us (39%)
  waiting for transfers between devices  44 us (30%)
  Pallas kernels  16.4 us (11%)
  other arithmetic  15.8 us (11%)
  local copies, waits for them, and re-layouts  9.29 us (6%)
    ppermute x12, starting transfers between devices, hop(): return lax.ppermute(value, DP, ring)  30 us
    ppermute x12, waiting for transfers between devices, hop(): return lax.ppermute(value, DP, ring)  23.4 us
    all_to_all x1, waiting for transfers between devices, per_device(): lax.all_to_all(wanted.reshape(mp, held, 2, piece, cols), 'mp', 0, 0, tile...  10.4 us
    all_to_all x1, waiting for transfers between devices, per_device(): lax.all_to_all(to_owner.reshape(mp, slots, piece, cols), 'mp', 0, 0, tile...  10.2 us
    all_to_all x1, starting transfers between devices, per_device(): lax.all_to_all(wanted.reshape(mp, held, 2, piece, cols), 'mp', 0, 0, tile...  7.21 us
    all_to_all x1, starting transfers between devices, per_device(): lax.all_to_all(to_owner.reshape(mp, slots, piece, cols), 'mp', 0, 0, tile...  7.17 us
    all_to_all x1, starting transfers between devices, per_device(): spread = lax.all_to_all(spread, 'mp', 0, 0, tiled=True)  7.03 us
    pallas_call x2, Pallas kernels, place(): pl.pallas_call(kernel, out_shape=jax.ShapeDtypeStruct(shape, BF16), in_sp...  5.82 us
  transfers between devices with their start and end apart: 26, of which 9 were waited for; matrix products, arithmetic and copies ran while one was open for 14% of the time, Pallas kernels for 9%

profile of v2, /device:TPU:64, one launch (start us, length us, event | category | flops | bytes accessed | tf_op | source)
XLA Modules:
  0.0 143.4 jit_solution(273537350019764486)
XLA Ops:
  0.7 1.0 dynamic-slice_bitcast_fusion.3
  1.6 0.1 collective-permute-start
  1.8 1.5 %dynamic-slice_bitcast_fusion.1 = (bf16[2,2,256,256]{3,2,1,0:T(8,128)(2,1)S(1)}, bf16[2,2,256,256]{3,2,1,0:T(8,128)(2,1)S(1)}, bf16[2,2,256,256]{3,2,1,0:T(8,128)(2,1)S(1)}) fusion(bf16[8,2,2,256,256]{4,3,2,1,0:T(8,128)(2,1)} %bitcast.67, s32[]{:T(128)S(6)} %select_n.105, s32[]{:T(128)S(6)} %select_n.109, s32[]{:T(128)S(6)} %select_n.101), kind=kLoop, calls=%fused_computation.20 | loop fusion | bytes 3145740 | tf_op jit(solution)/shard_map/reshape | solution.py:162
  3.3 0.5 collective-permute-start.2
  3.8 1.7 %fusion.5 = bf16[2,1,256,256]{3,2,0,1:T(8,128)(2,1)} fusion(bf16[2,1,256,256]{3,2,0,1:T(8,128)(2,1)S(1)} %collective-permute-done, bf16[8,2,2,256,256]{4,3,2,1,0:T(8,128)(2,1)} %bitcast.68, s32[]{:T(128)S(6)} %select_n.92, s32[]{:T(128)S(6)} %select_n.93), kind=kLoop, calls=%fused_computation.18 | loop fusion | flops 524288 | bytes 786440 | tf_op jit(solution)/shard_map/convert_element_type | solution.py:172
  5.5 1.9 %collective-permute-start.1 = (bf16[2,1,256,256]{3,2,0,1:T(8,128)(2,1)}, bf16[2,1,256,256]{3,2,0,1:T(8,128)(2,1)S(1)}, u32[]{:S(2)}, u32[]{:S(2)}) collective-permute-start(bf16[2,1,256,256]{3,2,0,1:T(8,128)(2,1)} %fusion.5), channel_id=1, source_target_pairs={{0,32},{32,64},{64,96},{96,128},{128,160},{160,192},{192,224},{224... | collective-permute-start | bytes 786440 | tf_op jit(solution)/shard_map/ppermute | solution.py:142
  7.4 4.7 %collective-permute-done.1 = bf16[2,1,256,256]{3,2,0,1:T(8,128)(2,1)S(1)} collective-permute-done((bf16[2,1,256,256]{3,2,0,1:T(8,128)(2,1)}, bf16[2,1,256,256]{3,2,0,1:T(8,128)(2,1)S(1)}, u32[]{:S(2)}, u32[]{:S(2)}) %collective-permute-start.1) | collective-permute-done | bytes 262176 | tf_op jit(solution)/shard_map/ppermute | solution.py:142
  12.1 1.3 fusion.1
  13.4 2.7 %collective-permute-start.3 = (bf16[2,2,256,256]{3,2,1,0:T(8,128)(2,1)S(1)}, bf16[2,2,256,256]{3,2,1,0:T(8,128)(2,1)}, u32[]{:S(2)}, u32[]{:S(2)}) collective-permute-start(bf16[2,2,256,256]{3,2,1,0:T(8,128)(2,1)S(1)} %fusion.1), channel_id=1, source_target_pairs={{0,32},{32,64},{64,96},{96,128},{128,160},{160,192},{192,224},{224... | collective-permute-start | bytes 1572872 | tf_op jit(solution)/shard_map/ppermute | solution.py:142
  16.2 1.1 convert_add_fusion.1
  17.3 5.5 %collective-permute-done.3 = bf16[2,2,256,256]{3,2,1,0:T(8,128)(2,1)} collective-permute-done((bf16[2,2,256,256]{3,2,1,0:T(8,128)(2,1)S(1)}, bf16[2,2,256,256]{3,2,1,0:T(8,128)(2,1)}, u32[]{:S(2)}, u32[]{:S(2)}) %collective-permute-start.3) | collective-permute-done | bytes 524320 | tf_op jit(solution)/shard_map/ppermute | solution.py:142
  22.9 1.2 add_convert_fusion.1
  24.0 3.7 %collective-permute-start.5 = (bf16[2,2,256,256]{3,2,1,0:T(8,128)(2,1)S(1)}, bf16[2,2,256,256]{3,2,1,0:T(8,128)(2,1)}, u32[]{:S(2)}, u32[]{:S(2)}) collective-permute-start(bf16[2,2,256,256]{3,2,1,0:T(8,128)(2,1)S(1)} %add_convert_fusion.1), channel_id=1, source_target_pairs={{0,32},{32,64},{64,96},{96,128},{128,160},{160,192},{192,224},{224... | collective-permute-start | bytes 1572872 | tf_op jit(solution)/shard_map/ppermute | solution.py:142
  27.7 2.2 %copy_bitcast_fusion = bf16[16,4,2,16,256]{4,3,2,1,0:T(8,128)(2,1)} fusion(bf16[4,1,16,16,256]{4,3,2,0,1:T(8,128)(2,1)S(1)} %bitcast.84, bf16[4,1,16,16,256]{4,3,2,0,1:T(8,128)(2,1)} %bitcast.85), kind=kLoop, calls=%fused_computation.6 | loop fusion | flops 524288 | bytes 2097152 | tf_op jit(solution)/shard_map/transpose | solution.py:178
  29.9 7.0 %all-to-all-start = ((bf16[16,4,2,16,256]{4,3,2,1,0:T(8,128)(2,1)}), bf16[16,4,2,16,256]{4,3,2,1,0:T(8,128)(2,1)S(1)}, u32[]{:S(2)}, u32[]{:S(2)}) async-start(bf16[16,4,2,16,256]{4,3,2,1,0:T(8,128)(2,1)} %copy_bitcast_fusion), calls=%async_computation | async-start | bytes 2097152 | tf_op jit(solution)/shard_map/all_to_all | solution.py:179
  36.9 1.2 convert_add_fusion
  38.1 1.2 add_convert_fusion
  39.3 3.9 %collective-permute-start.7 = (bf16[2,2,256,256]{3,2,1,0:T(8,128)(2,1)S(1)}, bf16[2,2,256,256]{3,2,1,0:T(8,128)(2,1)S(1)}, u32[]{:S(2)}, u32[]{:S(2)}) collective-permute-start(bf16[2,2,256,256]{3,2,1,0:T(8,128)(2,1)S(1)} %add_convert_fusion), channel_id=1, source_target_pairs={{0,32},{32,64},{64,96},{96,128},{128,160},{160,192},{192,224},{224... | collective-permute-start | bytes 1572872 | tf_op jit(solution)/shard_map/ppermute | solution.py:142
  43.1 0.1 reshape.113
  43.4 0.2 convert_reduce_fusion
  43.6 6.2 %collective-permute-done.7 = bf16[2,2,256,256]{3,2,1,0:T(8,128)(2,1)S(1)} collective-permute-done((bf16[2,2,256,256]{3,2,1,0:T(8,128)(2,1)S(1)}, bf16[2,2,256,256]{3,2,1,0:T(8,128)(2,1)S(1)}, u32[]{:S(2)}, u32[]{:S(2)}) %collective-permute-start.7) | collective-permute-done | bytes 524320 | tf_op jit(solution)/shard_map/ppermute | solution.py:142
  49.8 1.0 fusion.2
  50.8 0.1 collective-permute-start.8
  50.9 0.6 multiply_add_fusion.source_ref
  51.5 1.0 copy-done
  52.5 2.1 %pick.2 = bf16[32,2,16,256]{3,2,1,0:T(8,128)(2,1)} custom-call(s32[32]{0:T(128)} %multiply_add_fusion.source_ref, bf16[64,2,16,256]{3,2,1,0:T(8,128)(2,1)} %bitcast.74), custom_call_target="tpu_custom_call" | custom-call | tf_op jit(solution)/shard_map/pick/pallas_call | solution.py:32
  54.6 7.2 %all-to-all-start.1 = ((bf16[16,2,2,16,256]{4,3,2,1,0:T(8,128)(2,1)}), bf16[16,2,2,16,256]{4,3,2,1,0:T(8,128)(2,1)S(1)}, u32[]{:S(2)}, u32[]{:S(2)}) async-start(bf16[16,2,2,16,256]{4,3,2,1,0:T(8,128)(2,1)} %bitcast.77), calls=%async_computation.1 | async-start | bytes 1048576 | tf_op jit(solution)/shard_map/all_to_all | solution.py:181
  61.9 1.8 %fusion.4.grad_ref = bf16[2,256,256]{2,1,0:T(8,128)(2,1)} fusion(bf16[2,256,256]{2,1,0:T(8,128)(2,1)S(1)} %collective-permute-done.8, bf16[8,2,2,256,256]{4,3,2,1,0:T(8,128)(2,1)} %bitcast.73, s32[]{:T(128)S(6)} %select_n.111, s32[]{:T(128)S(6)} %select_n.112, bf16[2,2,256,256]{3,2,1,0:T(8,128)(2,1)S(1)} %collective-permute-done.7, s32[]{:T(128)S(6)} %select_n.93), kind=kLoop, calls=%fused_computation.16 | loop fusion | flops 786432 | bytes 1048588 | tf_op jit(solution)/shard_map/convert_element_type | solution.py:206
  63.6 10.4 %all-to-all-done.1.root_ref = bf16[16,2,2,16,256]{4,3,2,1,0:T(8,128)(2,1)S(1)} async-done(((bf16[16,2,2,16,256]{4,3,2,1,0:T(8,128)(2,1)}), bf16[16,2,2,16,256]{4,3,2,1,0:T(8,128)(2,1)S(1)}, u32[]{:S(2)}, u32[]{:S(2)}) %all-to-all-start.1) | async-done | bytes 524320 | tf_op jit(solution)/shard_map/all_to_all | solution.py:181
  74.0 0.8 copy-done.5
  74.8 2.2 %precondition.1 = bf16[2,256,256]{2,1,0:T(8,128)(2,1)} custom-call(bf16[2,256,256]{2,1,0:T(8,128)(2,1)} %fusion.4.grad_ref, bf16[16,2,2,16,256]{4,3,2,1,0:T(8,128)(2,1)} %copy-done.5), custom_call_target="tpu_custom_call" | custom-call | tf_op jit(solution)/shard_map/precondition/pallas_call | solution.py:51
  77.0 2.5 %collective-permute-start.10 = (bf16[2,256,256]{2,1,0:T(8,128)(2,1)}, bf16[2,256,256]{2,1,0:T(8,128)(2,1)S(1)}, u32[]{:S(2)}, u32[]{:S(2)}) collective-permute-start(bf16[2,256,256]{2,1,0:T(8,128)(2,1)} %precondition.1), channel_id=1, source_target_pairs={{0,32},{32,64},{64,96},{96,128},{128,160},{160,192},{192,224},{224... | collective-permute-start | bytes 786440 | tf_op jit(solution)/shard_map/ppermute | solution.py:142
  79.5 1.7 %collective-permute-start.11 = (bf16[2,256,256]{2,1,0:T(8,128)(2,1)S(1)}, bf16[2,256,256]{2,1,0:T(8,128)(2,1)S(1)}, u32[]{:S(2)}, u32[]{:S(2)}) collective-permute-start(bf16[2,256,256]{2,1,0:T(8,128)(2,1)S(1)} %collective-permute-done.9), channel_id=1, source_target_pairs={{0,32},{32,64},{64,96},{96,128},{128,160},{160,192},{192,224},{224... | collective-permute-start | bytes 786440 | tf_op jit(solution)/shard_map/ppermute | solution.py:142
  81.2 2.5 %collective-permute-done.10 = bf16[2,256,256]{2,1,0:T(8,128)(2,1)S(1)} collective-permute-done((bf16[2,256,256]{2,1,0:T(8,128)(2,1)}, bf16[2,256,256]{2,1,0:T(8,128)(2,1)S(1)}, u32[]{:S(2)}, u32[]{:S(2)}) %collective-permute-start.10) | collective-permute-done | bytes 262176 | tf_op jit(solution)/shard_map/ppermute | solution.py:142
  83.7 2.4 %collective-permute-start.13 = (bf16[2,256,256]{2,1,0:T(8,128)(2,1)S(1)}, bf16[2,256,256]{2,1,0:T(8,128)(2,1)S(1)}, u32[]{:S(2)}, u32[]{:S(2)}) collective-permute-start(bf16[2,256,256]{2,1,0:T(8,128)(2,1)S(1)} %collective-permute-done.10), channel_id=1, source_target_pairs={{0,32},{32,64},{64,96},{96,128},{128,160},{160,192},{192,224},{224... | collective-permute-start | bytes 786440 | tf_op jit(solution)/shard_map/ppermute | solution.py:142
  86.1 0.3 collective-permute-done.11
  86.4 2.5 %collective-permute-start.14 = (bf16[2,256,256]{2,1,0:T(8,128)(2,1)S(1)}, bf16[2,256,256]{2,1,0:T(8,128)(2,1)S(1)}, u32[]{:S(2)}, u32[]{:S(2)}) collective-permute-start(bf16[2,256,256]{2,1,0:T(8,128)(2,1)S(1)} %collective-permute-done.11), channel_id=1, source_target_pairs={{0,32},{32,64},{64,96},{96,128},{128,160},{160,192},{192,224},{224... | collective-permute-start | bytes 786440 | tf_op jit(solution)/shard_map/ppermute | solution.py:142
  88.9 1.2 collective-permute-done.13
  90.1 2.4 %collective-permute-start.16 = (bf16[2,256,256]{2,1,0:T(8,128)(2,1)S(1)}, bf16[2,256,256]{2,1,0:T(8,128)(2,1)S(1)}, u32[]{:S(2)}, u32[]{:S(2)}) collective-permute-start(bf16[2,256,256]{2,1,0:T(8,128)(2,1)S(1)} %collective-permute-done.13), channel_id=1, source_target_pairs={{0,32},{32,64},{64,96},{96,128},{128,160},{160,192},{192,224},{224... | collective-permute-start | bytes 786440 | tf_op jit(solution)/shard_map/ppermute | solution.py:142
  92.5 0.1 select_reduce_fusion
  92.5 1.7 %copy.22 = bf16[2,16,16,256]{3,2,0,1:T(8,128)(2,1)} copy(bf16[2,16,16,256]{3,2,1,0:T(8,128)(2,1)} %bitcast.75) | data formatting | bytes 524288 | tf_op jit(solution)/shard_map/reshape | solution.py:210
  94.2 3.5 %all-to-all-start.2 = ((bf16[16,2,16,256]{3,2,1,0:T(8,128)(2,1)}), bf16[16,2,16,256]{3,2,1,0:T(8,128)(2,1)S(1)}, u32[]{:S(2)}, u32[]{:S(2)}) async-start(bf16[16,2,16,256]{3,2,1,0:T(8,128)(2,1)} %bitcast.64), calls=%async_computation.2 | async-start | bytes 524288 | tf_op jit(solution)/shard_map/all_to_all | solution.py:211
  97.8 3.8 %collective-permute-start.17 = (bf16[2,256,256]{2,1,0:T(8,128)(2,1)S(1)}, bf16[2,256,256]{2,1,0:T(8,128)(2,1)S(1)}, u32[]{:S(2)}, u32[]{:S(2)}) collective-permute-start(bf16[2,256,256]{2,1,0:T(8,128)(2,1)S(1)} %collective-permute-done.14), channel_id=1, source_target_pairs={{0,32},{32,64},{64,96},{96,128},{128,160},{160,192},{192,224},{224... | collective-permute-start | bytes 786440 | tf_op jit(solution)/shard_map/ppermute | solution.py:142
  101.6 0.1 collective-permute-start.12
  101.7 0.1 collective-permute-start.19
  101.9 0.6 collective-permute-start.15
  102.5 3.0 %collective-permute-done.17 = bf16[2,256,256]{2,1,0:T(8,128)(2,1)S(1)} collective-permute-done((bf16[2,256,256]{2,1,0:T(8,128)(2,1)S(1)}, bf16[2,256,256]{2,1,0:T(8,128)(2,1)S(1)}, u32[]{:S(2)}, u32[]{:S(2)}) %collective-permute-start.17) | collective-permute-done | bytes 262176 | tf_op jit(solution)/shard_map/ppermute | solution.py:142
  105.4 0.7 constant_dynamic-slice_fusion
  106.1 2.5 %collective-permute-start.20 = (bf16[1,256,256]{2,1,0:T(8,128)(2,1)}, bf16[1,256,256]{2,1,0:T(8,128)(2,1)}, u32[]{:S(2)}, u32[]{:S(2)}) collective-permute-start(bf16[1,256,256]{2,1,0:T(8,128)(2,1)} %constant_dynamic-slice_fusion), channel_id=1, source_target_pairs={{0,32},{32,64},{64,96},{96,128},{128,160},{160,192},{192,224},{224... | collective-permute-start | bytes 393224 | tf_op jit(solution)/shard_map/ppermute | solution.py:142
  108.6 0.1 collective-permute-start.18
  108.7 0.7 broadcast_add_fusion.source_ref
  109.4 0.7 copy-done.7
  110.1 2.0 %pick.3 = bf16[64,16,256]{2,1,0:T(8,128)(2,1)} custom-call(s32[64]{0:T(128)} %broadcast_add_fusion.source_ref, bf16[32,16,256]{2,1,0:T(8,128)(2,1)} %bitcast.81), custom_call_target="tpu_custom_call" | custom-call | tf_op jit(solution)/shard_map/pick/pallas_call | solution.py:32
  112.1 7.2 %all-to-all-start.3 = ((bf16[16,4,16,256]{3,2,1,0:T(8,128)(2,1)}), bf16[16,4,16,256]{3,2,1,0:T(8,128)(2,1)S(1)}, u32[]{:S(2)}, u32[]{:S(2)}) async-start(bf16[16,4,16,256]{3,2,1,0:T(8,128)(2,1)} %bitcast.76), calls=%async_computation.3 | async-start | bytes 1048576 | tf_op jit(solution)/shard_map/all_to_all | solution.py:213
  119.2 1.0 pad_maximum_fusion.4.refs_1_
  120.3 0.2 collective-permute-start.21
  120.5 0.6 pad_add_fusion.where_ref
  121.1 10.2 %all-to-all-done.3.own_ref = bf16[16,4,16,256]{3,2,1,0:T(8,128)(2,1)S(1)} async-done(((bf16[16,4,16,256]{3,2,1,0:T(8,128)(2,1)}), bf16[16,4,16,256]{3,2,1,0:T(8,128)(2,1)S(1)}, u32[]{:S(2)}, u32[]{:S(2)}) %all-to-all-start.3) | async-done | bytes 524320 | tf_op jit(solution)/shard_map/all_to_all | solution.py:213
  131.3 0.8 copy-done.4
  132.1 4.3 %statistics.1 = (f32[4,256,256]{2,1,0:T(8,128)}, f32[4,256,256]{2,1,0:T(8,128)}) custom-call(bf16[16,4,16,256]{3,2,1,0:T(8,128)(2,1)} %copy-done.4, f32[4,256,256]{2,1,0:T(8,128)} %bitcast.78, f32[4,256,256]{2,1,0:T(8,128)} %bitcast.79), custom_call_target="tpu_custom_call" | custom-call | tf_op jit(solution)/shard_map/statistics/pallas_call | solution.py:74
  136.5 0.7 copy-done.8
  137.2 0.2 copy-done.9
  137.4 4.0 %place.2.refs_0_ = bf16[8,2,2,256,256]{4,3,2,1,0:T(8,128)(2,1)} custom-call(s32[2]{0:T(128)} %pad_add_fusion.where_ref, bf16[1,2,256,256]{3,2,1,0:T(8,128)(2,1)} %bitcast.80, bf16[1,2,256,256]{3,2,1,0:T(8,128)(2,1)} %bitcast.86, bf16[2,2,256,256]{3,2,1,0:T(8,128)(2,1)} %copy-done.1, bf16[2,2,256,256]{3,2,1,0:T(8,128)(2,1)} %copy-done.8, ...), custom_call_target="tpu_custom_call" | custom-call | tf_op jit(solution)/shard_map/place/pallas_call | solution.py:114
  141.4 1.9 %place.3 = bf16[8,2,2,256,256]{4,3,2,1,0:T(8,128)(2,1)} custom-call(s32[2]{0:T(128)} %pad_add_fusion.where_ref, bf16[8,2,2,256,256]{4,3,2,1,0:T(8,128)(2,1)} %place.2.refs_0_, bf16[2,1,256,256]{3,2,1,0:T(8,128)(2,1)} %copy-done.6, bf16[2,1,256,256]{3,2,1,0:T(8,128)(2,1)} %collective-permute-done.21.refs_2_), custom_call_target="tpu_custom_call", output_to_operand_aliasing={{}: (1, {})} | custom-call | tf_op jit(solution)/shard_map/place/pallas_call | solution.py:114
  (51 shorter events, 0.4 us)
Async XLA Ops:
  1.6 2.2 %collective-permute-start = (bf16[2,1,256,256]{3,2,0,1:T(8,128)(2,1)S(1)}, bf16[2,1,256,256]{3,2,0,1:T(8,128)(2,1)S(1)}, u32[]{:S(2)}, u32[]{:S(2)}) collective-permute-start(bf16[2,1,256,256]{3,2,0,1:T(8,128)(2,1)S(1)} %dynamic-slice_bitcast_fusion.3), channel_id=1, source_target_pairs={{0,16},{16,0},{1,17},{17,1},{2,18},{18,2},{3,19},{19,3},{4,20},{20... | collective-permute-start | bytes 786440 | tf_op jit(solution)/shard_map/ppermute | solution.py:145
  3.3 24.4 %copy-start.10 = (bf16[1,1,4,256,256]{4,3,2,1,0:T(8,128)(2,1)S(1)}, bf16[1,1,4,256,256]{4,3,2,1,0:T(8,128)(2,1)}, u32[]{:S(2)}) copy-start(bf16[1,1,4,256,256]{4,3,2,1,0:T(8,128)(2,1)} %param.10) | copy-start | bytes 1572868
  3.3 8.9 %collective-permute-start.2 = (bf16[2,2,256,256]{3,2,1,0:T(8,128)(2,1)S(1)}, bf16[2,2,256,256]{3,2,1,0:T(8,128)(2,1)S(1)}, u32[]{:S(2)}, u32[]{:S(2)}) collective-permute-start(bf16[2,2,256,256]{3,2,1,0:T(8,128)(2,1)S(1)} %get-tuple-element.23), channel_id=1, source_target_pairs={{0,16},{16,0},{1,17},{17,1},{2,18},{18,2},{3,19},{19,3},{4,20},{20... | collective-permute-start | bytes 1572872 | tf_op jit(solution)/shard_map/ppermute | solution.py:145
  5.5 6.6 %collective-permute-start.1 = (bf16[2,1,256,256]{3,2,0,1:T(8,128)(2,1)}, bf16[2,1,256,256]{3,2,0,1:T(8,128)(2,1)S(1)}, u32[]{:S(2)}, u32[]{:S(2)}) collective-permute-start(bf16[2,1,256,256]{3,2,0,1:T(8,128)(2,1)} %fusion.5), channel_id=1, source_target_pairs={{0,32},{32,64},{64,96},{96,128},{128,160},{160,192},{192,224},{224... | collective-permute-start | bytes 786440 | tf_op jit(solution)/shard_map/ppermute | solution.py:142
  7.4 8.7 %collective-permute-start.4 = (bf16[2,2,256,256]{3,2,1,0:T(8,128)(2,1)S(1)}, bf16[2,2,256,256]{3,2,1,0:T(8,128)(2,1)S(1)}, u32[]{:S(2)}, u32[]{:S(2)}) collective-permute-start(bf16[2,2,256,256]{3,2,1,0:T(8,128)(2,1)S(1)} %get-tuple-element.13), channel_id=1, source_target_pairs={{0,16},{16,0},{1,17},{17,1},{2,18},{18,2},{3,19},{19,3},{4,20},{20... | collective-permute-start | bytes 1572872 | tf_op jit(solution)/shard_map/ppermute | solution.py:145
  13.4 9.4 %collective-permute-start.3 = (bf16[2,2,256,256]{3,2,1,0:T(8,128)(2,1)S(1)}, bf16[2,2,256,256]{3,2,1,0:T(8,128)(2,1)}, u32[]{:S(2)}, u32[]{:S(2)}) collective-permute-start(bf16[2,2,256,256]{3,2,1,0:T(8,128)(2,1)S(1)} %fusion.1), channel_id=1, source_target_pairs={{0,32},{32,64},{64,96},{96,128},{128,160},{160,192},{192,224},{224... | collective-permute-start | bytes 1572872 | tf_op jit(solution)/shard_map/ppermute | solution.py:142
  16.2 20.8 %collective-permute-start.6 = (bf16[2,2,256,256]{3,2,1,0:T(8,128)(2,1)S(1)}, bf16[2,2,256,256]{3,2,1,0:T(8,128)(2,1)S(1)}, u32[]{:S(2)}, u32[]{:S(2)}) collective-permute-start(bf16[2,2,256,256]{3,2,1,0:T(8,128)(2,1)S(1)} %get-tuple-element.15), channel_id=1, source_target_pairs={{0,16},{16,0},{1,17},{17,1},{2,18},{18,2},{3,19},{19,3},{4,20},{20... | collective-permute-start | bytes 1572872 | tf_op jit(solution)/shard_map/ppermute | solution.py:145
  24.0 14.1 %collective-permute-start.5 = (bf16[2,2,256,256]{3,2,1,0:T(8,128)(2,1)S(1)}, bf16[2,2,256,256]{3,2,1,0:T(8,128)(2,1)}, u32[]{:S(2)}, u32[]{:S(2)}) collective-permute-start(bf16[2,2,256,256]{3,2,1,0:T(8,128)(2,1)S(1)} %add_convert_fusion.1), channel_id=1, source_target_pairs={{0,32},{32,64},{64,96},{96,128},{128,160},{160,192},{192,224},{224... | collective-permute-start | bytes 1572872 | tf_op jit(solution)/shard_map/ppermute | solution.py:142
  27.7 15.4 %copy-start.12 = (s32[512]{0:T(512)S(1)}, s32[512]{0:T(512)}, u32[]{:S(2)}) copy-start(s32[512]{0:T(512)} %param.11) | copy-start | bytes 6148
  29.9 21.7 %all-to-all-start = ((bf16[16,4,2,16,256]{4,3,2,1,0:T(8,128)(2,1)}), bf16[16,4,2,16,256]{4,3,2,1,0:T(8,128)(2,1)S(1)}, u32[]{:S(2)}, u32[]{:S(2)}) async-start(bf16[16,4,2,16,256]{4,3,2,1,0:T(8,128)(2,1)} %copy_bitcast_fusion), calls=%async_computation | async-start | bytes 2097152 | tf_op jit(solution)/shard_map/all_to_all | solution.py:179
  39.3 10.6 %collective-permute-start.7 = (bf16[2,2,256,256]{3,2,1,0:T(8,128)(2,1)S(1)}, bf16[2,2,256,256]{3,2,1,0:T(8,128)(2,1)S(1)}, u32[]{:S(2)}, u32[]{:S(2)}) collective-permute-start(bf16[2,2,256,256]{3,2,1,0:T(8,128)(2,1)S(1)} %add_convert_fusion), channel_id=1, source_target_pairs={{0,32},{32,64},{64,96},{96,128},{128,160},{160,192},{192,224},{224... | collective-permute-start | bytes 1572872 | tf_op jit(solution)/shard_map/ppermute | solution.py:142
  50.8 11.0 %collective-permute-start.8 = (bf16[2,256,256]{2,1,0:T(8,128)(2,1)S(1)}, bf16[2,256,256]{2,1,0:T(8,128)(2,1)S(1)}, u32[]{:S(2)}, u32[]{:S(2)}) collective-permute-start(bf16[2,256,256]{2,1,0:T(8,128)(2,1)S(1)} %fusion.2), channel_id=1, source_target_pairs={{0,16},{16,0},{1,17},{17,1},{2,18},{18,2},{3,19},{19,3},{4,20},{20... | collective-permute-start | bytes 786440 | tf_op jit(solution)/shard_map/ppermute | solution.py:145
  51.5 40.9 %copy-start.13 = (s32[32]{0:T(128)S(1)}, s32[32]{0:T(128)}, u32[]{:S(2)}) copy-start(s32[32]{0:T(128)} %multiply_add_fusion.source_ref) | copy-start | bytes 388
  51.5 1.0 copy-start
  54.6 19.4 %all-to-all-start.1 = ((bf16[16,2,2,16,256]{4,3,2,1,0:T(8,128)(2,1)}), bf16[16,2,2,16,256]{4,3,2,1,0:T(8,128)(2,1)S(1)}, u32[]{:S(2)}, u32[]{:S(2)}) async-start(bf16[16,2,2,16,256]{4,3,2,1,0:T(8,128)(2,1)} %bitcast.77), calls=%async_computation.1 | async-start | bytes 1048576 | tf_op jit(solution)/shard_map/all_to_all | solution.py:181
  74.0 0.8 copy-start.5
  77.0 2.5 %collective-permute-start.9 = (bf16[2,256,256]{2,1,0:T(8,128)(2,1)}, bf16[2,256,256]{2,1,0:T(8,128)(2,1)S(1)}, u32[]{:S(2)}, u32[]{:S(2)}) collective-permute-start(bf16[2,256,256]{2,1,0:T(8,128)(2,1)} %precondition.1), channel_id=1, source_target_pairs={{0,16},{16,0},{1,17},{17,1},{2,18},{18,2},{3,19},{19,3},{4,20},{20... | collective-permute-start | bytes 786440 | tf_op jit(solution)/shard_map/ppermute | solution.py:145
  77.0 6.7 %collective-permute-start.10 = (bf16[2,256,256]{2,1,0:T(8,128)(2,1)}, bf16[2,256,256]{2,1,0:T(8,128)(2,1)S(1)}, u32[]{:S(2)}, u32[]{:S(2)}) collective-permute-start(bf16[2,256,256]{2,1,0:T(8,128)(2,1)} %precondition.1), channel_id=1, source_target_pairs={{0,32},{32,64},{64,96},{96,128},{128,160},{160,192},{192,224},{224... | collective-permute-start | bytes 786440 | tf_op jit(solution)/shard_map/ppermute | solution.py:142
  79.5 9.4 %copy-start.11 = (bf16[2,256,256]{2,1,0:T(8,128)(2,1)}, bf16[2,256,256]{2,1,0:T(8,128)(2,1)S(1)}, u32[]{:S(2)}) copy-start(bf16[2,256,256]{2,1,0:T(8,128)(2,1)S(1)} %collective-permute-done.9) | copy-start | bytes 786436
  79.5 6.9 %collective-permute-start.11 = (bf16[2,256,256]{2,1,0:T(8,128)(2,1)S(1)}, bf16[2,256,256]{2,1,0:T(8,128)(2,1)S(1)}, u32[]{:S(2)}, u32[]{:S(2)}) collective-permute-start(bf16[2,256,256]{2,1,0:T(8,128)(2,1)S(1)} %collective-permute-done.9), channel_id=1, source_target_pairs={{0,32},{32,64},{64,96},{96,128},{128,160},{160,192},{192,224},{224... | collective-permute-start | bytes 786440 | tf_op jit(solution)/shard_map/ppermute | solution.py:142
  83.7 6.4 %collective-permute-start.13 = (bf16[2,256,256]{2,1,0:T(8,128)(2,1)S(1)}, bf16[2,256,256]{2,1,0:T(8,128)(2,1)S(1)}, u32[]{:S(2)}, u32[]{:S(2)}) collective-permute-start(bf16[2,256,256]{2,1,0:T(8,128)(2,1)S(1)} %collective-permute-done.10), channel_id=1, source_target_pairs={{0,32},{32,64},{64,96},{96,128},{128,160},{160,192},{192,224},{224... | collective-permute-start | bytes 786440 | tf_op jit(solution)/shard_map/ppermute | solution.py:142
  86.4 11.4 %collective-permute-start.14 = (bf16[2,256,256]{2,1,0:T(8,128)(2,1)S(1)}, bf16[2,256,256]{2,1,0:T(8,128)(2,1)S(1)}, u32[]{:S(2)}, u32[]{:S(2)}) collective-permute-start(bf16[2,256,256]{2,1,0:T(8,128)(2,1)S(1)} %collective-permute-done.11), channel_id=1, source_target_pairs={{0,32},{32,64},{64,96},{96,128},{128,160},{160,192},{192,224},{224... | collective-permute-start | bytes 786440 | tf_op jit(solution)/shard_map/ppermute | solution.py:142
  90.1 11.6 %collective-permute-start.16 = (bf16[2,256,256]{2,1,0:T(8,128)(2,1)S(1)}, bf16[2,256,256]{2,1,0:T(8,128)(2,1)S(1)}, u32[]{:S(2)}, u32[]{:S(2)}) collective-permute-start(bf16[2,256,256]{2,1,0:T(8,128)(2,1)S(1)} %collective-permute-done.13), channel_id=1, source_target_pairs={{0,32},{32,64},{64,96},{96,128},{128,160},{160,192},{192,224},{224... | collective-permute-start | bytes 786440 | tf_op jit(solution)/shard_map/ppermute | solution.py:142
  94.2 15.2 %all-to-all-start.2 = ((bf16[16,2,16,256]{3,2,1,0:T(8,128)(2,1)}), bf16[16,2,16,256]{3,2,1,0:T(8,128)(2,1)S(1)}, u32[]{:S(2)}, u32[]{:S(2)}) async-start(bf16[16,2,16,256]{3,2,1,0:T(8,128)(2,1)} %bitcast.64), calls=%async_computation.2 | async-start | bytes 524288 | tf_op jit(solution)/shard_map/all_to_all | solution.py:211
  97.8 7.6 %collective-permute-start.17 = (bf16[2,256,256]{2,1,0:T(8,128)(2,1)S(1)}, bf16[2,256,256]{2,1,0:T(8,128)(2,1)S(1)}, u32[]{:S(2)}, u32[]{:S(2)}) collective-permute-start(bf16[2,256,256]{2,1,0:T(8,128)(2,1)S(1)} %collective-permute-done.14), channel_id=1, source_target_pairs={{0,32},{32,64},{64,96},{96,128},{128,160},{160,192},{192,224},{224... | collective-permute-start | bytes 786440 | tf_op jit(solution)/shard_map/ppermute | solution.py:142
  101.6 34.9 %copy-start.1 = (bf16[2,2,256,256]{3,2,1,0:T(8,128)(2,1)}, bf16[2,2,256,256]{3,2,1,0:T(8,128)(2,1)S(1)}, u32[]{:S(2)}) copy-start(bf16[2,2,256,256]{3,2,1,0:T(8,128)(2,1)S(1)} %pad_maximum_fusion.1.refs_2_) | copy-start | bytes 1572868
  101.6 34.8 %collective-permute-start.12 = (bf16[2,2,256,256]{3,2,1,0:T(8,128)(2,1)S(1)}, bf16[2,2,256,256]{3,2,1,0:T(8,128)(2,1)S(1)}, u32[]{:S(2)}, u32[]{:S(2)}) collective-permute-start(bf16[2,2,256,256]{3,2,1,0:T(8,128)(2,1)S(1)} %pad_maximum_fusion.1.refs_2_), channel_id=1, source_target_pairs={{0,16},{16,0},{1,17},{17,1},{2,18},{18,2},{3,19},{19,3},{4,20},{20... | collective-permute-start | bytes 1572872 | tf_op jit(solution)/shard_map/ppermute | solution.py:145
  101.7 17.5 %collective-permute-start.19 = (bf16[1,256,256]{2,1,0:T(8,128)(2,1)S(1)}, bf16[1,256,256]{2,1,0:T(8,128)(2,1)}, u32[]{:S(2)}, u32[]{:S(2)}) collective-permute-start(bf16[1,256,256]{2,1,0:T(8,128)(2,1)S(1)} %constant_dynamic-slice_fusion.1), channel_id=1, source_target_pairs={{0,32},{32,64},{64,96},{96,128},{128,160},{160,192},{192,224},{224... | collective-permute-start | bytes 393224 | tf_op jit(solution)/shard_map/ppermute | solution.py:142
  101.9 34.6 %copy-start.2 = (bf16[2,2,256,256]{3,2,1,0:T(8,128)(2,1)}, bf16[2,2,256,256]{3,2,1,0:T(8,128)(2,1)S(1)}, u32[]{:S(2)}) copy-start(bf16[2,2,256,256]{3,2,1,0:T(8,128)(2,1)S(1)} %pad_maximum_fusion.2.refs_4_) | copy-start | bytes 1572868
  101.9 34.5 %collective-permute-start.15 = (bf16[2,2,256,256]{3,2,1,0:T(8,128)(2,1)S(1)}, bf16[2,2,256,256]{3,2,1,0:T(8,128)(2,1)S(1)}, u32[]{:S(2)}, u32[]{:S(2)}) collective-permute-start(bf16[2,2,256,256]{3,2,1,0:T(8,128)(2,1)S(1)} %pad_maximum_fusion.2.refs_4_), channel_id=1, source_target_pairs={{0,16},{16,0},{1,17},{17,1},{2,18},{18,2},{3,19},{19,3},{4,20},{20... | collective-permute-start | bytes 1572872 | tf_op jit(solution)/shard_map/ppermute | solution.py:145
  106.1 13.2 %collective-permute-start.20 = (bf16[1,256,256]{2,1,0:T(8,128)(2,1)}, bf16[1,256,256]{2,1,0:T(8,128)(2,1)}, u32[]{:S(2)}, u32[]{:S(2)}) collective-permute-start(bf16[1,256,256]{2,1,0:T(8,128)(2,1)} %constant_dynamic-slice_fusion), channel_id=1, source_target_pairs={{0,32},{32,64},{64,96},{96,128},{128,160},{160,192},{192,224},{224... | collective-permute-start | bytes 393224 | tf_op jit(solution)/shard_map/ppermute | solution.py:142
  108.6 27.9 %copy-start.3 = (bf16[2,2,256,256]{3,2,1,0:T(8,128)(2,1)}, bf16[2,2,256,256]{3,2,1,0:T(8,128)(2,1)S(1)}, u32[]{:S(2)}) copy-start(bf16[2,2,256,256]{3,2,1,0:T(8,128)(2,1)S(1)} %pad_maximum_fusion.3.refs_6_) | copy-start | bytes 1572868
  108.6 27.8 %collective-permute-start.18 = (bf16[2,2,256,256]{3,2,1,0:T(8,128)(2,1)S(1)}, bf16[2,2,256,256]{3,2,1,0:T(8,128)(2,1)}, u32[]{:S(2)}, u32[]{:S(2)}) collective-permute-start(bf16[2,2,256,256]{3,2,1,0:T(8,128)(2,1)S(1)} %pad_maximum_fusion.3.refs_6_), channel_id=1, source_target_pairs={{0,16},{16,0},{1,17},{17,1},{2,18},{18,2},{3,19},{19,3},{4,20},{20... | collective-permute-start | bytes 1572872 | tf_op jit(solution)/shard_map/ppermute | solution.py:145
  109.4 0.7 copy-start.7
  112.1 19.3 %all-to-all-start.3 = ((bf16[16,4,16,256]{3,2,1,0:T(8,128)(2,1)}), bf16[16,4,16,256]{3,2,1,0:T(8,128)(2,1)S(1)}, u32[]{:S(2)}, u32[]{:S(2)}) async-start(bf16[16,4,16,256]{3,2,1,0:T(8,128)(2,1)} %bitcast.76), calls=%async_computation.3 | async-start | bytes 1048576 | tf_op jit(solution)/shard_map/all_to_all | solution.py:213
  120.2 21.1 %copy-start.6 = (bf16[2,1,256,256]{3,2,1,0:T(8,128)(2,1)}, bf16[2,1,256,256]{3,2,1,0:T(8,128)(2,1)S(1)}, u32[]{:S(2)}) copy-start(bf16[2,1,256,256]{3,2,1,0:T(8,128)(2,1)S(1)} %pad_maximum_fusion.4.refs_1_) | copy-start | bytes 786436
  120.3 21.1 %collective-permute-start.21 = (bf16[2,1,256,256]{3,2,1,0:T(8,128)(2,1)S(1)}, bf16[2,1,256,256]{3,2,1,0:T(8,128)(2,1)}, u32[]{:S(2)}, u32[]{:S(2)}) collective-permute-start(bf16[2,1,256,256]{3,2,1,0:T(8,128)(2,1)S(1)} %pad_maximum_fusion.4.refs_1_), channel_id=1, source_target_pairs={{0,16},{16,0},{1,17},{17,1},{2,18},{18,2},{3,19},{19,3},{4,20},{20... | collective-permute-start | bytes 786440 | tf_op jit(solution)/shard_map/ppermute | solution.py:145
  131.3 0.8 copy-start.4
  136.4 0.8 copy-start.8
  136.4 1.0 copy-start.9

commit v3 on v2

--- a/solution.py
+++ b/solution.py
@@ -95,15 +95,14 @@
         if not fresh:
             refs.pop(0)
         z, core = where_ref[0], where_ref[1]
-        way = 1 - 2 * core
         copies = []
         for ref, (places, value) in zip(refs, pieces):
             for i, (step, cross, part) in enumerate(places):
-                at = lax.rem(z + way * step + zs, zs)
+                at = lax.rem(z + step + zs, zs)
                 side = 1 - core if cross else core
                 target = out_ref.at[at, side]
                 if part is not None:
-                    target = target.at[pl.ds(1 - core if part else core, 1)]
+                    target = target.at[pl.ds(part, 1)]
                 copies.append(pltpu.make_async_copy(ref.at[i], target, sem.at[len(copies)]))
         for copy in copies:
             copy.start()
@@ -127,7 +126,6 @@
     mp = lax.axis_size("mp")
     z = lax.axis_index("z")
     core = lax.axis_index("core")
-    way = 1 - 2 * core
     dp = z * 2 + core
     _, per_shard, rows, cols = grad_parts.shape
     held = per_shard // (2 * zs)
@@ -135,11 +133,10 @@
     piece = rows // mp
     far = zs // 2
     grads = grad_parts.reshape(zs, 2, held, rows, cols)
-    ring = [(2 * i, 2 * ((i + 1) % zs)) for i in range(zs)]
-    ring += [(2 * i + 1, 2 * ((i - 1) % zs) + 1) for i in range(zs)]
-
-    def hop(value):
-        return lax.ppermute(value, DP, ring)
+    ways = [[(i, (i + 1) % zs) for i in range(zs)], [(i, (i - 1) % zs) for i in range(zs)]]
+
+    def hop(value, way):
+        return lax.ppermute(value, "z", ways[way])
 
     def swap(value):
         return lax.ppermute(value, "core", [(0, 1), (1, 0)])
@@ -154,83 +151,86 @@
     hit = keys[:, None] == key[None, :]
     source = jnp.sum(jnp.where(hit, pos[None, :] + 1, 0), axis=1) - 1
 
-    def rows_for(step, part):
+    def rows_of(step, which):
         at = (z + step + zs) % zs
-        if part is None:
-            return lax.dynamic_slice(
-                grads, (at, 0, 0, 0, 0), (1, 2, held, rows, cols)
-            ).reshape(2, held, rows, cols)
         return lax.dynamic_slice(
-            grads, (at, 0, part, 0, 0), (1, 2, 1, rows, cols)
-        ).reshape(2, 1, rows, cols)
-
-    def base(step, theirs, part=None):
-        return rows_for(way * step, part).astype(F32) + theirs.astype(F32)
-
-    theirs = swap(rows_for(-way * far, 1 - core))
-    theirs3 = swap(rows_for(-way * (far - 1), None))
-    moving = base(far, theirs, core).astype(BF16)
-    came = hop(moving)
+            grads, (at, which, 0, 0, 0), (1, 1, held, rows, cols)
+        ).reshape(held, rows, cols)
+
+    def base(step, *others):
+        at = (z + step + zs) % zs
+        at = tie(at, *others) if others else at
+        given = lax.dynamic_slice(theirs, (at, 0, 0, 0), (1, held, rows, cols))[0]
+        mine = lax.dynamic_slice(grads, (at, core, 0, 0, 0), (1, 1, held, rows, cols))
+        value = mine.reshape(held, rows, cols).astype(F32) + given.astype(F32)
+        return lax.optimization_barrier(value)
+
+    farthest = swap(rows_of(far, 1 - core))
+    theirs = lax.dynamic_slice(
+        grads, (0, 1 - core, 0, 0, 0), (zs, 1, held, rows, cols)
+    ).reshape(zs, held, rows, cols)
+    moving = rows_of(far, core)
+    moving = [
+        (moving[way : way + 1].astype(F32) + farthest[way : way + 1].astype(F32)).astype(BF16)
+        for way in range(2)
+    ]
+    theirs = swap(tie(theirs, *moving))
+    came = [hop(moving[way], way) for way in range(2)]
 
     spread = jnp.stack([left_root[0, 0], right_root[0, 0]], axis=1).reshape(
         slots, 2, mp, piece, cols
     )
-    spread = tie(jnp.moveaxis(spread, 2, 0), moving)
+    spread = jnp.moveaxis(tie(spread, *moving), 2, 0)
     spread = lax.all_to_all(spread, "mp", 0, 0, tiled=True)
-    wanted = pick(key, spread.reshape(mp * slots, 2, piece, cols))
-    roots = lax.all_to_all(wanted.reshape(mp, held, 2, piece, cols), "mp", 0, 0, tiled=True)
-
-    nearer = base(far - 1, tie(theirs3, moving))
-    mine = jnp.where(
-        jnp.arange(held)[None, :, None, None] == core,
-        jnp.broadcast_to(came, nearer.shape).astype(F32),
-        0,
-    )
+
+    first = jnp.arange(held)[:, None, None]
+    came = [
+        jnp.where(first == way, jnp.broadcast_to(came[way], (held, rows, cols)).astype(F32), 0)
+        for way in range(2)
+    ]
     for step in range(far - 1, 0, -1):
-        before = moving
-        moving = (mine + nearer).astype(BF16)
-        came = hop(moving)
-        if step > 1:
-            theirs = swap(tie(rows_for(-way * (step - 1), None), before))
-            nearer = lax.optimization_barrier(base(step - 1, tie(theirs, moving)))
-            mine = came.astype(F32)
-
-    def side(value, which):
-        return lax.dynamic_slice(value, (which, 0, 0, 0), (1, held, rows, cols))[0]
-
-    here = lax.dynamic_slice(grads, (z, 0, 0, 0, 0), (1, 2, held, rows, cols))[0]
-    give = (side(came, 1 - core).astype(F32) + side(here, 1 - core).astype(F32)).astype(BF16)
-    taken = swap(give)
+        added = [base(step, *moving), base(-step, *moving)]
+        moving = [(came[way].astype(F32) + added[way]).astype(BF16) for way in range(2)]
+        if step == far - 2:
+            wanted = pick(key, tie(spread, *moving).reshape(mp * slots, 2, piece, cols))
+            wanted = wanted.reshape(mp, held, 2, piece, cols)
+            roots = lax.all_to_all(wanted, "mp", 0, 0, tiled=True)
+        came = [hop(moving[way], way) for way in range(2)]
     blocks = (
-        side(came, core).astype(F32) + side(here, core).astype(F32) + taken.astype(F32)
+        came[0].astype(F32) + came[1].astype(F32) + base(0, *moving)
     ).astype(BF16)
 
-    result = precondition(blocks, roots)
-
-    sliced = jnp.moveaxis(tie(blocks, result).reshape(held, mp, piece, cols), 1, 0)
-    sliced = lax.all_to_all(sliced, "mp", 0, 0, tiled=True)
-    to_owner = pick(source, sliced.reshape(mp * held, piece, cols))
-    own = lax.all_to_all(to_owner.reshape(mp, slots, piece, cols), "mp", 0, 0, tiled=True)
-    left_updated, right_updated = statistics(own, left_stats[0, 0], right_stats[0, 0])
+    sliced = jnp.moveaxis(blocks.reshape(held, mp, piece, cols), 1, 0)
+    result = precondition(tie(blocks, sliced), roots)
+
+    arrived = lax.all_to_all(sliced, "mp", 0, 0, tiled=True)
 
     shape = (zs, 2, held, rows, cols)
     where = jnp.stack([z, core])
-    beside = swap(result)
-    pieces = [([(0, False, None)], result[None]), ([(0, True, None)], beside[None])]
-    flow = [result, beside]
+    pieces = [([(0, False, None)], result[None]), ([(0, True, None)], swap(result)[None])]
+    flow = [result, result]
     for step in range(1, far):
-        flow = [hop(value) for value in flow]
+        flow = [hop(flow[way], way) for way in range(2)]
+        if step == far - 2:
+            flow = tie(flow, to_owner)
+        if step == far - 1:
+            flow = tie(flow, own)
+        if step == far - 3:
+            to_owner = pick(source, tie(arrived, *flow).reshape(mp * held, piece, cols))
+            own = lax.all_to_all(
+                to_owner.reshape(mp, slots, piece, cols), "mp", 0, 0, tiled=True
+            )
         pair = jnp.stack(flow)
-        got = swap(pair)
-        pieces.append(([(-step, False, None), (-step, True, None)], pair))
-        pieces.append(([(step, True, None), (step, False, None)], got))
-    flow = [
-        hop(lax.dynamic_slice(value, (core, 0, 0), (1, rows, cols))) for value in flow
+        for cross, value in ((False, pair), (True, swap(pair))):
+            pieces.append(([(-step, cross, None), (step, cross, None)], value))
+    flow = [hop(flow[way][way : way + 1], way) for way in range(2)]
+    left_updated, right_updated = statistics(own, left_stats[0, 0], right_stats[0, 0])
+    direction = place(tie(where, left_updated), pieces, None, shape)
+    pair = jnp.stack(tie(flow, direction))
+    late = [
+        ([(-far, cross, 0), (far, cross, 1)], value)
+        for cross, value in ((False, pair), (True, swap(pair)))
     ]
-    pair = jnp.stack(flow)
-    got = swap(pair)
-    late = [([(far, False, 0), (far, True, 0)], pair), ([(far, True, 1), (far, False, 1)], got)]
-    direction = place(where, pieces, None, shape)
     direction = place(where, late, direction, shape)
     return (
         direction.reshape(per_shard, rows, cols),

time: 145 us -> 117 us (0.81)
  the two profiles are of different devices: /device:TPU:64 before, /device:TPU:1 now
where the time goes in v3:
time: 117 us
  starting transfers between devices  57.8 us (49%)
  waiting for transfers between devices  20.6 us (18%)
  Pallas kernels  16.5 us (14%)
  other arithmetic  10.7 us (9%)
  local copies, waits for them, and re-layouts  9.64 us (8%)
  between operations  1.34 us (1%)
    ppermute x16, starting transfers between devices, hop(): return lax.ppermute(value, 'z', ways[way])  19.4 us
    ppermute x7, starting transfers between devices, swap(): return lax.ppermute(value, 'core', [(0, 1), (1, 0)])  18.4 us
    ppermute x16, waiting for transfers between devices, hop(): return lax.ppermute(value, 'z', ways[way])  7.08 us
    all_to_all x1, waiting for transfers between devices, per_device(): roots = lax.all_to_all(wanted, 'mp', 0, 0, tiled=True)  7.03 us
    all_to_all x1, starting transfers between devices, per_device(): spread = lax.all_to_all(spread, 'mp', 0, 0, tiled=True)  6.77 us
    all_to_all x1, starting transfers between devices, per_device(): roots = lax.all_to_all(wanted, 'mp', 0, 0, tiled=True)  6.08 us
    pallas_call x2, Pallas kernels, place(): pl.pallas_call(kernel, out_shape=jax.ShapeDtypeStruct(shape, BF16), in_sp...  5.81 us
    add x4, other arithmetic, base(): value = mine.reshape(held, rows, cols).astype(F32) + given.astype(F32)  4.99 us
  transfers between devices with their start and end apart: 27, of which 7 were waited for; matrix products, arithmetic and copies ran while one was open for 11% of the time, Pallas kernels for 11%

profile of v3, /device:TPU:1, one launch (start us, length us, event | category | flops | bytes accessed | tf_op | source)
XLA Modules:
  0.0 116.5 jit_solution(1017840322263259996)
XLA Ops:
  0.7 1.0 dynamic-slice_bitcast_fusion.1
  1.6 3.3 %collective-permute-start = (bf16[2,256,256]{2,1,0:T(8,128)(2,1)S(1)}, bf16[2,256,256]{2,1,0:T(8,128)(2,1)S(1)}, u32[]{:S(2)}, u32[]{:S(2)}) collective-permute-start(bf16[2,256,256]{2,1,0:T(8,128)(2,1)S(1)} %dynamic-slice_bitcast_fusion.1), channel_id=1, source_target_pairs={{0,16},{16,0},{1,17},{17,1},{2,18},{18,2},{3,19},{19,3},{4,20},{20... | collective-permute-start | bytes 786440 | tf_op jit(solution)/shard_map/ppermute | solution.py:142
  5.0 1.8 %dynamic-slice_bitcast_fusion = bf16[8,2,256,256]{3,2,1,0:T(8,128)(2,1)S(1)} fusion(bf16[8,2,2,256,256]{4,3,2,1,0:T(8,128)(2,1)} %bitcast.93, s32[]{:T(128)S(6)} %select_n.102), kind=kLoop, calls=%fused_computation | loop fusion | bytes 4194308 | tf_op jit(solution)/shard_map/reshape | solution.py:171
  6.8 1.7 %fusion = (bf16[1,256,256]{2,1,0:T(8,128)(2,1)}, bf16[1,256,256]{2,1,0:T(8,128)(2,1)S(1)}) fusion(bf16[2,256,256]{2,1,0:T(8,128)(2,1)S(1)} %collective-permute-done, bf16[8,2,2,256,256]{4,3,2,1,0:T(8,128)(2,1)} %bitcast.94, s32[]{:T(128)S(6)} %select_n.100, s32[]{:T(128)S(6)} %select_n.101, s32[]{:T(128)S(6)} %add.243), kind=kLoop, calls=%fused_computation.21 | loop fusion | flops 524288 | bytes 786444 | tf_op jit(solution)/shard_map/convert_element_type | solution.py:174
  8.5 0.5 iota_compare_fusion.3
  9.1 0.1 pad_maximum_fusion
  9.2 3.9 %collective-permute-start.4 = (bf16[1,256,256]{2,1,0:T(8,128)(2,1)}, bf16[1,256,256]{2,1,0:T(8,128)(2,1)S(1)}, u32[]{:S(2)}, u32[]{:S(2)}) collective-permute-start(bf16[1,256,256]{2,1,0:T(8,128)(2,1)} %get-tuple-element.51), channel_id=1, source_target_pairs={{0,224},{32,0},{64,32},{96,64},{128,96},{160,128},{192,160},{224,1... | collective-permute-start | bytes 393224 | tf_op jit(solution)/shard_map/ppermute | solution.py:139
  13.1 0.1 reshape.139
  13.3 0.1 reshape.140
  13.4 1.1 copy.19
  14.5 0.2 convert_reduce_fusion
  14.7 0.1 collective-permute-start.1
  14.8 6.8 %all-to-all-start.1 = ((bf16[16,4,2,16,256]{4,3,2,1,0:T(8,128)(2,1)}), bf16[16,4,2,16,256]{4,3,2,1,0:T(8,128)(2,1)S(1)}, u32[]{:S(2)}, u32[]{:S(2)}) async-start(bf16[16,4,2,16,256]{4,3,2,1,0:T(8,128)(2,1)} %bitcast.27), calls=%async_computation.1 | async-start | bytes 2097152 | tf_op jit(solution)/shard_map/all_to_all | solution.py:184
  21.6 1.3 %convert_add_fusion.5 = (f32[2,256,256]{2,1,0:T(8,128)S(1)}, f32[2,256,256]{2,1,0:T(8,128)S(1)}) fusion(bf16[8,2,256,256]{3,2,1,0:T(8,128)(2,1)} %collective-permute-done.2, s32[]{:T(128)S(6)} %select_n.109, bf16[8,2,2,256,256]{4,3,2,1,0:T(8,128)(2,1)} %bitcast.95, s32[]{:T(128)S(6)} %select_n.101, s32[]{:T(128)S(6)} %select_n.105), kind=kLoop, calls=%fused_computation.10 | loop fusion | flops 786432 | bytes 2097164 | tf_op jit(solution)/shard_map/add | solution.py:165
  22.9 0.8 add_convert_fusion.6
  23.7 0.1 collective-permute-start.3
  23.8 0.1 add_convert_fusion.5
  23.9 2.7 %collective-permute-start.6 = (bf16[2,256,256]{2,1,0:T(8,128)(2,1)S(1)}, bf16[2,256,256]{2,1,0:T(8,128)(2,1)S(1)}, u32[]{:S(2)}, u32[]{:S(2)}) collective-permute-start(bf16[2,256,256]{2,1,0:T(8,128)(2,1)S(1)} %add_convert_fusion.5), channel_id=1, source_target_pairs={{0,224},{32,0},{64,32},{96,64},{128,96},{160,128},{192,160},{224,1... | collective-permute-start | bytes 786440 | tf_op jit(solution)/shard_map/ppermute | solution.py:139
  26.7 1.3 %convert_add_fusion.3 = (f32[2,256,256]{2,1,0:T(8,128)S(1)}, f32[2,256,256]{2,1,0:T(8,128)S(1)}) fusion(bf16[8,2,256,256]{3,2,1,0:T(8,128)(2,1)} %collective-permute-done.2, s32[]{:T(128)S(6)} %select_n.113, bf16[8,2,2,256,256]{4,3,2,1,0:T(8,128)(2,1)} %bitcast.96, s32[]{:T(128)S(6)} %select_n.101, s32[]{:T(128)S(6)} %select_n.110), kind=kLoop, calls=%fused_computation.8 | loop fusion | flops 786432 | bytes 2097164 | tf_op jit(solution)/shard_map/add | solution.py:165
  28.0 3.8 %collective-permute-done.3 = bf16[2,256,256]{2,1,0:T(8,128)(2,1)S(1)} collective-permute-done((bf16[2,256,256]{2,1,0:T(8,128)(2,1)S(1)}, bf16[2,256,256]{2,1,0:T(8,128)(2,1)S(1)}, u32[]{:S(2)}, u32[]{:S(2)}) %collective-permute-start.3) | collective-permute-done | bytes 262176 | tf_op jit(solution)/shard_map/ppermute | solution.py:139
  31.8 0.1 collective-permute-start.5
  32.0 2.7 %collective-permute-start.8 = (bf16[2,256,256]{2,1,0:T(8,128)(2,1)S(1)}, bf16[2,256,256]{2,1,0:T(8,128)(2,1)S(1)}, u32[]{:S(2)}, u32[]{:S(2)}) collective-permute-start(bf16[2,256,256]{2,1,0:T(8,128)(2,1)S(1)} %add_convert_fusion.3), channel_id=1, source_target_pairs={{0,224},{32,0},{64,32},{96,64},{128,96},{160,128},{192,160},{224,1... | collective-permute-start | bytes 786440 | tf_op jit(solution)/shard_map/ppermute | solution.py:139
  34.8 1.3 %convert_add_fusion.1 = (f32[2,256,256]{2,1,0:T(8,128)S(1)}, f32[2,256,256]{2,1,0:T(8,128)S(1)}) fusion(bf16[8,2,256,256]{3,2,1,0:T(8,128)(2,1)} %collective-permute-done.2, s32[]{:T(128)S(6)} %select_n.116, bf16[8,2,2,256,256]{4,3,2,1,0:T(8,128)(2,1)} %bitcast.97, s32[]{:T(128)S(6)} %select_n.101, s32[]{:T(128)S(6)} %select_n.114), kind=kLoop, calls=%fused_computation.6 | loop fusion | flops 786432 | bytes 2097164 | tf_op jit(solution)/shard_map/add | solution.py:165
  36.1 2.9 %collective-permute-done.5 = bf16[2,256,256]{2,1,0:T(8,128)(2,1)S(1)} collective-permute-done((bf16[2,256,256]{2,1,0:T(8,128)(2,1)S(1)}, bf16[2,256,256]{2,1,0:T(8,128)(2,1)S(1)}, u32[]{:S(2)}, u32[]{:S(2)}) %collective-permute-start.5) | collective-permute-done | bytes 262176 | tf_op jit(solution)/shard_map/ppermute | solution.py:139
  39.0 0.1 collective-permute-start.7
  39.2 2.7 %collective-permute-start.9 = (bf16[2,256,256]{2,1,0:T(8,128)(2,1)S(1)}, bf16[2,256,256]{2,1,0:T(8,128)(2,1)S(1)}, u32[]{:S(2)}, u32[]{:S(2)}) collective-permute-start(bf16[2,256,256]{2,1,0:T(8,128)(2,1)S(1)} %add_convert_fusion.1), channel_id=1, source_target_pairs={{0,224},{32,0},{64,32},{96,64},{128,96},{160,128},{192,160},{224,1... | collective-permute-start | bytes 786440 | tf_op jit(solution)/shard_map/ppermute | solution.py:139
  41.9 0.5 iota_add_fusion
  42.5 1.0 copy-done
  43.4 2.1 %pick.2 = bf16[32,2,16,256]{3,2,1,0:T(8,128)(2,1)} custom-call(s32[32]{0:T(128)} %get-tuple-element.54.source_ref, bf16[64,2,16,256]{3,2,1,0:T(8,128)(2,1)} %bitcast.99), custom_call_target="tpu_custom_call" | custom-call | tf_op jit(solution)/shard_map/pick/pallas_call | solution.py:32
  45.6 6.1 %all-to-all-start.2 = ((bf16[16,2,2,16,256]{4,3,2,1,0:T(8,128)(2,1)}), bf16[16,2,2,16,256]{4,3,2,1,0:T(8,128)(2,1)S(1)}, u32[]{:S(2)}, u32[]{:S(2)}) async-start(bf16[16,2,2,16,256]{4,3,2,1,0:T(8,128)(2,1)} %bitcast.101), calls=%async_computation.2 | async-start | bytes 1048576 | tf_op jit(solution)/shard_map/all_to_all | solution.py:197
  51.7 1.1 convert_add_fusion
  52.8 0.1 add_convert_fusion.grad_ref
  52.9 0.8 copy.21
  53.7 7.0 %all-to-all-done.2.root_ref = bf16[16,2,2,16,256]{4,3,2,1,0:T(8,128)(2,1)S(1)} async-done(((bf16[16,2,2,16,256]{4,3,2,1,0:T(8,128)(2,1)}), bf16[16,2,2,16,256]{4,3,2,1,0:T(8,128)(2,1)S(1)}, u32[]{:S(2)}, u32[]{:S(2)}) %all-to-all-start.2) | async-done | bytes 524320 | tf_op jit(solution)/shard_map/all_to_all | solution.py:197
  60.7 0.8 copy-done.6
  61.5 2.2 %precondition.1 = bf16[2,256,256]{2,1,0:T(8,128)(2,1)} custom-call(bf16[2,256,256]{2,1,0:T(8,128)(2,1)} %copy-done.1, bf16[16,2,2,16,256]{4,3,2,1,0:T(8,128)(2,1)} %copy-done.6), custom_call_target="tpu_custom_call" | custom-call | tf_op jit(solution)/shard_map/precondition/pallas_call | solution.py:51
  63.8 1.5 %collective-permute-start.10 = (bf16[2,256,256]{2,1,0:T(8,128)(2,1)}, bf16[2,256,256]{2,1,0:T(8,128)(2,1)S(1)}, u32[]{:S(2)}, u32[]{:S(2)}) collective-permute-start(bf16[2,256,256]{2,1,0:T(8,128)(2,1)} %precondition.1), channel_id=1, source_target_pairs={{0,32},{32,64},{64,96},{96,128},{128,160},{160,192},{192,224},{224... | collective-permute-start | bytes 786440 | tf_op jit(solution)/shard_map/ppermute | solution.py:139
  65.2 3.5 %all-to-all-start = ((bf16[16,2,16,256]{3,2,1,0:T(8,128)(2,1)}), bf16[16,2,16,256]{3,2,1,0:T(8,128)(2,1)S(1)}, u32[]{:S(2)}, u32[]{:S(2)}) async-start(bf16[16,2,16,256]{3,2,1,0:T(8,128)(2,1)} %bitcast.90), calls=%async_computation | async-start | bytes 524288 | tf_op jit(solution)/shard_map/all_to_all | solution.py:206
  68.8 0.1 select_reduce_fusion
  68.9 0.3 collective-permute-done.11
  69.2 1.3 %collective-permute-start.15 = (bf16[2,256,256]{2,1,0:T(8,128)(2,1)S(1)}, bf16[2,256,256]{2,1,0:T(8,128)(2,1)S(1)}, u32[]{:S(2)}, u32[]{:S(2)}) collective-permute-start(bf16[2,256,256]{2,1,0:T(8,128)(2,1)S(1)} %collective-permute-done.11), channel_id=1, source_target_pairs={{0,224},{32,0},{64,32},{96,64},{128,96},{160,128},{192,160},{224,1... | collective-permute-start | bytes 786440 | tf_op jit(solution)/shard_map/ppermute | solution.py:139
  70.5 0.5 collective-permute-start.14
  70.9 0.5 broadcast_add_fusion.source_ref
  71.5 4.6 %all-to-all-done = bf16[16,2,16,256]{3,2,1,0:T(8,128)(2,1)S(1)} async-done(((bf16[16,2,16,256]{3,2,1,0:T(8,128)(2,1)}), bf16[16,2,16,256]{3,2,1,0:T(8,128)(2,1)S(1)}, u32[]{:S(2)}, u32[]{:S(2)}) %all-to-all-start) | async-done | bytes 262176 | tf_op jit(solution)/shard_map/all_to_all | solution.py:206
  76.0 0.7 copy-done.9
  76.7 2.0 %pick.3 = bf16[64,16,256]{2,1,0:T(8,128)(2,1)} custom-call(s32[64]{0:T(128)} %broadcast_add_fusion.source_ref, bf16[32,16,256]{2,1,0:T(8,128)(2,1)} %bitcast.106), custom_call_target="tpu_custom_call" | custom-call | tf_op jit(solution)/shard_map/pick/pallas_call | solution.py:32
  78.7 3.6 %all-to-all-start.3 = ((bf16[16,4,16,256]{3,2,1,0:T(8,128)(2,1)}), bf16[16,4,16,256]{3,2,1,0:T(8,128)(2,1)S(1)}, u32[]{:S(2)}, u32[]{:S(2)}) async-start(bf16[16,4,16,256]{3,2,1,0:T(8,128)(2,1)} %bitcast.102), calls=%async_computation.3 | async-start | bytes 1048576 | tf_op jit(solution)/shard_map/all_to_all | solution.py:220
  82.3 0.1 collective-permute-start.17
  82.4 2.7 %collective-permute-start.18 = (bf16[2,256,256]{2,1,0:T(8,128)(2,1)S(1)}, bf16[2,256,256]{2,1,0:T(8,128)(2,1)S(1)}, u32[]{:S(2)}, u32[]{:S(2)}) collective-permute-start(bf16[2,256,256]{2,1,0:T(8,128)(2,1)S(1)} %collective-permute-done.15), channel_id=1, source_target_pairs={{0,224},{32,0},{64,32},{96,64},{128,96},{160,128},{192,160},{224,1... | collective-permute-start | bytes 786440 | tf_op jit(solution)/shard_map/ppermute | solution.py:139
  85.1 7.5 %collective-permute-start.13 = (bf16[2,2,256,256]{3,2,1,0:T(8,128)(2,1)S(1)}, bf16[2,2,256,256]{3,2,1,0:T(8,128)(2,1)S(1)}, u32[]{:S(2)}, u32[]{:S(2)}) collective-permute-start(bf16[2,2,256,256]{3,2,1,0:T(8,128)(2,1)S(1)} %pad_maximum_fusion.1.refs_2_), channel_id=1, source_target_pairs={{0,16},{16,0},{1,17},{17,1},{2,18},{18,2},{3,19},{19,3},{4,20},{20... | collective-permute-start | bytes 1572872 | tf_op jit(solution)/shard_map/ppermute | solution.py:142
  92.7 0.1 collective-permute-start.16
  92.9 6.5 %collective-permute-start.19 = (bf16[2,2,256,256]{3,2,1,0:T(8,128)(2,1)S(1)}, bf16[2,2,256,256]{3,2,1,0:T(8,128)(2,1)}, u32[]{:S(2)}, u32[]{:S(2)}) collective-permute-start(bf16[2,2,256,256]{3,2,1,0:T(8,128)(2,1)S(1)} %pad_maximum_fusion.3.refs_6_), channel_id=1, source_target_pairs={{0,16},{16,0},{1,17},{17,1},{2,18},{18,2},{3,19},{19,3},{4,20},{20... | collective-permute-start | bytes 1572872 | tf_op jit(solution)/shard_map/ppermute | solution.py:142
  99.4 0.1 collective-permute-start.12
  99.5 1.0 collective-permute-start.21
  100.5 0.7 collective-permute-done.12
  101.3 0.7 copy-done.13
  102.0 0.7 pad_add_fusion.where_ref
  102.6 4.3 %statistics.1 = (f32[4,256,256]{2,1,0:T(8,128)}, f32[4,256,256]{2,1,0:T(8,128)}) custom-call(bf16[16,4,16,256]{3,2,1,0:T(8,128)(2,1)} %copy-done.2, f32[4,256,256]{2,1,0:T(8,128)} %bitcast.103, f32[4,256,256]{2,1,0:T(8,128)} %bitcast.104), custom_call_target="tpu_custom_call" | custom-call | tf_op jit(solution)/shard_map/statistics/pallas_call | solution.py:74
  107.0 0.8 copy-done.10
  107.8 4.0 %place.2.refs_0_ = bf16[8,2,2,256,256]{4,3,2,1,0:T(8,128)(2,1)} custom-call(s32[2]{0:T(128)} %pad_add_fusion.where_ref, bf16[1,2,256,256]{3,2,1,0:T(8,128)(2,1)} %bitcast.105, bf16[1,2,256,256]{3,2,1,0:T(8,128)(2,1)} %bitcast.111, bf16[2,2,256,256]{3,2,1,0:T(8,128)(2,1)} %copy-done.3, bf16[2,2,256,256]{3,2,1,0:T(8,128)(2,1)} %copy-done.10, ...), custom_call_target="tpu_custom_call" | custom-call | tf_op jit(solution)/shard_map/place/pallas_call | solution.py:113
  111.8 0.8 collective-permute-start.22
  112.6 1.2 collective-permute-done.22.refs_2_
  113.8 0.7 copy-done.14
  114.5 1.9 %place.3 = bf16[8,2,2,256,256]{4,3,2,1,0:T(8,128)(2,1)} custom-call(s32[2]{0:T(128)} %pad_add_fusion.where_ref, bf16[8,2,2,256,256]{4,3,2,1,0:T(8,128)(2,1)} %place.2.refs_0_, bf16[2,1,256,256]{3,2,1,0:T(8,128)(2,1)} %copy-done.7, bf16[2,1,256,256]{3,2,1,0:T(8,128)(2,1)} %copy-done.14), custom_call_target="tpu_custom_call", output_to_operand_aliasing={{}: (1, {})} | custom-call | tf_op jit(solution)/shard_map/place/pallas_call | solution.py:113
  (65 shorter events, 0.7 us)
Async XLA Ops:
  0.6 12.4 %copy-start.15 = (s32[512]{0:T(512)S(1)}, s32[512]{0:T(512)}, u32[]{:S(2)}) copy-start(s32[512]{0:T(512)} %param.11) | copy-start | bytes 6148
  1.6 5.2 %collective-permute-start = (bf16[2,256,256]{2,1,0:T(8,128)(2,1)S(1)}, bf16[2,256,256]{2,1,0:T(8,128)(2,1)S(1)}, u32[]{:S(2)}, u32[]{:S(2)}) collective-permute-start(bf16[2,256,256]{2,1,0:T(8,128)(2,1)S(1)} %dynamic-slice_bitcast_fusion.1), channel_id=1, source_target_pairs={{0,16},{16,0},{1,17},{17,1},{2,18},{18,2},{3,19},{19,3},{4,20},{20... | collective-permute-start | bytes 786440 | tf_op jit(solution)/shard_map/ppermute | solution.py:142
  5.0 4.1 %copy-start.11 = (bf16[1,1,4,256,256]{4,3,2,1,0:T(8,128)(2,1)S(1)}, bf16[1,1,4,256,256]{4,3,2,1,0:T(8,128)(2,1)}, u32[]{:S(2)}) copy-start(bf16[1,1,4,256,256]{4,3,2,1,0:T(8,128)(2,1)} %param.10) | copy-start | bytes 1572868
  5.0 4.1 %copy-start.12 = (bf16[1,1,4,256,256]{4,3,2,1,0:T(8,128)(2,1)S(1)}, bf16[1,1,4,256,256]{4,3,2,1,0:T(8,128)(2,1)}, u32[]{:S(2)}) copy-start(bf16[1,1,4,256,256]{4,3,2,1,0:T(8,128)(2,1)} %param.9) | copy-start | bytes 1572868
  8.5 13.1 %collective-permute-start.2 = (bf16[8,2,256,256]{3,2,1,0:T(8,128)(2,1)S(1)}, bf16[8,2,256,256]{3,2,1,0:T(8,128)(2,1)}, u32[]{:S(2)}, u32[]{:S(2)}) collective-permute-start(bf16[8,2,256,256]{3,2,1,0:T(8,128)(2,1)S(1)} %dynamic-slice_bitcast_fusion), channel_id=1, source_target_pairs={{0,16},{16,0},{1,17},{17,1},{2,18},{18,2},{3,19},{19,3},{4,20},{20... | collective-permute-start | bytes 6291464 | tf_op jit(solution)/shard_map/ppermute | solution.py:142
  9.2 12.4 %collective-permute-start.4 = (bf16[1,256,256]{2,1,0:T(8,128)(2,1)}, bf16[1,256,256]{2,1,0:T(8,128)(2,1)S(1)}, u32[]{:S(2)}, u32[]{:S(2)}) collective-permute-start(bf16[1,256,256]{2,1,0:T(8,128)(2,1)} %get-tuple-element.51), channel_id=1, source_target_pairs={{0,224},{32,0},{64,32},{96,64},{128,96},{160,128},{192,160},{224,1... | collective-permute-start | bytes 393224 | tf_op jit(solution)/shard_map/ppermute | solution.py:139
  14.7 6.9 %collective-permute-start.1 = (bf16[1,256,256]{2,1,0:T(8,128)(2,1)S(1)}, bf16[1,256,256]{2,1,0:T(8,128)(2,1)S(1)}, u32[]{:S(2)}, u32[]{:S(2)}) collective-permute-start(bf16[1,256,256]{2,1,0:T(8,128)(2,1)S(1)} %get-tuple-element.52), channel_id=1, source_target_pairs={{0,32},{32,64},{64,96},{96,128},{128,160},{160,192},{192,224},{224... | collective-permute-start | bytes 393224 | tf_op jit(solution)/shard_map/ppermute | solution.py:139
  14.8 27.7 %all-to-all-start.1 = ((bf16[16,4,2,16,256]{4,3,2,1,0:T(8,128)(2,1)}), bf16[16,4,2,16,256]{4,3,2,1,0:T(8,128)(2,1)S(1)}, u32[]{:S(2)}, u32[]{:S(2)}) async-start(bf16[16,4,2,16,256]{4,3,2,1,0:T(8,128)(2,1)} %bitcast.27), calls=%async_computation.1 | async-start | bytes 2097152 | tf_op jit(solution)/shard_map/all_to_all | solution.py:184
  23.7 8.1 %collective-permute-start.3 = (bf16[2,256,256]{2,1,0:T(8,128)(2,1)S(1)}, bf16[2,256,256]{2,1,0:T(8,128)(2,1)S(1)}, u32[]{:S(2)}, u32[]{:S(2)}) collective-permute-start(bf16[2,256,256]{2,1,0:T(8,128)(2,1)S(1)} %add_convert_fusion.6), channel_id=1, source_target_pairs={{0,32},{32,64},{64,96},{96,128},{128,160},{160,192},{192,224},{224... | collective-permute-start | bytes 786440 | tf_op jit(solution)/shard_map/ppermute | solution.py:139
  23.9 8.0 %collective-permute-start.6 = (bf16[2,256,256]{2,1,0:T(8,128)(2,1)S(1)}, bf16[2,256,256]{2,1,0:T(8,128)(2,1)S(1)}, u32[]{:S(2)}, u32[]{:S(2)}) collective-permute-start(bf16[2,256,256]{2,1,0:T(8,128)(2,1)S(1)} %add_convert_fusion.5), channel_id=1, source_target_pairs={{0,224},{32,0},{64,32},{96,64},{128,96},{160,128},{192,160},{224,1... | collective-permute-start | bytes 786440 | tf_op jit(solution)/shard_map/ppermute | solution.py:139
  31.8 7.1 %collective-permute-start.5 = (bf16[2,256,256]{2,1,0:T(8,128)(2,1)S(1)}, bf16[2,256,256]{2,1,0:T(8,128)(2,1)S(1)}, u32[]{:S(2)}, u32[]{:S(2)}) collective-permute-start(bf16[2,256,256]{2,1,0:T(8,128)(2,1)S(1)} %add_convert_fusion.4), channel_id=1, source_target_pairs={{0,32},{32,64},{64,96},{96,128},{128,160},{160,192},{192,224},{224... | collective-permute-start | bytes 786440 | tf_op jit(solution)/shard_map/ppermute | solution.py:139
  32.0 7.1 %collective-permute-start.8 = (bf16[2,256,256]{2,1,0:T(8,128)(2,1)S(1)}, bf16[2,256,256]{2,1,0:T(8,128)(2,1)S(1)}, u32[]{:S(2)}, u32[]{:S(2)}) collective-permute-start(bf16[2,256,256]{2,1,0:T(8,128)(2,1)S(1)} %add_convert_fusion.3), channel_id=1, source_target_pairs={{0,224},{32,0},{64,32},{96,64},{128,96},{160,128},{192,160},{224,1... | collective-permute-start | bytes 786440 | tf_op jit(solution)/shard_map/ppermute | solution.py:139
  39.0 13.7 %collective-permute-start.7 = (bf16[2,256,256]{2,1,0:T(8,128)(2,1)S(1)}, bf16[2,256,256]{2,1,0:T(8,128)(2,1)S(1)}, u32[]{:S(2)}, u32[]{:S(2)}) collective-permute-start(bf16[2,256,256]{2,1,0:T(8,128)(2,1)S(1)} %add_convert_fusion.2), channel_id=1, source_target_pairs={{0,32},{32,64},{64,96},{96,128},{128,160},{160,192},{192,224},{224... | collective-permute-start | bytes 786440 | tf_op jit(solution)/shard_map/ppermute | solution.py:139
  39.2 13.6 %collective-permute-start.9 = (bf16[2,256,256]{2,1,0:T(8,128)(2,1)S(1)}, bf16[2,256,256]{2,1,0:T(8,128)(2,1)S(1)}, u32[]{:S(2)}, u32[]{:S(2)}) collective-permute-start(bf16[2,256,256]{2,1,0:T(8,128)(2,1)S(1)} %add_convert_fusion.1), channel_id=1, source_target_pairs={{0,224},{32,0},{64,32},{96,64},{128,96},{160,128},{192,160},{224,1... | collective-permute-start | bytes 786440 | tf_op jit(solution)/shard_map/ppermute | solution.py:139
  42.4 26.3 %copy-start.16 = (s32[32]{0:T(128)S(1)}, s32[32]{0:T(128)}, u32[]{:S(2)}) copy-start(s32[32]{0:T(128)} %get-tuple-element.54.source_ref) | copy-start | bytes 388
  42.5 1.0 copy-start
  45.6 15.1 %all-to-all-start.2 = ((bf16[16,2,2,16,256]{4,3,2,1,0:T(8,128)(2,1)}), bf16[16,2,2,16,256]{4,3,2,1,0:T(8,128)(2,1)S(1)}, u32[]{:S(2)}, u32[]{:S(2)}) async-start(bf16[16,2,2,16,256]{4,3,2,1,0:T(8,128)(2,1)} %bitcast.101), calls=%async_computation.2 | async-start | bytes 1048576 | tf_op jit(solution)/shard_map/all_to_all | solution.py:197
  52.9 7.8 %copy-start.1 = (bf16[2,256,256]{2,1,0:T(8,128)(2,1)}, bf16[2,256,256]{2,1,0:T(8,128)(2,1)S(1)}, u32[]{:S(2)}) copy-start(bf16[2,256,256]{2,1,0:T(8,128)(2,1)S(1)} %add_convert_fusion.grad_ref) | copy-start | bytes 786436
  60.7 0.8 copy-start.6
  63.7 35.6 %copy-start.8 = (bf16[2,256,256]{2,1,0:T(8,128)(2,1)S(1)}, bf16[2,256,256]{2,1,0:T(8,128)(2,1)}, u32[]{:S(2)}) copy-start(bf16[2,256,256]{2,1,0:T(8,128)(2,1)} %precondition.1) | copy-start | bytes 786436
  63.7 5.4 %collective-permute-start.11 = (bf16[2,256,256]{2,1,0:T(8,128)(2,1)}, bf16[2,256,256]{2,1,0:T(8,128)(2,1)S(1)}, u32[]{:S(2)}, u32[]{:S(2)}) collective-permute-start(bf16[2,256,256]{2,1,0:T(8,128)(2,1)} %precondition.1), channel_id=1, source_target_pairs={{0,224},{32,0},{64,32},{96,64},{128,96},{160,128},{192,160},{224,1... | collective-permute-start | bytes 786440 | tf_op jit(solution)/shard_map/ppermute | solution.py:139
  63.8 6.7 %collective-permute-start.10 = (bf16[2,256,256]{2,1,0:T(8,128)(2,1)}, bf16[2,256,256]{2,1,0:T(8,128)(2,1)S(1)}, u32[]{:S(2)}, u32[]{:S(2)}) collective-permute-start(bf16[2,256,256]{2,1,0:T(8,128)(2,1)} %precondition.1), channel_id=1, source_target_pairs={{0,32},{32,64},{64,96},{96,128},{128,160},{160,192},{192,224},{224... | collective-permute-start | bytes 786440 | tf_op jit(solution)/shard_map/ppermute | solution.py:139
  65.2 10.8 %all-to-all-start = ((bf16[16,2,16,256]{3,2,1,0:T(8,128)(2,1)}), bf16[16,2,16,256]{3,2,1,0:T(8,128)(2,1)S(1)}, u32[]{:S(2)}, u32[]{:S(2)}) async-start(bf16[16,2,16,256]{3,2,1,0:T(8,128)(2,1)} %bitcast.90), calls=%async_computation | async-start | bytes 524288 | tf_op jit(solution)/shard_map/all_to_all | solution.py:206
  69.2 13.1 %collective-permute-start.15 = (bf16[2,256,256]{2,1,0:T(8,128)(2,1)S(1)}, bf16[2,256,256]{2,1,0:T(8,128)(2,1)S(1)}, u32[]{:S(2)}, u32[]{:S(2)}) collective-permute-start(bf16[2,256,256]{2,1,0:T(8,128)(2,1)S(1)} %collective-permute-done.11), channel_id=1, source_target_pairs={{0,224},{32,0},{64,32},{96,64},{128,96},{160,128},{192,160},{224,1... | collective-permute-start | bytes 786440 | tf_op jit(solution)/shard_map/ppermute | solution.py:139
  70.5 11.8 %collective-permute-start.14 = (bf16[2,256,256]{2,1,0:T(8,128)(2,1)S(1)}, bf16[2,256,256]{2,1,0:T(8,128)(2,1)S(1)}, u32[]{:S(2)}, u32[]{:S(2)}) collective-permute-start(bf16[2,256,256]{2,1,0:T(8,128)(2,1)S(1)} %collective-permute-done.10), channel_id=1, source_target_pairs={{0,32},{32,64},{64,96},{96,128},{128,160},{160,192},{192,224},{224... | collective-permute-start | bytes 786440 | tf_op jit(solution)/shard_map/ppermute | solution.py:139
  76.0 0.7 copy-start.9
  78.7 14.1 %all-to-all-start.3 = ((bf16[16,4,16,256]{3,2,1,0:T(8,128)(2,1)}), bf16[16,4,16,256]{3,2,1,0:T(8,128)(2,1)S(1)}, u32[]{:S(2)}, u32[]{:S(2)}) async-start(bf16[16,4,16,256]{3,2,1,0:T(8,128)(2,1)} %bitcast.102), calls=%async_computation.3 | async-start | bytes 1048576 | tf_op jit(solution)/shard_map/all_to_all | solution.py:220
  82.3 10.5 %collective-permute-start.17 = (bf16[2,256,256]{2,1,0:T(8,128)(2,1)S(1)}, bf16[2,256,256]{2,1,0:T(8,128)(2,1)S(1)}, u32[]{:S(2)}, u32[]{:S(2)}) collective-permute-start(bf16[2,256,256]{2,1,0:T(8,128)(2,1)S(1)} %collective-permute-done.14), channel_id=1, source_target_pairs={{0,32},{32,64},{64,96},{96,128},{128,160},{160,192},{192,224},{224... | collective-permute-start | bytes 786440 | tf_op jit(solution)/shard_map/ppermute | solution.py:139
  82.4 10.4 %collective-permute-start.18 = (bf16[2,256,256]{2,1,0:T(8,128)(2,1)S(1)}, bf16[2,256,256]{2,1,0:T(8,128)(2,1)S(1)}, u32[]{:S(2)}, u32[]{:S(2)}) collective-permute-start(bf16[2,256,256]{2,1,0:T(8,128)(2,1)S(1)} %collective-permute-done.15), channel_id=1, source_target_pairs={{0,224},{32,0},{64,32},{96,64},{128,96},{160,128},{192,160},{224,1... | collective-permute-start | bytes 786440 | tf_op jit(solution)/shard_map/ppermute | solution.py:139
  85.1 21.9 %copy-start.3 = (bf16[2,2,256,256]{3,2,1,0:T(8,128)(2,1)}, bf16[2,2,256,256]{3,2,1,0:T(8,128)(2,1)S(1)}, u32[]{:S(2)}) copy-start(bf16[2,2,256,256]{3,2,1,0:T(8,128)(2,1)S(1)} %pad_maximum_fusion.1.refs_2_) | copy-start | bytes 1572868
  85.1 21.8 %collective-permute-start.13 = (bf16[2,2,256,256]{3,2,1,0:T(8,128)(2,1)S(1)}, bf16[2,2,256,256]{3,2,1,0:T(8,128)(2,1)S(1)}, u32[]{:S(2)}, u32[]{:S(2)}) collective-permute-start(bf16[2,2,256,256]{3,2,1,0:T(8,128)(2,1)S(1)} %pad_maximum_fusion.1.refs_2_), channel_id=1, source_target_pairs={{0,16},{16,0},{1,17},{17,1},{2,18},{18,2},{3,19},{19,3},{4,20},{20... | collective-permute-start | bytes 1572872 | tf_op jit(solution)/shard_map/ppermute | solution.py:142
  92.7 14.3 %copy-start.4 = (bf16[2,2,256,256]{3,2,1,0:T(8,128)(2,1)}, bf16[2,2,256,256]{3,2,1,0:T(8,128)(2,1)S(1)}, u32[]{:S(2)}) copy-start(bf16[2,2,256,256]{3,2,1,0:T(8,128)(2,1)S(1)} %pad_maximum_fusion.2.refs_4_) | copy-start | bytes 1572868
  92.7 14.3 %collective-permute-start.16 = (bf16[2,2,256,256]{3,2,1,0:T(8,128)(2,1)S(1)}, bf16[2,2,256,256]{3,2,1,0:T(8,128)(2,1)}, u32[]{:S(2)}, u32[]{:S(2)}) collective-permute-start(bf16[2,2,256,256]{3,2,1,0:T(8,128)(2,1)S(1)} %pad_maximum_fusion.2.refs_4_), channel_id=1, source_target_pairs={{0,16},{16,0},{1,17},{17,1},{2,18},{18,2},{3,19},{19,3},{4,20},{20... | collective-permute-start | bytes 1572872 | tf_op jit(solution)/shard_map/ppermute | solution.py:142
  92.8 9.9 %copy-start.2 = (bf16[16,4,16,256]{3,2,1,0:T(8,128)(2,1)}, bf16[16,4,16,256]{3,2,1,0:T(8,128)(2,1)S(1)}, u32[]{:S(2)}) copy-start(bf16[16,4,16,256]{3,2,1,0:T(8,128)(2,1)S(1)} %all-to-all-done.3.own_ref) | copy-start | bytes 1572868
  92.9 14.1 %copy-start.5 = (bf16[2,2,256,256]{3,2,1,0:T(8,128)(2,1)}, bf16[2,2,256,256]{3,2,1,0:T(8,128)(2,1)S(1)}, u32[]{:S(2)}) copy-start(bf16[2,2,256,256]{3,2,1,0:T(8,128)(2,1)S(1)} %pad_maximum_fusion.3.refs_6_) | copy-start | bytes 1572868
  92.9 14.1 %collective-permute-start.19 = (bf16[2,2,256,256]{3,2,1,0:T(8,128)(2,1)S(1)}, bf16[2,2,256,256]{3,2,1,0:T(8,128)(2,1)}, u32[]{:S(2)}, u32[]{:S(2)}) collective-permute-start(bf16[2,2,256,256]{3,2,1,0:T(8,128)(2,1)S(1)} %pad_maximum_fusion.3.refs_6_), channel_id=1, source_target_pairs={{0,16},{16,0},{1,17},{17,1},{2,18},{18,2},{3,19},{19,3},{4,20},{20... | collective-permute-start | bytes 1572872 | tf_op jit(solution)/shard_map/ppermute | solution.py:142
  99.4 1.9 %collective-permute-start.12 = (bf16[2,256,256]{2,1,0:T(8,128)(2,1)S(1)}, bf16[2,256,256]{2,1,0:T(8,128)(2,1)S(1)}, u32[]{:S(2)}, u32[]{:S(2)}) collective-permute-start(bf16[2,256,256]{2,1,0:T(8,128)(2,1)S(1)} %copy-done.8), channel_id=1, source_target_pairs={{0,16},{16,0},{1,17},{17,1},{2,18},{18,2},{3,19},{19,3},{4,20},{20... | collective-permute-start | bytes 786440 | tf_op jit(solution)/shard_map/ppermute | solution.py:142
  99.5 12.2 %collective-permute-start.21 = (bf16[1,256,256]{2,1,0:T(8,128)(2,1)S(1)}, bf16[1,256,256]{2,1,0:T(8,128)(2,1)S(1)}, u32[]{:S(2)}, u32[]{:S(2)}) collective-permute-start(bf16[1,256,256]{2,1,0:T(8,128)(2,1)S(1)} %slice.25), channel_id=1, source_target_pairs={{0,224},{32,0},{64,32},{96,64},{128,96},{160,128},{192,160},{224,1... | collective-permute-start | bytes 393224 | tf_op jit(solution)/shard_map/ppermute | solution.py:139
  101.3 0.7 copy-start.13
  102.0 9.8 %collective-permute-start.20 = (bf16[1,256,256]{2,1,0:T(8,128)(2,1)S(1)}, bf16[1,256,256]{2,1,0:T(8,128)(2,1)S(1)}, u32[]{:S(2)}, u32[]{:S(2)}) collective-permute-start(bf16[1,256,256]{2,1,0:T(8,128)(2,1)S(1)} %slice.24), channel_id=1, source_target_pairs={{0,32},{32,64},{64,96},{96,128},{128,160},{160,192},{192,224},{224... | collective-permute-start | bytes 393224 | tf_op jit(solution)/shard_map/ppermute | solution.py:139
  106.9 0.8 copy-start.10
  111.8 2.0 %copy-start.7 = (bf16[2,1,256,256]{3,2,1,0:T(8,128)(2,1)}, bf16[2,1,256,256]{3,2,1,0:T(8,128)(2,1)S(1)}, u32[]{:S(2)}) copy-start(bf16[2,1,256,256]{3,2,1,0:T(8,128)(2,1)S(1)} %pad_maximum_fusion.4.refs_1_) | copy-start | bytes 786436
  111.8 2.0 %collective-permute-start.22 = (bf16[2,1,256,256]{3,2,1,0:T(8,128)(2,1)S(1)}, bf16[2,1,256,256]{3,2,1,0:T(8,128)(2,1)S(1)}, u32[]{:S(2)}, u32[]{:S(2)}) collective-permute-start(bf16[2,1,256,256]{3,2,1,0:T(8,128)(2,1)S(1)} %pad_maximum_fusion.4.refs_1_), channel_id=1, source_target_pairs={{0,16},{16,0},{1,17},{17,1},{2,18},{18,2},{3,19},{19,3},{4,20},{20... | collective-permute-start | bytes 786440 | tf_op jit(solution)/shard_map/ppermute | solution.py:142
  113.8 0.7 copy-start.14

commit v4 on v3

--- a/solution.py
+++ b/solution.py
@@ -12,6 +12,11 @@
 SMEM = pl.BlockSpec(memory_space=pltpu.SMEM)
 VMEM = pl.BlockSpec(memory_space=pltpu.VMEM)
 ANYWHERE = pl.BlockSpec(memory_space=pl.ANY)
+LIMIT = pltpu.CompilerParams(vmem_limit_bytes=12 * 2**20)
+
+
+def near(value):
+    return pltpu.with_memory_space_constraint(value, pltpu.VMEM)
 
 
 def tie(value, *others):
@@ -34,8 +39,9 @@
         out_shape=jax.ShapeDtypeStruct((*source.shape, *values.shape[1:]), values.dtype),
         in_specs=[SMEM, VMEM],
         out_specs=VMEM,
+        compiler_params=LIMIT,
         name="pick",
-    )(source, values)
+    )(source, near(values))
 
 
 def precond_kernel(grad_ref, root_ref, out_ref):
@@ -53,13 +59,14 @@
         out_shape=jax.ShapeDtypeStruct(grads.shape, BF16),
         in_specs=[VMEM, VMEM],
         out_specs=VMEM,
+        compiler_params=LIMIT,
         name="precondition",
-    )(grads, roots)
+    )(near(grads), near(roots))
 
 
 def statistics_kernel(own_ref, left_ref, right_ref, left_out_ref, right_out_ref):
     peers, _, piece, cols = own_ref.shape
-    own = own_ref[:, 0].reshape(peers * piece, cols)
+    own = own_ref[:, pl.program_id(0)].reshape(peers * piece, cols)
     left_out_ref[0] = left_ref[0] + lax.dot_general(
         own, own, (((1,), (1,)), ((), ())), preferred_element_type=F32
     )
@@ -69,7 +76,7 @@
 
 
 def statistics(own, left, right):
-    peers, slots, piece, cols = own.shape
+    slots = own.shape[1]
     one = pl.BlockSpec((1, *left.shape[1:]), lambda s: (s, 0, 0))
     return pl.pallas_call(
         statistics_kernel,
@@ -78,10 +85,11 @@
             jax.ShapeDtypeStruct(left.shape, F32),
             jax.ShapeDtypeStruct(right.shape, F32),
         ),
-        in_specs=[pl.BlockSpec((peers, 1, piece, cols), lambda s: (0, s, 0, 0)), one, one],
+        in_specs=[VMEM, one, one],
         out_specs=(one, one),
+        compiler_params=LIMIT,
         name="statistics",
-    )(own, left, right)
+    )(near(own), left, right)
 
 
 def place(where, pieces, direction, shape):
@@ -109,7 +117,7 @@
         for copy in copies:
             copy.wait()
 
-    operands = ([] if fresh else [direction]) + [value for _, value in pieces]
+    operands = ([] if fresh else [direction]) + [near(value) for _, value in pieces]
     return pl.pallas_call(
         kernel,
         out_shape=jax.ShapeDtypeStruct(shape, BF16),
@@ -117,6 +125,7 @@
         out_specs=ANYWHERE,
         scratch_shapes=[pltpu.SemaphoreType.DMA((sum(len(p) for p, _ in pieces),))],
         input_output_aliases={} if fresh else {1: 0},
+        compiler_params=LIMIT,
         name="place",
     )(where, *operands)
 
@@ -197,7 +206,7 @@
             roots = lax.all_to_all(wanted, "mp", 0, 0, tiled=True)
         came = [hop(moving[way], way) for way in range(2)]
     blocks = (
-        came[0].astype(F32) + came[1].astype(F32) + base(0, *moving)
+        came[0].astype(F32) + came[1].astype(F32) + base(0, *moving, roots)
     ).astype(BF16)
 
     sliced = jnp.moveaxis(blocks.reshape(held, mp, piece, cols), 1, 0)

time: 117 us -> 108 us (0.923)
  Pallas kernels: 16.5 us -> 10.1 us
  waiting for transfers between devices: 20.6 us -> 16.9 us
  local copies, waits for them, and re-layouts: 9.64 us -> 7.87 us
  starting transfers between devices: 57.8 us -> 59.3 us
    ppermute x16, starting transfers between devices: 19.4 us -> 23.5 us  [hop(): return lax.ppermute(value, 'z', ways[way])]
    unnamed x34 -> x6, local copies, waits for them, and re-layouts: 4.67 us -> 1.24 us
    ppermute x16, waiting for transfers between devices: 7.08 us -> 3.8 us  [hop(): return lax.ppermute(value, 'z', ways[way])]
    all_to_all x1, waiting for transfers between devices: 0.01 us -> 2.87 us  [per_device(): spread = lax.all_to_all(spread, 'mp', 0, 0, tiled=True)]
    all_to_all x1, waiting for transfers between devices: 7.03 us -> 4.8 us  [per_device(): roots = lax.all_to_all(wanted, 'mp', 0, 0, tiled=True)]
    all_to_all x1, starting transfers between devices: 6.08 us -> 3.94 us  [per_device(): roots = lax.all_to_all(wanted, 'mp', 0, 0, tiled=True)]
    another operation x3, other arithmetic: 0.15 us -> 2.21 us  [per_device(): pair = jnp.stack(flow)]
    pallas_call x1, Pallas kernels: 4.31 us -> 2.36 us  [statistics(): pl.pallas_call(statistics_kernel, grid=(slots,), out_shape=(jax.ShapeDtyp...]
  transfers between devices with their start and end apart: 27 -> 27, of which waited for: 7 -> 5; matrix products, arithmetic and copies ran while one was open for 11% -> 13% of each run, Pallas kernels for 11% -> 8%
where the time goes in v4:
time: 108 us; the launch traced here: 107 us
  starting transfers between devices  59.3 us (55%)
  waiting for transfers between devices  16.9 us (16%)
  other arithmetic  11.2 us (10%)
  Pallas kernels  10.1 us (9%)
  local copies, waits for them, and re-layouts  7.87 us (7%)
  between operations  1.24 us (1%)
    ppermute x16, starting transfers between devices, hop(): return lax.ppermute(value, 'z', ways[way])  23.5 us
    ppermute x7, starting transfers between devices, swap(): return lax.ppermute(value, 'core', [(0, 1), (1, 0)])  16.5 us
    all_to_all x1, starting transfers between devices, per_device(): spread = lax.all_to_all(spread, 'mp', 0, 0, tiled=True)  6.76 us
    add x4, other arithmetic, base(): value = mine.reshape(held, rows, cols).astype(F32) + given.astype(F32)  4.99 us
    all_to_all x1, starting transfers between devices, per_device(): arrived = lax.all_to_all(sliced, 'mp', 0, 0, tiled=True)  4.9 us
    all_to_all x1, waiting for transfers between devices, per_device(): roots = lax.all_to_all(wanted, 'mp', 0, 0, tiled=True)  4.8 us
    pallas_call x2, Pallas kernels, place(): pl.pallas_call(kernel, out_shape=jax.ShapeDtypeStruct(shape, BF16), in_sp...  4.37 us
    all_to_all x1, waiting for transfers between devices, per_device(): arrived = lax.all_to_all(sliced, 'mp', 0, 0, tiled=True)  4.28 us
  transfers between devices with their start and end apart: 27, of which 5 were waited for; matrix products, arithmetic and copies ran while one was open for 13% of the time, Pallas kernels for 8%

profile of v4, /device:TPU:1, one launch (start us, length us, event | category | flops | bytes accessed | tf_op | source)
XLA Modules:
  0.0 106.7 jit_solution(10097225004137749618)
XLA Ops:
  0.7 1.0 dynamic-slice_bitcast_fusion.1
  1.6 3.3 %collective-permute-start = (bf16[2,256,256]{2,1,0:T(8,128)(2,1)S(1)}, bf16[2,256,256]{2,1,0:T(8,128)(2,1)S(1)}, u32[]{:S(2)}, u32[]{:S(2)}) collective-permute-start(bf16[2,256,256]{2,1,0:T(8,128)(2,1)S(1)} %dynamic-slice_bitcast_fusion.1), channel_id=1, source_target_pairs={{0,16},{16,0},{1,17},{17,1},{2,18},{18,2},{3,19},{19,3},{4,20},{20... | collective-permute-start | bytes 786440 | tf_op jit(solution)/shard_map/ppermute | solution.py:151
  5.0 1.7 %dynamic-slice_bitcast_fusion = bf16[8,2,256,256]{3,2,1,0:T(8,128)(2,1)S(1)} fusion(bf16[8,2,2,256,256]{4,3,2,1,0:T(8,128)(2,1)} %bitcast.100, s32[]{:T(128)S(6)} %select_n.102), kind=kLoop, calls=%fused_computation | loop fusion | bytes 4194308 | tf_op jit(solution)/shard_map/reshape | solution.py:180
  6.7 1.7 %fusion = (bf16[1,256,256]{2,1,0:T(8,128)(2,1)}, bf16[1,256,256]{2,1,0:T(8,128)(2,1)S(1)}) fusion(bf16[2,256,256]{2,1,0:T(8,128)(2,1)S(1)} %collective-permute-done, bf16[8,2,2,256,256]{4,3,2,1,0:T(8,128)(2,1)} %bitcast.101, s32[]{:T(128)S(6)} %select_n.100, s32[]{:T(128)S(6)} %select_n.101, s32[]{:T(128)S(6)} %add.243), kind=kLoop, calls=%fused_computation.21 | loop fusion | flops 524288 | bytes 786444 | tf_op jit(solution)/shard_map/convert_element_type | solution.py:183
  8.4 0.0 collective-permute-start.2
  8.4 0.1 reshape.139
  8.6 0.1 reshape.140
  8.7 0.2 convert_reduce_fusion
  8.9 1.3 %pad_maximum_fusion = bf16[4,2,16,16,256]{4,3,2,0,1:T(8,128)(2,1)S(1)} fusion(bf16[4,1,16,16,256]{4,3,2,0,1:T(8,128)(2,1)} %bitcast.106, bf16[4,1,16,16,256]{4,3,2,0,1:T(8,128)(2,1)} %bitcast.107), kind=kLoop, calls=%fused_computation.1 | loop fusion | flops 524288 | bytes 2097152 | tf_op jit(solution)/shard_map/stack | solution.py:189
  10.2 3.9 %collective-permute-start.4 = (bf16[1,256,256]{2,1,0:T(8,128)(2,1)}, bf16[1,256,256]{2,1,0:T(8,128)(2,1)S(1)}, u32[]{:S(2)}, u32[]{:S(2)}) collective-permute-start(bf16[1,256,256]{2,1,0:T(8,128)(2,1)} %get-tuple-element.51), channel_id=1, source_target_pairs={{0,224},{32,0},{64,32},{96,64},{128,96},{160,128},{192,160},{224,1... | collective-permute-start | bytes 393224 | tf_op jit(solution)/shard_map/ppermute | solution.py:148
  14.1 1.1 %copy.19 = bf16[4,2,16,16,256]{4,3,1,0,2:T(8,128)(2,1)} copy(bf16[4,2,16,16,256]{4,3,2,0,1:T(8,128)(2,1)S(1)} %pad_maximum_fusion) | data formatting | bytes 2097152 | tf_op jit(solution)/shard_map/stack | solution.py:189
  15.3 0.0 collective-permute-start.1
  15.3 6.8 %all-to-all-start = ((bf16[16,4,2,16,256]{4,3,2,1,0:T(8,128)(2,1)}), bf16[16,4,2,16,256]{4,3,2,1,0:T(8,128)(2,1)S(1)}, u32[]{:S(2)}, u32[]{:S(2)}) async-start(bf16[16,4,2,16,256]{4,3,2,1,0:T(8,128)(2,1)} %bitcast.23), calls=%async_computation | async-start | bytes 2097152 | tf_op jit(solution)/shard_map/all_to_all | solution.py:193
  22.1 1.3 %convert_add_fusion.5 = (f32[2,256,256]{2,1,0:T(8,128)S(1)}, f32[2,256,256]{2,1,0:T(8,128)S(1)}) fusion(bf16[8,2,256,256]{3,2,1,0:T(8,128)(2,1)} %collective-permute-done.2, s32[]{:T(128)S(6)} %select_n.109, bf16[8,2,2,256,256]{4,3,2,1,0:T(8,128)(2,1)} %bitcast.102, s32[]{:T(128)S(6)} %select_n.101, s32[]{:T(128)S(6)} %select_n.105), kind=kLoop, calls=%fused_computation.10 | loop fusion | flops 786432 | bytes 2097164 | tf_op jit(solution)/shard_map/add | solution.py:174
  23.4 0.1 add_convert_fusion.6
  23.6 0.1 collective-permute-start.3
  23.7 0.1 add_convert_fusion.5
  23.8 2.7 %collective-permute-start.6 = (bf16[2,256,256]{2,1,0:T(8,128)(2,1)S(1)}, bf16[2,256,256]{2,1,0:T(8,128)(2,1)S(1)}, u32[]{:S(2)}, u32[]{:S(2)}) collective-permute-start(bf16[2,256,256]{2,1,0:T(8,128)(2,1)S(1)} %add_convert_fusion.5), channel_id=1, source_target_pairs={{0,224},{32,0},{64,32},{96,64},{128,96},{160,128},{192,160},{224,1... | collective-permute-start | bytes 786440 | tf_op jit(solution)/shard_map/ppermute | solution.py:148
  26.5 1.3 %convert_add_fusion.3 = (f32[2,256,256]{2,1,0:T(8,128)S(1)}, f32[2,256,256]{2,1,0:T(8,128)S(1)}) fusion(bf16[8,2,256,256]{3,2,1,0:T(8,128)(2,1)} %collective-permute-done.2, s32[]{:T(128)S(6)} %select_n.113, bf16[8,2,2,256,256]{4,3,2,1,0:T(8,128)(2,1)} %bitcast.103, s32[]{:T(128)S(6)} %select_n.101, s32[]{:T(128)S(6)} %select_n.110), kind=kLoop, calls=%fused_computation.8 | loop fusion | flops 786432 | bytes 2097164 | tf_op jit(solution)/shard_map/add | solution.py:174
  27.8 3.8 %collective-permute-done.3 = bf16[2,256,256]{2,1,0:T(8,128)(2,1)S(1)} collective-permute-done((bf16[2,256,256]{2,1,0:T(8,128)(2,1)S(1)}, bf16[2,256,256]{2,1,0:T(8,128)(2,1)S(1)}, u32[]{:S(2)}, u32[]{:S(2)}) %collective-permute-start.3) | collective-permute-done | bytes 262176 | tf_op jit(solution)/shard_map/ppermute | solution.py:148
  31.6 0.1 add_convert_fusion.4
  31.7 0.1 collective-permute-start.5
  31.8 0.1 add_convert_fusion.3
  31.8 2.7 %collective-permute-start.8 = (bf16[2,256,256]{2,1,0:T(8,128)(2,1)S(1)}, bf16[2,256,256]{2,1,0:T(8,128)(2,1)S(1)}, u32[]{:S(2)}, u32[]{:S(2)}) collective-permute-start(bf16[2,256,256]{2,1,0:T(8,128)(2,1)S(1)} %add_convert_fusion.3), channel_id=1, source_target_pairs={{0,224},{32,0},{64,32},{96,64},{128,96},{160,128},{192,160},{224,1... | collective-permute-start | bytes 786440 | tf_op jit(solution)/shard_map/ppermute | solution.py:148
  34.6 2.9 %all-to-all-done = bf16[16,4,2,16,256]{4,3,2,1,0:T(8,128)(2,1)S(1)} async-done(((bf16[16,4,2,16,256]{4,3,2,1,0:T(8,128)(2,1)}), bf16[16,4,2,16,256]{4,3,2,1,0:T(8,128)(2,1)S(1)}, u32[]{:S(2)}, u32[]{:S(2)}) %all-to-all-start) | async-done | bytes 1048608 | tf_op jit(solution)/shard_map/all_to_all | solution.py:193
  37.4 1.4 %pick.2 = bf16[32,2,16,256]{3,2,1,0:T(8,128)(2,1)} custom-call(s32[32]{0:T(128)S(1)} %get-tuple-element.54.source_ref, bf16[64,2,16,256]{3,2,1,0:T(8,128)(2,1)S(1)} %bitcast.91), custom_call_target="tpu_custom_call" | custom-call | tf_op jit(solution)/shard_map/pick/pallas_call | solution.py:37
  38.9 3.9 %all-to-all-start.1 = ((bf16[16,2,2,16,256]{4,3,2,1,0:T(8,128)(2,1)}), bf16[16,2,2,16,256]{4,3,2,1,0:T(8,128)(2,1)S(1)}, u32[]{:S(2)}, u32[]{:S(2)}) async-start(bf16[16,2,2,16,256]{4,3,2,1,0:T(8,128)(2,1)} %bitcast.25), calls=%async_computation.1 | async-start | bytes 1048576 | tf_op jit(solution)/shard_map/all_to_all | solution.py:206
  42.8 1.3 %convert_add_fusion.1 = (f32[2,256,256]{2,1,0:T(8,128)S(1)}, f32[2,256,256]{2,1,0:T(8,128)S(1)}) fusion(bf16[8,2,256,256]{3,2,1,0:T(8,128)(2,1)} %collective-permute-done.2, s32[]{:T(128)S(6)} %select_n.116, bf16[8,2,2,256,256]{4,3,2,1,0:T(8,128)(2,1)} %bitcast.104, s32[]{:T(128)S(6)} %select_n.101, s32[]{:T(128)S(6)} %select_n.114), kind=kLoop, calls=%fused_computation.6 | loop fusion | flops 786432 | bytes 2097164 | tf_op jit(solution)/shard_map/add | solution.py:174
  44.2 0.1 add_convert_fusion.2
  44.2 0.1 collective-permute-start.7
  44.3 0.1 add_convert_fusion.1
  44.4 2.7 %collective-permute-start.9 = (bf16[2,256,256]{2,1,0:T(8,128)(2,1)S(1)}, bf16[2,256,256]{2,1,0:T(8,128)(2,1)S(1)}, u32[]{:S(2)}, u32[]{:S(2)}) collective-permute-start(bf16[2,256,256]{2,1,0:T(8,128)(2,1)S(1)} %add_convert_fusion.1), channel_id=1, source_target_pairs={{0,224},{32,0},{64,32},{96,64},{128,96},{160,128},{192,160},{224,1... | collective-permute-start | bytes 786440 | tf_op jit(solution)/shard_map/ppermute | solution.py:148
  47.1 4.8 %all-to-all-done.1.root_ref = bf16[16,2,2,16,256]{4,3,2,1,0:T(8,128)(2,1)S(1)} async-done(((bf16[16,2,2,16,256]{4,3,2,1,0:T(8,128)(2,1)}), bf16[16,2,2,16,256]{4,3,2,1,0:T(8,128)(2,1)S(1)}, u32[]{:S(2)}, u32[]{:S(2)}) %all-to-all-start.1) | async-done | bytes 524320 | tf_op jit(solution)/shard_map/all_to_all | solution.py:206
  51.9 1.1 %convert_add_fusion = f32[2,256,256]{2,1,0:T(8,128)S(1)} fusion(bf16[8,2,256,256]{3,2,1,0:T(8,128)(2,1)} %collective-permute-done.2, s32[]{:T(128)S(6)} %select_n.118, bf16[8,2,2,256,256]{4,3,2,1,0:T(8,128)(2,1)} %bitcast.105, s32[]{:T(128)S(6)} %select_n.101), kind=kLoop, calls=%fused_computation.5 | loop fusion | flops 393216 | bytes 1048584 | tf_op jit(solution)/shard_map/add | solution.py:174
  53.0 0.0 copy-start
  53.0 0.1 add_convert_fusion.grad_ref
  53.2 0.7 copy.21
  53.9 0.4 precondition.1
  54.3 2.5 %collective-permute-start.11 = (bf16[2,256,256]{2,1,0:T(8,128)(2,1)S(1)}, bf16[2,256,256]{2,1,0:T(8,128)(2,1)S(1)}, u32[]{:S(2)}, u32[]{:S(2)}) collective-permute-start(bf16[2,256,256]{2,1,0:T(8,128)(2,1)S(1)} %precondition.1), channel_id=1, source_target_pairs={{0,224},{32,0},{64,32},{96,64},{128,96},{160,128},{192,160},{224,1... | collective-permute-start | bytes 786440 | tf_op jit(solution)/shard_map/ppermute | solution.py:148
  56.7 4.9 %all-to-all-start.2 = ((bf16[16,2,16,256]{3,2,1,0:T(8,128)(2,1)}), bf16[16,2,16,256]{3,2,1,0:T(8,128)(2,1)S(1)}, u32[]{:S(2)}, u32[]{:S(2)}) async-start(bf16[16,2,16,256]{3,2,1,0:T(8,128)(2,1)} %bitcast.90), calls=%async_computation.2 | async-start | bytes 524288 | tf_op jit(solution)/shard_map/all_to_all | solution.py:215
  61.7 0.1 select_reduce_fusion
  61.8 2.9 %collective-permute-start.15 = (bf16[2,256,256]{2,1,0:T(8,128)(2,1)S(1)}, bf16[2,256,256]{2,1,0:T(8,128)(2,1)}, u32[]{:S(2)}, u32[]{:S(2)}) collective-permute-start(bf16[2,256,256]{2,1,0:T(8,128)(2,1)S(1)} %collective-permute-done.11), channel_id=1, source_target_pairs={{0,224},{32,0},{64,32},{96,64},{128,96},{160,128},{192,160},{224,1... | collective-permute-start | bytes 786440 | tf_op jit(solution)/shard_map/ppermute | solution.py:148
  64.7 4.3 %all-to-all-done.2 = bf16[16,2,16,256]{3,2,1,0:T(8,128)(2,1)S(1)} async-done(((bf16[16,2,16,256]{3,2,1,0:T(8,128)(2,1)}), bf16[16,2,16,256]{3,2,1,0:T(8,128)(2,1)S(1)}, u32[]{:S(2)}, u32[]{:S(2)}) %all-to-all-start.2) | async-done | bytes 262176 | tf_op jit(solution)/shard_map/all_to_all | solution.py:215
  69.0 1.5 %pick.3 = bf16[64,16,256]{2,1,0:T(8,128)(2,1)} custom-call(s32[64]{0:T(128)S(1)} %broadcast_add_fusion.source_ref, bf16[32,16,256]{2,1,0:T(8,128)(2,1)S(1)} %bitcast.96), custom_call_target="tpu_custom_call" | custom-call | tf_op jit(solution)/shard_map/pick/pallas_call | solution.py:37
  70.5 3.7 %all-to-all-start.3 = ((bf16[16,4,16,256]{3,2,1,0:T(8,128)(2,1)}), bf16[16,4,16,256]{3,2,1,0:T(8,128)(2,1)S(1)}, u32[]{:S(2)}, u32[]{:S(2)}) async-start(bf16[16,4,16,256]{3,2,1,0:T(8,128)(2,1)} %bitcast.31), calls=%async_computation.3 | async-start | bytes 1048576 | tf_op jit(solution)/shard_map/all_to_all | solution.py:229
  74.2 0.1 collective-permute-start.17
  74.3 2.7 %collective-permute-start.18 = (bf16[2,256,256]{2,1,0:T(8,128)(2,1)}, bf16[2,256,256]{2,1,0:T(8,128)(2,1)}, u32[]{:S(2)}, u32[]{:S(2)}) collective-permute-start(bf16[2,256,256]{2,1,0:T(8,128)(2,1)} %collective-permute-done.15), channel_id=1, source_target_pairs={{0,224},{32,0},{64,32},{96,64},{128,96},{160,128},{192,160},{224,1... | collective-permute-start | bytes 786440 | tf_op jit(solution)/shard_map/ppermute | solution.py:148
  77.0 0.1 pad_maximum_fusion.1.refs_2_
  77.0 6.8 %collective-permute-start.13 = (bf16[2,2,256,256]{3,2,1,0:T(8,128)(2,1)S(1)}, bf16[2,2,256,256]{3,2,1,0:T(8,128)(2,1)S(1)}, u32[]{:S(2)}, u32[]{:S(2)}) collective-permute-start(bf16[2,2,256,256]{3,2,1,0:T(8,128)(2,1)S(1)} %pad_maximum_fusion.1.refs_2_), channel_id=1, source_target_pairs={{0,16},{16,0},{1,17},{17,1},{2,18},{18,2},{3,19},{19,3},{4,20},{20... | collective-permute-start | bytes 1572872 | tf_op jit(solution)/shard_map/ppermute | solution.py:151
  83.8 1.1 %pad_maximum_fusion.2.refs_4_ = bf16[2,2,256,256]{3,2,1,0:T(8,128)(2,1)S(1)} fusion(bf16[1,2,256,256]{3,2,1,0:T(8,128)(2,1)} %bitcast.39, bf16[1,2,256,256]{3,2,1,0:T(8,128)(2,1)} %bitcast.38), kind=kLoop, calls=%fused_computation.3 | loop fusion | flops 262144 | bytes 1048576 | tf_op jit(solution)/shard_map/stack | solution.py:232
  84.9 0.1 collective-permute-start.16
  85.0 1.1 %pad_maximum_fusion.3.refs_6_ = bf16[2,2,256,256]{3,2,1,0:T(8,128)(2,1)S(1)} fusion(bf16[1,2,256,256]{3,2,1,0:T(8,128)(2,1)} %bitcast.41, bf16[1,2,256,256]{3,2,1,0:T(8,128)(2,1)} %bitcast.40), kind=kLoop, calls=%fused_computation.4 | loop fusion | flops 262144 | bytes 1048576 | tf_op jit(solution)/shard_map/stack | solution.py:232
  86.1 5.4 %collective-permute-start.19 = (bf16[2,2,256,256]{3,2,1,0:T(8,128)(2,1)S(1)}, bf16[2,2,256,256]{3,2,1,0:T(8,128)(2,1)S(1)}, u32[]{:S(2)}, u32[]{:S(2)}) collective-permute-start(bf16[2,2,256,256]{3,2,1,0:T(8,128)(2,1)S(1)} %pad_maximum_fusion.3.refs_6_), channel_id=1, source_target_pairs={{0,16},{16,0},{1,17},{17,1},{2,18},{18,2},{3,19},{19,3},{4,20},{20... | collective-permute-start | bytes 1572872 | tf_op jit(solution)/shard_map/ppermute | solution.py:151
  91.5 0.1 collective-permute-start.12
  91.6 0.9 slice.24
  92.5 0.9 slice.25
  93.4 3.0 %collective-permute-start.21 = (bf16[1,256,256]{2,1,0:T(8,128)(2,1)S(1)}, bf16[1,256,256]{2,1,0:T(8,128)(2,1)S(1)}, u32[]{:S(2)}, u32[]{:S(2)}) collective-permute-start(bf16[1,256,256]{2,1,0:T(8,128)(2,1)S(1)} %slice.25), channel_id=1, source_target_pairs={{0,224},{32,0},{64,32},{96,64},{128,96},{160,128},{192,160},{224,1... | collective-permute-start | bytes 393224 | tf_op jit(solution)/shard_map/ppermute | solution.py:148
  96.5 0.1 pad_add_fusion.where_ref
  96.6 1.2 %copy-done.1 = f32[1,1,4,256,256]{4,3,2,1,0:T(8,128)S(1)} copy-done((f32[1,1,4,256,256]{4,3,2,1,0:T(8,128)S(1)}, f32[1,1,4,256,256]{4,3,2,1,0:T(8,128)}, u32[]{:S(2)}) %copy-start.1) | copy-done | bytes 1048600
  97.8 2.4 %statistics.1 = (f32[4,256,256]{2,1,0:T(8,128)}, f32[4,256,256]{2,1,0:T(8,128)}) custom-call(bf16[16,4,16,256]{3,2,1,0:T(8,128)(2,1)S(1)} %all-to-all-done.3.own_ref, f32[4,256,256]{2,1,0:T(8,128)S(1)} %bitcast.93, f32[4,256,256]{2,1,0:T(8,128)S(1)} %bitcast.94), custom_call_target="tpu_custom_call" | custom-call | tf_op jit(solution)/shard_map/statistics/pallas_call | solution.py:81
  100.2 3.0 %place.2.refs_0_ = bf16[8,2,2,256,256]{4,3,2,1,0:T(8,128)(2,1)} custom-call(s32[2]{0:T(128)S(1)} %pad_add_fusion.where_ref, bf16[1,2,256,256]{3,2,1,0:T(8,128)(2,1)S(1)} %bitcast.95, bf16[1,2,256,256]{3,2,1,0:T(8,128)(2,1)S(1)} %bitcast.97, bf16[2,2,256,256]{3,2,1,0:T(8,128)(2,1)S(1)} %pad_maximum_fusion.1.refs_2_, ...), custom_call_target="tpu_custom_call" | custom-call | tf_op jit(solution)/shard_map/place/pallas_call | solution.py:121
  103.2 0.8 collective-permute-start.22
  104.0 1.2 %collective-permute-done.22.refs_2_ = bf16[2,1,256,256]{3,2,1,0:T(8,128)(2,1)S(1)} collective-permute-done((bf16[2,1,256,256]{3,2,1,0:T(8,128)(2,1)S(1)}, bf16[2,1,256,256]{3,2,1,0:T(8,128)(2,1)S(1)}, u32[]{:S(2)}, u32[]{:S(2)}) %collective-permute-start.22) | collective-permute-done | bytes 262176 | tf_op jit(solution)/shard_map/ppermute | solution.py:151
  105.2 1.4 %place.3 = bf16[8,2,2,256,256]{4,3,2,1,0:T(8,128)(2,1)} custom-call(s32[2]{0:T(128)S(1)} %pad_add_fusion.where_ref, bf16[8,2,2,256,256]{4,3,2,1,0:T(8,128)(2,1)} %place.2.refs_0_, bf16[2,1,256,256]{3,2,1,0:T(8,128)(2,1)S(1)} %pad_maximum_fusion.4.refs_1_, bf16[2,1,256,256]{3,2,1,0:T(8,128)(2,1)S(1)} %collective-permute-done.22.refs_2_), custom_call_target="tpu_custom_call", output_to_operand_aliasing={{}: (1, {})} | custom-call | tf_op jit(solution)/shard_map/place/pallas_call | solution.py:121
  (37 shorter events, 0.2 us)
Async XLA Ops:
  0.6 7.8 %copy-start.2 = (s32[512]{0:T(512)S(1)}, s32[512]{0:T(512)}, u32[]{:S(2)}) copy-start(s32[512]{0:T(512)} %param.11) | copy-start | bytes 6148
  1.6 5.1 %collective-permute-start = (bf16[2,256,256]{2,1,0:T(8,128)(2,1)S(1)}, bf16[2,256,256]{2,1,0:T(8,128)(2,1)S(1)}, u32[]{:S(2)}, u32[]{:S(2)}) collective-permute-start(bf16[2,256,256]{2,1,0:T(8,128)(2,1)S(1)} %dynamic-slice_bitcast_fusion.1), channel_id=1, source_target_pairs={{0,16},{16,0},{1,17},{17,1},{2,18},{18,2},{3,19},{19,3},{4,20},{20... | collective-permute-start | bytes 786440 | tf_op jit(solution)/shard_map/ppermute | solution.py:151
  8.4 13.7 %collective-permute-start.2 = (bf16[8,2,256,256]{3,2,1,0:T(8,128)(2,1)S(1)}, bf16[8,2,256,256]{3,2,1,0:T(8,128)(2,1)}, u32[]{:S(2)}, u32[]{:S(2)}) collective-permute-start(bf16[8,2,256,256]{3,2,1,0:T(8,128)(2,1)S(1)} %dynamic-slice_bitcast_fusion), channel_id=1, source_target_pairs={{0,16},{16,0},{1,17},{17,1},{2,18},{18,2},{3,19},{19,3},{4,20},{20... | collective-permute-start | bytes 6291464 | tf_op jit(solution)/shard_map/ppermute | solution.py:151
  10.2 11.8 %collective-permute-start.4 = (bf16[1,256,256]{2,1,0:T(8,128)(2,1)}, bf16[1,256,256]{2,1,0:T(8,128)(2,1)S(1)}, u32[]{:S(2)}, u32[]{:S(2)}) collective-permute-start(bf16[1,256,256]{2,1,0:T(8,128)(2,1)} %get-tuple-element.51), channel_id=1, source_target_pairs={{0,224},{32,0},{64,32},{96,64},{128,96},{160,128},{192,160},{224,1... | collective-permute-start | bytes 393224 | tf_op jit(solution)/shard_map/ppermute | solution.py:148
  15.3 6.8 %collective-permute-start.1 = (bf16[1,256,256]{2,1,0:T(8,128)(2,1)S(1)}, bf16[1,256,256]{2,1,0:T(8,128)(2,1)S(1)}, u32[]{:S(2)}, u32[]{:S(2)}) collective-permute-start(bf16[1,256,256]{2,1,0:T(8,128)(2,1)S(1)} %get-tuple-element.52), channel_id=1, source_target_pairs={{0,32},{32,64},{64,96},{96,128},{128,160},{160,192},{192,224},{224... | collective-permute-start | bytes 393224 | tf_op jit(solution)/shard_map/ppermute | solution.py:148
  15.3 22.2 %all-to-all-start = ((bf16[16,4,2,16,256]{4,3,2,1,0:T(8,128)(2,1)}), bf16[16,4,2,16,256]{4,3,2,1,0:T(8,128)(2,1)S(1)}, u32[]{:S(2)}, u32[]{:S(2)}) async-start(bf16[16,4,2,16,256]{4,3,2,1,0:T(8,128)(2,1)} %bitcast.23), calls=%async_computation | async-start | bytes 2097152 | tf_op jit(solution)/shard_map/all_to_all | solution.py:193
  23.6 8.0 %collective-permute-start.3 = (bf16[2,256,256]{2,1,0:T(8,128)(2,1)S(1)}, bf16[2,256,256]{2,1,0:T(8,128)(2,1)S(1)}, u32[]{:S(2)}, u32[]{:S(2)}) collective-permute-start(bf16[2,256,256]{2,1,0:T(8,128)(2,1)S(1)} %add_convert_fusion.6), channel_id=1, source_target_pairs={{0,32},{32,64},{64,96},{96,128},{128,160},{160,192},{192,224},{224... | collective-permute-start | bytes 786440 | tf_op jit(solution)/shard_map/ppermute | solution.py:148
  23.8 8.0 %collective-permute-start.6 = (bf16[2,256,256]{2,1,0:T(8,128)(2,1)S(1)}, bf16[2,256,256]{2,1,0:T(8,128)(2,1)S(1)}, u32[]{:S(2)}, u32[]{:S(2)}) collective-permute-start(bf16[2,256,256]{2,1,0:T(8,128)(2,1)S(1)} %add_convert_fusion.5), channel_id=1, source_target_pairs={{0,224},{32,0},{64,32},{96,64},{128,96},{160,128},{192,160},{224,1... | collective-permute-start | bytes 786440 | tf_op jit(solution)/shard_map/ppermute | solution.py:148
  31.7 12.5 %collective-permute-start.5 = (bf16[2,256,256]{2,1,0:T(8,128)(2,1)S(1)}, bf16[2,256,256]{2,1,0:T(8,128)(2,1)S(1)}, u32[]{:S(2)}, u32[]{:S(2)}) collective-permute-start(bf16[2,256,256]{2,1,0:T(8,128)(2,1)S(1)} %add_convert_fusion.4), channel_id=1, source_target_pairs={{0,32},{32,64},{64,96},{96,128},{128,160},{160,192},{192,224},{224... | collective-permute-start | bytes 786440 | tf_op jit(solution)/shard_map/ppermute | solution.py:148
  31.8 12.5 %collective-permute-start.8 = (bf16[2,256,256]{2,1,0:T(8,128)(2,1)S(1)}, bf16[2,256,256]{2,1,0:T(8,128)(2,1)S(1)}, u32[]{:S(2)}, u32[]{:S(2)}) collective-permute-start(bf16[2,256,256]{2,1,0:T(8,128)(2,1)S(1)} %add_convert_fusion.3), channel_id=1, source_target_pairs={{0,224},{32,0},{64,32},{96,64},{128,96},{160,128},{192,160},{224,1... | collective-permute-start | bytes 786440 | tf_op jit(solution)/shard_map/ppermute | solution.py:148
  38.9 13.0 %all-to-all-start.1 = ((bf16[16,2,2,16,256]{4,3,2,1,0:T(8,128)(2,1)}), bf16[16,2,2,16,256]{4,3,2,1,0:T(8,128)(2,1)S(1)}, u32[]{:S(2)}, u32[]{:S(2)}) async-start(bf16[16,2,2,16,256]{4,3,2,1,0:T(8,128)(2,1)} %bitcast.25), calls=%async_computation.1 | async-start | bytes 1048576 | tf_op jit(solution)/shard_map/all_to_all | solution.py:206
  44.2 8.8 %collective-permute-start.7 = (bf16[2,256,256]{2,1,0:T(8,128)(2,1)S(1)}, bf16[2,256,256]{2,1,0:T(8,128)(2,1)S(1)}, u32[]{:S(2)}, u32[]{:S(2)}) collective-permute-start(bf16[2,256,256]{2,1,0:T(8,128)(2,1)S(1)} %add_convert_fusion.2), channel_id=1, source_target_pairs={{0,32},{32,64},{64,96},{96,128},{128,160},{160,192},{192,224},{224... | collective-permute-start | bytes 786440 | tf_op jit(solution)/shard_map/ppermute | solution.py:148
  44.4 8.6 %collective-permute-start.9 = (bf16[2,256,256]{2,1,0:T(8,128)(2,1)S(1)}, bf16[2,256,256]{2,1,0:T(8,128)(2,1)S(1)}, u32[]{:S(2)}, u32[]{:S(2)}) collective-permute-start(bf16[2,256,256]{2,1,0:T(8,128)(2,1)S(1)} %add_convert_fusion.1), channel_id=1, source_target_pairs={{0,224},{32,0},{64,32},{96,64},{128,96},{160,128},{192,160},{224,1... | collective-permute-start | bytes 786440 | tf_op jit(solution)/shard_map/ppermute | solution.py:148
  53.0 43.5 %copy-start = (f32[1,1,4,256,256]{4,3,2,1,0:T(8,128)S(1)}, f32[1,1,4,256,256]{4,3,2,1,0:T(8,128)}, u32[]{:S(2)}) copy-start(f32[1,1,4,256,256]{4,3,2,1,0:T(8,128)} %param.7) | copy-start | bytes 3145732
  54.3 7.5 %collective-permute-start.11 = (bf16[2,256,256]{2,1,0:T(8,128)(2,1)S(1)}, bf16[2,256,256]{2,1,0:T(8,128)(2,1)S(1)}, u32[]{:S(2)}, u32[]{:S(2)}) collective-permute-start(bf16[2,256,256]{2,1,0:T(8,128)(2,1)S(1)} %precondition.1), channel_id=1, source_target_pairs={{0,224},{32,0},{64,32},{96,64},{128,96},{160,128},{192,160},{224,1... | collective-permute-start | bytes 786440 | tf_op jit(solution)/shard_map/ppermute | solution.py:148
  56.7 7.9 %collective-permute-start.10 = (bf16[2,256,256]{2,1,0:T(8,128)(2,1)S(1)}, bf16[2,256,256]{2,1,0:T(8,128)(2,1)S(1)}, u32[]{:S(2)}, u32[]{:S(2)}) collective-permute-start(bf16[2,256,256]{2,1,0:T(8,128)(2,1)S(1)} %precondition.1), channel_id=1, source_target_pairs={{0,32},{32,64},{64,96},{96,128},{128,160},{160,192},{192,224},{224... | collective-permute-start | bytes 786440 | tf_op jit(solution)/shard_map/ppermute | solution.py:148
  56.7 12.2 %all-to-all-start.2 = ((bf16[16,2,16,256]{3,2,1,0:T(8,128)(2,1)}), bf16[16,2,16,256]{3,2,1,0:T(8,128)(2,1)S(1)}, u32[]{:S(2)}, u32[]{:S(2)}) async-start(bf16[16,2,16,256]{3,2,1,0:T(8,128)(2,1)} %bitcast.90), calls=%async_computation.2 | async-start | bytes 524288 | tf_op jit(solution)/shard_map/all_to_all | solution.py:215
  61.8 12.5 %collective-permute-start.15 = (bf16[2,256,256]{2,1,0:T(8,128)(2,1)S(1)}, bf16[2,256,256]{2,1,0:T(8,128)(2,1)}, u32[]{:S(2)}, u32[]{:S(2)}) collective-permute-start(bf16[2,256,256]{2,1,0:T(8,128)(2,1)S(1)} %collective-permute-done.11), channel_id=1, source_target_pairs={{0,224},{32,0},{64,32},{96,64},{128,96},{160,128},{192,160},{224,1... | collective-permute-start | bytes 786440 | tf_op jit(solution)/shard_map/ppermute | solution.py:148
  64.7 9.5 %collective-permute-start.14 = (bf16[2,256,256]{2,1,0:T(8,128)(2,1)S(1)}, bf16[2,256,256]{2,1,0:T(8,128)(2,1)}, u32[]{:S(2)}, u32[]{:S(2)}) collective-permute-start(bf16[2,256,256]{2,1,0:T(8,128)(2,1)S(1)} %collective-permute-done.10), channel_id=1, source_target_pairs={{0,32},{32,64},{64,96},{96,128},{128,160},{160,192},{192,224},{224... | collective-permute-start | bytes 786440 | tf_op jit(solution)/shard_map/ppermute | solution.py:148
  70.5 14.5 %all-to-all-start.3 = ((bf16[16,4,16,256]{3,2,1,0:T(8,128)(2,1)}), bf16[16,4,16,256]{3,2,1,0:T(8,128)(2,1)S(1)}, u32[]{:S(2)}, u32[]{:S(2)}) async-start(bf16[16,4,16,256]{3,2,1,0:T(8,128)(2,1)} %bitcast.31), calls=%async_computation.3 | async-start | bytes 1048576 | tf_op jit(solution)/shard_map/all_to_all | solution.py:229
  74.2 10.8 %collective-permute-start.17 = (bf16[2,256,256]{2,1,0:T(8,128)(2,1)}, bf16[2,256,256]{2,1,0:T(8,128)(2,1)}, u32[]{:S(2)}, u32[]{:S(2)}) collective-permute-start(bf16[2,256,256]{2,1,0:T(8,128)(2,1)} %collective-permute-done.14), channel_id=1, source_target_pairs={{0,32},{32,64},{64,96},{96,128},{128,160},{160,192},{192,224},{224... | collective-permute-start | bytes 786440 | tf_op jit(solution)/shard_map/ppermute | solution.py:148
  74.3 10.7 %collective-permute-start.18 = (bf16[2,256,256]{2,1,0:T(8,128)(2,1)}, bf16[2,256,256]{2,1,0:T(8,128)(2,1)}, u32[]{:S(2)}, u32[]{:S(2)}) collective-permute-start(bf16[2,256,256]{2,1,0:T(8,128)(2,1)} %collective-permute-done.15), channel_id=1, source_target_pairs={{0,224},{32,0},{64,32},{96,64},{128,96},{160,128},{192,160},{224,1... | collective-permute-start | bytes 786440 | tf_op jit(solution)/shard_map/ppermute | solution.py:148
  77.0 23.1 %collective-permute-start.13 = (bf16[2,2,256,256]{3,2,1,0:T(8,128)(2,1)S(1)}, bf16[2,2,256,256]{3,2,1,0:T(8,128)(2,1)S(1)}, u32[]{:S(2)}, u32[]{:S(2)}) collective-permute-start(bf16[2,2,256,256]{3,2,1,0:T(8,128)(2,1)S(1)} %pad_maximum_fusion.1.refs_2_), channel_id=1, source_target_pairs={{0,16},{16,0},{1,17},{17,1},{2,18},{18,2},{3,19},{19,3},{4,20},{20... | collective-permute-start | bytes 1572872 | tf_op jit(solution)/shard_map/ppermute | solution.py:151
  84.9 15.3 %collective-permute-start.16 = (bf16[2,2,256,256]{3,2,1,0:T(8,128)(2,1)S(1)}, bf16[2,2,256,256]{3,2,1,0:T(8,128)(2,1)}, u32[]{:S(2)}, u32[]{:S(2)}) collective-permute-start(bf16[2,2,256,256]{3,2,1,0:T(8,128)(2,1)S(1)} %pad_maximum_fusion.2.refs_4_), channel_id=1, source_target_pairs={{0,16},{16,0},{1,17},{17,1},{2,18},{18,2},{3,19},{19,3},{4,20},{20... | collective-permute-start | bytes 1572872 | tf_op jit(solution)/shard_map/ppermute | solution.py:151
  86.1 14.1 %collective-permute-start.19 = (bf16[2,2,256,256]{3,2,1,0:T(8,128)(2,1)S(1)}, bf16[2,2,256,256]{3,2,1,0:T(8,128)(2,1)S(1)}, u32[]{:S(2)}, u32[]{:S(2)}) collective-permute-start(bf16[2,2,256,256]{3,2,1,0:T(8,128)(2,1)S(1)} %pad_maximum_fusion.3.refs_6_), channel_id=1, source_target_pairs={{0,16},{16,0},{1,17},{17,1},{2,18},{18,2},{3,19},{19,3},{4,20},{20... | collective-permute-start | bytes 1572872 | tf_op jit(solution)/shard_map/ppermute | solution.py:151
  91.5 5.0 %collective-permute-start.12 = (bf16[2,256,256]{2,1,0:T(8,128)(2,1)S(1)}, bf16[2,256,256]{2,1,0:T(8,128)(2,1)S(1)}, u32[]{:S(2)}, u32[]{:S(2)}) collective-permute-start(bf16[2,256,256]{2,1,0:T(8,128)(2,1)S(1)} %precondition.1), channel_id=1, source_target_pairs={{0,16},{16,0},{1,17},{17,1},{2,18},{18,2},{3,19},{19,3},{4,20},{20... | collective-permute-start | bytes 786440 | tf_op jit(solution)/shard_map/ppermute | solution.py:151
  93.4 9.7 %collective-permute-start.21 = (bf16[1,256,256]{2,1,0:T(8,128)(2,1)S(1)}, bf16[1,256,256]{2,1,0:T(8,128)(2,1)S(1)}, u32[]{:S(2)}, u32[]{:S(2)}) collective-permute-start(bf16[1,256,256]{2,1,0:T(8,128)(2,1)S(1)} %slice.25), channel_id=1, source_target_pairs={{0,224},{32,0},{64,32},{96,64},{128,96},{160,128},{192,160},{224,1... | collective-permute-start | bytes 393224 | tf_op jit(solution)/shard_map/ppermute | solution.py:148
  96.5 6.7 %collective-permute-start.20 = (bf16[1,256,256]{2,1,0:T(8,128)(2,1)S(1)}, bf16[1,256,256]{2,1,0:T(8,128)(2,1)S(1)}, u32[]{:S(2)}, u32[]{:S(2)}) collective-permute-start(bf16[1,256,256]{2,1,0:T(8,128)(2,1)S(1)} %slice.24), channel_id=1, source_target_pairs={{0,32},{32,64},{64,96},{96,128},{128,160},{160,192},{192,224},{224... | collective-permute-start | bytes 393224 | tf_op jit(solution)/shard_map/ppermute | solution.py:148
  96.6 1.2 %copy-start.1 = (f32[1,1,4,256,256]{4,3,2,1,0:T(8,128)S(1)}, f32[1,1,4,256,256]{4,3,2,1,0:T(8,128)}, u32[]{:S(2)}) copy-start(f32[1,1,4,256,256]{4,3,2,1,0:T(8,128)} %param.8) | copy-start | bytes 3145732
  103.2 1.9 %collective-permute-start.22 = (bf16[2,1,256,256]{3,2,1,0:T(8,128)(2,1)S(1)}, bf16[2,1,256,256]{3,2,1,0:T(8,128)(2,1)S(1)}, u32[]{:S(2)}, u32[]{:S(2)}) collective-permute-start(bf16[2,1,256,256]{3,2,1,0:T(8,128)(2,1)S(1)} %pad_maximum_fusion.4.refs_1_), channel_id=1, source_target_pairs={{0,16},{16,0},{1,17},{17,1},{2,18},{18,2},{3,19},{19,3},{4,20},{20... | collective-permute-start | bytes 786440 | tf_op jit(solution)/shard_map/ppermute | solution.py:151

commit v5 on v4

--- a/solution.py
+++ b/solution.py
@@ -44,24 +44,49 @@
     )(source, near(values))
 
 
-def precond_kernel(grad_ref, root_ref, out_ref):
+def precond_kernel(grad_ref, root_ref, out_ref, sliced_ref):
     held, rows, cols = grad_ref.shape
     for j in range(held):
         left = root_ref[:, j, 0].reshape(rows, rows)
         right = root_ref[:, j, 1].reshape(cols, cols)
         half = jnp.dot(left, grad_ref[j], preferred_element_type=F32).astype(BF16)
         out_ref[j] = jnp.dot(half, right, preferred_element_type=F32).astype(BF16)
+        sliced_ref[:, j] = grad_ref[j].reshape(sliced_ref.shape[0], *sliced_ref.shape[2:])
 
 
 def precondition(grads, roots):
+    held, rows, cols = grads.shape
+    peers = roots.shape[0]
     return pl.pallas_call(
         precond_kernel,
-        out_shape=jax.ShapeDtypeStruct(grads.shape, BF16),
+        out_shape=(
+            jax.ShapeDtypeStruct(grads.shape, BF16),
+            jax.ShapeDtypeStruct((peers, held, rows // peers, cols), BF16),
+        ),
         in_specs=[VMEM, VMEM],
-        out_specs=VMEM,
+        out_specs=(VMEM, VMEM),
         compiler_params=LIMIT,
         name="precondition",
     )(near(grads), near(roots))
+
+
+def part_kernel(up_ref, down_ref, up_part_ref, down_part_ref, pair_ref):
+    up_part_ref[...] = up_ref[0:1]
+    down_part_ref[...] = down_ref[1:2]
+    pair_ref[0] = up_ref[...]
+    pair_ref[1] = down_ref[...]
+
+
+def part(up, down):
+    one = jax.ShapeDtypeStruct((1, *up.shape[1:]), BF16)
+    return pl.pallas_call(
+        part_kernel,
+        out_shape=(one, one, jax.ShapeDtypeStruct((2, *up.shape), BF16)),
+        in_specs=[VMEM, VMEM],
+        out_specs=(VMEM, VMEM, VMEM),
+        compiler_params=LIMIT,
+        name="part",
+    )(near(up), near(down))
 
 
 def statistics_kernel(own_ref, left_ref, right_ref, left_out_ref, right_out_ref):
@@ -89,7 +114,7 @@
         out_specs=(one, one),
         compiler_params=LIMIT,
         name="statistics",
-    )(near(own), left, right)
+    )(near(own), *(pltpu.with_memory_space_constraint(x, pltpu.HBM) for x in (left, right)))
 
 
 def place(where, pieces, direction, shape):
@@ -209,14 +234,13 @@
         came[0].astype(F32) + came[1].astype(F32) + base(0, *moving, roots)
     ).astype(BF16)
 
-    sliced = jnp.moveaxis(blocks.reshape(held, mp, piece, cols), 1, 0)
-    result = precondition(tie(blocks, sliced), roots)
+    result, sliced = precondition(blocks, roots)
 
     arrived = lax.all_to_all(sliced, "mp", 0, 0, tiled=True)
 
     shape = (zs, 2, held, rows, cols)
     where = jnp.stack([z, core])
-    pieces = [([(0, False, None)], result[None]), ([(0, True, None)], swap(result)[None])]
+    pieces = []
     flow = [result, result]
     for step in range(1, far):
         flow = [hop(flow[way], way) for way in range(2)]
@@ -229,10 +253,17 @@
             own = lax.all_to_all(
                 to_owner.reshape(mp, slots, piece, cols), "mp", 0, 0, tiled=True
             )
-        pair = jnp.stack(flow)
-        for cross, value in ((False, pair), (True, swap(pair))):
-            pieces.append(([(-step, cross, None), (step, cross, None)], value))
-    flow = [hop(flow[way][way : way + 1], way) for way in range(2)]
+        steps = [-step, step]
+        if step == far - 1:
+            *halves, group = part(*flow)
+        elif step == 1:
+            steps = [0, *steps]
+            group = jnp.stack([result, *flow])
+        else:
+            group = jnp.stack(flow)
+        for cross, value in ((False, group), (True, swap(group))):
+            pieces.append(([(at, cross, None) for at in steps], value))
+    flow = [hop(halves[way], way) for way in range(2)]
     left_updated, right_updated = statistics(own, left_stats[0, 0], right_stats[0, 0])
     direction = place(tie(where, left_updated), pieces, None, shape)
     pair = jnp.stack(tie(flow, direction))

time: 108 us -> 105 us (0.972)
  local copies, waits for them, and re-layouts: 7.87 us -> 4.09 us
  Pallas kernels: 10.1 us -> 13.1 us
    slice x2 -> x0, local copies, waits for them, and re-layouts: 1.83 us -> none  [per_device(): flow = [hop(flow[way][way:way + 1], way) for way in range(2)]]
    pallas_call x1, Pallas kernels: 2.36 us -> 4.18 us  [statistics(): pl.pallas_call(statistics_kernel, grid=(slots,), out_shape=(jax.ShapeDtyp...]
    pallas_call x1 -> x2, Pallas kernels: 0.4 us -> 2.05 us  [the longest x1 1.05 us: precondition(): pl.pallas_call(precond_kernel, out_shape=(jax.ShapeDtypeStruct(grads.shap...]
    unnamed x6 -> x2, local copies, waits for them, and re-layouts: 1.24 us -> 0.01 us
    another operation x3 -> x2, other arithmetic: 2.21 us -> 1.17 us  [the longest x1 1.08 us: per_device(): group = jnp.stack(flow)]
    ppermute x7 -> x6, starting transfers between devices: 16.5 us -> 16.1 us  [swap(): return lax.ppermute(value, 'core', [(0, 1), (1, 0)])]
  transfers between devices with their start and end apart: 27 -> 26, of which waited for: 5 -> 5; matrix products, arithmetic and copies ran while one was open for 13% -> 11% of each run, Pallas kernels for 8% -> 10%
where the time goes in v5:
time: 105 us; the launch traced here: 104 us
  starting transfers between devices  58.8 us (56%)
  waiting for transfers between devices  16.9 us (16%)
  Pallas kernels  13.1 us (12%)
  other arithmetic  10.2 us (10%)
  local copies, waits for them, and re-layouts  4.09 us (4%)
  between operations  1.22 us (1%)
    ppermute x16, starting transfers between devices, hop(): return lax.ppermute(value, 'z', ways[way])  23.4 us
    ppermute x6, starting transfers between devices, swap(): return lax.ppermute(value, 'core', [(0, 1), (1, 0)])  16.1 us
    all_to_all x1, starting transfers between devices, per_device(): spread = lax.all_to_all(spread, 'mp', 0, 0, tiled=True)  6.76 us
    add x4, other arithmetic, base(): value = mine.reshape(held, rows, cols).astype(F32) + given.astype(F32)  4.99 us
    all_to_all x1, starting transfers between devices, per_device(): arrived = lax.all_to_all(sliced, 'mp', 0, 0, tiled=True)  4.93 us
    all_to_all x1, waiting for transfers between devices, per_device(): roots = lax.all_to_all(wanted, 'mp', 0, 0, tiled=True)  4.79 us
    all_to_all x1, waiting for transfers between devices, per_device(): arrived = lax.all_to_all(sliced, 'mp', 0, 0, tiled=True)  4.28 us
    pallas_call x1, Pallas kernels, statistics(): pl.pallas_call(statistics_kernel, grid=(slots,), out_shape=(jax.ShapeDtyp...  4.18 us
  transfers between devices with their start and end apart: 26, of which 5 were waited for; matrix products, arithmetic and copies ran while one was open for 11% of the time, Pallas kernels for 10%

profile of v5, /device:TPU:1, one launch (start us, length us, event | category | flops | bytes accessed | tf_op | source)
XLA Modules:
  0.0 104.3 jit_solution(18127475999301441794)
XLA Ops:
  0.7 1.0 dynamic-slice_bitcast_fusion.1
  1.6 3.3 %collective-permute-start = (bf16[2,256,256]{2,1,0:T(8,128)(2,1)S(1)}, bf16[2,256,256]{2,1,0:T(8,128)(2,1)S(1)}, u32[]{:S(2)}, u32[]{:S(2)}) collective-permute-start(bf16[2,256,256]{2,1,0:T(8,128)(2,1)S(1)} %dynamic-slice_bitcast_fusion.1), channel_id=1, source_target_pairs={{0,16},{16,0},{1,17},{17,1},{2,18},{18,2},{3,19},{19,3},{4,20},{20... | collective-permute-start | bytes 786440 | tf_op jit(solution)/shard_map/ppermute | solution.py:176
  5.0 1.7 %dynamic-slice_bitcast_fusion = bf16[8,2,256,256]{3,2,1,0:T(8,128)(2,1)S(1)} fusion(bf16[8,2,2,256,256]{4,3,2,1,0:T(8,128)(2,1)} %bitcast.89, s32[]{:T(128)S(6)} %select_n.102), kind=kLoop, calls=%fused_computation | loop fusion | bytes 4194308 | tf_op jit(solution)/shard_map/reshape | solution.py:205
  6.7 1.7 %fusion = (bf16[1,256,256]{2,1,0:T(8,128)(2,1)}, bf16[1,256,256]{2,1,0:T(8,128)(2,1)S(1)}) fusion(bf16[2,256,256]{2,1,0:T(8,128)(2,1)S(1)} %collective-permute-done, bf16[8,2,2,256,256]{4,3,2,1,0:T(8,128)(2,1)} %bitcast.90, s32[]{:T(128)S(6)} %select_n.100, s32[]{:T(128)S(6)} %select_n.101, s32[]{:T(128)S(6)} %add.243), kind=kLoop, calls=%fused_computation.20 | loop fusion | flops 524288 | bytes 786444 | tf_op jit(solution)/shard_map/convert_element_type | solution.py:208
  8.4 0.0 collective-permute-start.2
  8.4 0.1 reshape.136
  8.6 0.1 reshape.137
  8.7 0.2 convert_reduce_fusion
  8.9 1.3 %pad_maximum_fusion = bf16[4,2,16,16,256]{4,3,2,0,1:T(8,128)(2,1)S(1)} fusion(bf16[4,1,16,16,256]{4,3,2,0,1:T(8,128)(2,1)} %bitcast.97, bf16[4,1,16,16,256]{4,3,2,0,1:T(8,128)(2,1)} %bitcast.98), kind=kLoop, calls=%fused_computation.1 | loop fusion | flops 524288 | bytes 2097152 | tf_op jit(solution)/shard_map/stack | solution.py:214
  10.2 3.9 %collective-permute-start.4 = (bf16[1,256,256]{2,1,0:T(8,128)(2,1)}, bf16[1,256,256]{2,1,0:T(8,128)(2,1)S(1)}, u32[]{:S(2)}, u32[]{:S(2)}) collective-permute-start(bf16[1,256,256]{2,1,0:T(8,128)(2,1)} %get-tuple-element.59), channel_id=1, source_target_pairs={{0,224},{32,0},{64,32},{96,64},{128,96},{160,128},{192,160},{224,1... | collective-permute-start | bytes 393224 | tf_op jit(solution)/shard_map/ppermute | solution.py:173
  14.1 1.1 %copy.16 = bf16[4,2,16,16,256]{4,3,1,0,2:T(8,128)(2,1)} copy(bf16[4,2,16,16,256]{4,3,2,0,1:T(8,128)(2,1)S(1)} %pad_maximum_fusion) | data formatting | bytes 2097152 | tf_op jit(solution)/shard_map/stack | solution.py:214
  15.3 0.0 collective-permute-start.1
  15.3 6.8 %all-to-all-start = ((bf16[16,4,2,16,256]{4,3,2,1,0:T(8,128)(2,1)}), bf16[16,4,2,16,256]{4,3,2,1,0:T(8,128)(2,1)S(1)}, u32[]{:S(2)}, u32[]{:S(2)}) async-start(bf16[16,4,2,16,256]{4,3,2,1,0:T(8,128)(2,1)} %bitcast.23), calls=%async_computation | async-start | bytes 2097152 | tf_op jit(solution)/shard_map/all_to_all | solution.py:218
  22.1 1.3 %convert_add_fusion.5 = (f32[2,256,256]{2,1,0:T(8,128)S(1)}, f32[2,256,256]{2,1,0:T(8,128)S(1)}) fusion(bf16[8,2,256,256]{3,2,1,0:T(8,128)(2,1)} %collective-permute-done.2, s32[]{:T(128)S(6)} %select_n.109, bf16[8,2,2,256,256]{4,3,2,1,0:T(8,128)(2,1)} %bitcast.91, s32[]{:T(128)S(6)} %select_n.101, s32[]{:T(128)S(6)} %select_n.105), kind=kLoop, calls=%fused_computation.9 | loop fusion | flops 786432 | bytes 2097164 | tf_op jit(solution)/shard_map/add | solution.py:199
  23.4 0.1 add_convert_fusion.6
  23.6 0.1 collective-permute-start.3
  23.7 0.1 add_convert_fusion.5
  23.8 2.7 %collective-permute-start.6 = (bf16[2,256,256]{2,1,0:T(8,128)(2,1)S(1)}, bf16[2,256,256]{2,1,0:T(8,128)(2,1)S(1)}, u32[]{:S(2)}, u32[]{:S(2)}) collective-permute-start(bf16[2,256,256]{2,1,0:T(8,128)(2,1)S(1)} %add_convert_fusion.5), channel_id=1, source_target_pairs={{0,224},{32,0},{64,32},{96,64},{128,96},{160,128},{192,160},{224,1... | collective-permute-start | bytes 786440 | tf_op jit(solution)/shard_map/ppermute | solution.py:173
  26.5 1.3 %convert_add_fusion.3 = (f32[2,256,256]{2,1,0:T(8,128)S(1)}, f32[2,256,256]{2,1,0:T(8,128)S(1)}) fusion(bf16[8,2,256,256]{3,2,1,0:T(8,128)(2,1)} %collective-permute-done.2, s32[]{:T(128)S(6)} %select_n.113, bf16[8,2,2,256,256]{4,3,2,1,0:T(8,128)(2,1)} %bitcast.92, s32[]{:T(128)S(6)} %select_n.101, s32[]{:T(128)S(6)} %select_n.110), kind=kLoop, calls=%fused_computation.7 | loop fusion | flops 786432 | bytes 2097164 | tf_op jit(solution)/shard_map/add | solution.py:199
  27.8 3.8 %collective-permute-done.3 = bf16[2,256,256]{2,1,0:T(8,128)(2,1)S(1)} collective-permute-done((bf16[2,256,256]{2,1,0:T(8,128)(2,1)S(1)}, bf16[2,256,256]{2,1,0:T(8,128)(2,1)S(1)}, u32[]{:S(2)}, u32[]{:S(2)}) %collective-permute-start.3) | collective-permute-done | bytes 262176 | tf_op jit(solution)/shard_map/ppermute | solution.py:173
  31.6 0.1 add_convert_fusion.4
  31.7 0.1 collective-permute-start.5
  31.8 0.0 collective-permute-done.6
  31.8 0.1 add_convert_fusion.3
  31.9 2.7 %collective-permute-start.8 = (bf16[2,256,256]{2,1,0:T(8,128)(2,1)S(1)}, bf16[2,256,256]{2,1,0:T(8,128)(2,1)S(1)}, u32[]{:S(2)}, u32[]{:S(2)}) collective-permute-start(bf16[2,256,256]{2,1,0:T(8,128)(2,1)S(1)} %add_convert_fusion.3), channel_id=1, source_target_pairs={{0,224},{32,0},{64,32},{96,64},{128,96},{160,128},{192,160},{224,1... | collective-permute-start | bytes 786440 | tf_op jit(solution)/shard_map/ppermute | solution.py:173
  34.6 2.9 %all-to-all-done = bf16[16,4,2,16,256]{4,3,2,1,0:T(8,128)(2,1)S(1)} async-done(((bf16[16,4,2,16,256]{4,3,2,1,0:T(8,128)(2,1)}), bf16[16,4,2,16,256]{4,3,2,1,0:T(8,128)(2,1)S(1)}, u32[]{:S(2)}, u32[]{:S(2)}) %all-to-all-start) | async-done | bytes 1048608 | tf_op jit(solution)/shard_map/all_to_all | solution.py:218
  37.4 1.4 %pick.2 = bf16[32,2,16,256]{3,2,1,0:T(8,128)(2,1)} custom-call(s32[32]{0:T(128)S(1)} %get-tuple-element.62.source_ref, bf16[64,2,16,256]{3,2,1,0:T(8,128)(2,1)S(1)} %bitcast.84), custom_call_target="tpu_custom_call" | custom-call | tf_op jit(solution)/shard_map/pick/pallas_call | solution.py:37
  38.9 3.9 %all-to-all-start.1 = ((bf16[16,2,2,16,256]{4,3,2,1,0:T(8,128)(2,1)}), bf16[16,2,2,16,256]{4,3,2,1,0:T(8,128)(2,1)S(1)}, u32[]{:S(2)}, u32[]{:S(2)}) async-start(bf16[16,2,2,16,256]{4,3,2,1,0:T(8,128)(2,1)} %bitcast.25), calls=%async_computation.1 | async-start | bytes 1048576 | tf_op jit(solution)/shard_map/all_to_all | solution.py:231
  42.8 1.3 %convert_add_fusion.1 = (f32[2,256,256]{2,1,0:T(8,128)S(1)}, f32[2,256,256]{2,1,0:T(8,128)S(1)}) fusion(bf16[8,2,256,256]{3,2,1,0:T(8,128)(2,1)} %collective-permute-done.2, s32[]{:T(128)S(6)} %select_n.116, bf16[8,2,2,256,256]{4,3,2,1,0:T(8,128)(2,1)} %bitcast.93, s32[]{:T(128)S(6)} %select_n.101, s32[]{:T(128)S(6)} %select_n.114), kind=kLoop, calls=%fused_computation.5 | loop fusion | flops 786432 | bytes 2097164 | tf_op jit(solution)/shard_map/add | solution.py:199
  44.2 0.0 collective-permute-done.5
  44.2 0.1 add_convert_fusion.2
  44.2 0.1 collective-permute-start.7
  44.3 0.0 collective-permute-done.8
  44.3 0.1 add_convert_fusion.1
  44.4 2.7 %collective-permute-start.9 = (bf16[2,256,256]{2,1,0:T(8,128)(2,1)S(1)}, bf16[2,256,256]{2,1,0:T(8,128)(2,1)S(1)}, u32[]{:S(2)}, u32[]{:S(2)}) collective-permute-start(bf16[2,256,256]{2,1,0:T(8,128)(2,1)S(1)} %add_convert_fusion.1), channel_id=1, source_target_pairs={{0,224},{32,0},{64,32},{96,64},{128,96},{160,128},{192,160},{224,1... | collective-permute-start | bytes 786440 | tf_op jit(solution)/shard_map/ppermute | solution.py:173
  47.1 4.8 %all-to-all-done.1.root_ref = bf16[16,2,2,16,256]{4,3,2,1,0:T(8,128)(2,1)S(1)} async-done(((bf16[16,2,2,16,256]{4,3,2,1,0:T(8,128)(2,1)}), bf16[16,2,2,16,256]{4,3,2,1,0:T(8,128)(2,1)S(1)}, u32[]{:S(2)}, u32[]{:S(2)}) %all-to-all-start.1) | async-done | bytes 524320 | tf_op jit(solution)/shard_map/all_to_all | solution.py:231
  51.9 1.1 %convert_add_fusion = f32[2,256,256]{2,1,0:T(8,128)S(1)} fusion(bf16[8,2,256,256]{3,2,1,0:T(8,128)(2,1)} %collective-permute-done.2, s32[]{:T(128)S(6)} %select_n.118, bf16[8,2,2,256,256]{4,3,2,1,0:T(8,128)(2,1)} %bitcast.94, s32[]{:T(128)S(6)} %select_n.101), kind=kLoop, calls=%fused_computation.4 | loop fusion | flops 393216 | bytes 1048584 | tf_op jit(solution)/shard_map/add | solution.py:199
  53.0 0.0 collective-permute-done.9
  53.0 0.1 add_convert_fusion.grad_ref
  53.1 1.0 %precondition.1 = (bf16[2,256,256]{2,1,0:T(8,128)(2,1)S(1)}, bf16[16,2,16,256]{3,2,1,0:T(8,128)(2,1)}) custom-call(bf16[2,256,256]{2,1,0:T(8,128)(2,1)S(1)} %add_convert_fusion.grad_ref, bf16[16,2,2,16,256]{4,3,2,1,0:T(8,128)(2,1)S(1)} %all-to-all-done.1.root_ref), custom_call_target="tpu_custom_call" | custom-call | tf_op jit(solution)/shard_map/precondition/pallas_call | solution.py:60
  54.2 2.4 %collective-permute-start.11 = (bf16[2,256,256]{2,1,0:T(8,128)(2,1)S(1)}, bf16[2,256,256]{2,1,0:T(8,128)(2,1)S(1)}, u32[]{:S(2)}, u32[]{:S(2)}) collective-permute-start(bf16[2,256,256]{2,1,0:T(8,128)(2,1)S(1)} %get-tuple-element.39), channel_id=1, source_target_pairs={{0,224},{32,0},{64,32},{96,64},{128,96},{160,128},{192,160},{224,1... | collective-permute-start | bytes 786440 | tf_op jit(solution)/shard_map/ppermute | solution.py:173
  56.6 0.0 collective-permute-start.10
  56.6 4.9 %all-to-all-start.2 = ((bf16[16,2,16,256]{3,2,1,0:T(8,128)(2,1)}), bf16[16,2,16,256]{3,2,1,0:T(8,128)(2,1)S(1)}, u32[]{:S(2)}, u32[]{:S(2)}) async-start(bf16[16,2,16,256]{3,2,1,0:T(8,128)(2,1)} %get-tuple-element.38), calls=%async_computation.2 | async-start | bytes 524288 | tf_op jit(solution)/shard_map/all_to_all | solution.py:239
  61.5 0.1 select_reduce_fusion
  61.6 0.0 collective-permute-done.11
  61.6 2.9 %collective-permute-start.14 = (bf16[2,256,256]{2,1,0:T(8,128)(2,1)S(1)}, bf16[2,256,256]{2,1,0:T(8,128)(2,1)}, u32[]{:S(2)}, u32[]{:S(2)}) collective-permute-start(bf16[2,256,256]{2,1,0:T(8,128)(2,1)S(1)} %collective-permute-done.11), channel_id=1, source_target_pairs={{0,224},{32,0},{64,32},{96,64},{128,96},{160,128},{192,160},{224,1... | collective-permute-start | bytes 786440 | tf_op jit(solution)/shard_map/ppermute | solution.py:173
  64.5 4.3 %all-to-all-done.2 = bf16[16,2,16,256]{3,2,1,0:T(8,128)(2,1)S(1)} async-done(((bf16[16,2,16,256]{3,2,1,0:T(8,128)(2,1)}), bf16[16,2,16,256]{3,2,1,0:T(8,128)(2,1)S(1)}, u32[]{:S(2)}, u32[]{:S(2)}) %all-to-all-start.2) | async-done | bytes 262176 | tf_op jit(solution)/shard_map/all_to_all | solution.py:239
  68.8 1.5 %pick.3 = bf16[64,16,256]{2,1,0:T(8,128)(2,1)} custom-call(s32[64]{0:T(128)S(1)} %broadcast_add_fusion.source_ref, bf16[32,16,256]{2,1,0:T(8,128)(2,1)S(1)} %bitcast.85), custom_call_target="tpu_custom_call" | custom-call | tf_op jit(solution)/shard_map/pick/pallas_call | solution.py:37
  70.4 3.7 %all-to-all-start.3 = ((bf16[16,4,16,256]{3,2,1,0:T(8,128)(2,1)}), bf16[16,4,16,256]{3,2,1,0:T(8,128)(2,1)S(1)}, u32[]{:S(2)}, u32[]{:S(2)}) async-start(bf16[16,4,16,256]{3,2,1,0:T(8,128)(2,1)} %bitcast.29), calls=%async_computation.3 | async-start | bytes 1048576 | tf_op jit(solution)/shard_map/all_to_all | solution.py:253
  74.1 0.1 collective-permute-start.16
  74.2 2.7 %collective-permute-start.17 = (bf16[2,256,256]{2,1,0:T(8,128)(2,1)}, bf16[2,256,256]{2,1,0:T(8,128)(2,1)}, u32[]{:S(2)}, u32[]{:S(2)}) collective-permute-start(bf16[2,256,256]{2,1,0:T(8,128)(2,1)} %collective-permute-done.14), channel_id=1, source_target_pairs={{0,224},{32,0},{64,32},{96,64},{128,96},{160,128},{192,160},{224,1... | collective-permute-start | bytes 786440 | tf_op jit(solution)/shard_map/ppermute | solution.py:173
  76.8 0.1 pad_maximum_fusion.1.refs_0_
  76.9 6.8 %collective-permute-start.12 = (bf16[3,2,256,256]{3,2,1,0:T(8,128)(2,1)S(1)}, bf16[3,2,256,256]{3,2,1,0:T(8,128)(2,1)S(1)}, u32[]{:S(2)}, u32[]{:S(2)}) collective-permute-start(bf16[3,2,256,256]{3,2,1,0:T(8,128)(2,1)S(1)} %pad_maximum_fusion.1.refs_0_), channel_id=1, source_target_pairs={{0,16},{16,0},{1,17},{17,1},{2,18},{18,2},{3,19},{19,3},{4,20},{20... | collective-permute-start | bytes 2359304 | tf_op jit(solution)/shard_map/ppermute | solution.py:176
  83.7 1.1 %pad_maximum_fusion.2.refs_2_ = bf16[2,2,256,256]{3,2,1,0:T(8,128)(2,1)S(1)} fusion(bf16[1,2,256,256]{3,2,1,0:T(8,128)(2,1)} %bitcast.36, bf16[1,2,256,256]{3,2,1,0:T(8,128)(2,1)} %bitcast.35), kind=kLoop, calls=%fused_computation.3 | loop fusion | flops 262144 | bytes 1048576 | tf_op jit(solution)/shard_map/stack | solution.py:263
  84.8 0.1 collective-permute-start.15
  84.9 1.0 part.1
  85.9 5.4 %collective-permute-start.18 = (bf16[2,2,256,256]{3,2,1,0:T(8,128)(2,1)S(1)}, bf16[2,2,256,256]{3,2,1,0:T(8,128)(2,1)S(1)}, u32[]{:S(2)}, u32[]{:S(2)}) collective-permute-start(bf16[2,2,256,256]{3,2,1,0:T(8,128)(2,1)S(1)} %get-tuple-element.47.refs_4_), channel_id=1, source_target_pairs={{0,16},{16,0},{1,17},{17,1},{2,18},{18,2},{3,19},{19,3},{4,20},{20... | collective-permute-start | bytes 1572872 | tf_op jit(solution)/shard_map/ppermute | solution.py:176
  91.3 3.0 %collective-permute-start.20 = (bf16[1,256,256]{2,1,0:T(8,128)(2,1)S(1)}, bf16[1,256,256]{2,1,0:T(8,128)(2,1)S(1)}, u32[]{:S(2)}, u32[]{:S(2)}) collective-permute-start(bf16[1,256,256]{2,1,0:T(8,128)(2,1)S(1)} %get-tuple-element.49), channel_id=1, source_target_pairs={{0,224},{32,0},{64,32},{96,64},{128,96},{160,128},{192,160},{224,1... | collective-permute-start | bytes 393224 | tf_op jit(solution)/shard_map/ppermute | solution.py:173
  94.2 0.1 pad_add_fusion.where_ref
  94.3 4.2 %statistics.1 = (f32[4,256,256]{2,1,0:T(8,128)}, f32[4,256,256]{2,1,0:T(8,128)}) custom-call(bf16[16,4,16,256]{3,2,1,0:T(8,128)(2,1)S(1)} %all-to-all-done.3.own_ref, f32[4,256,256]{2,1,0:T(8,128)} %bitcast.95, f32[4,256,256]{2,1,0:T(8,128)} %bitcast.96), custom_call_target="tpu_custom_call" | custom-call | tf_op jit(solution)/shard_map/statistics/pallas_call | solution.py:106
  98.5 2.5 %place.2.refs_0_ = bf16[8,2,2,256,256]{4,3,2,1,0:T(8,128)(2,1)} custom-call(s32[2]{0:T(128)S(1)} %pad_add_fusion.where_ref, bf16[3,2,256,256]{3,2,1,0:T(8,128)(2,1)S(1)} %pad_maximum_fusion.1.refs_0_, bf16[3,2,256,256]{3,2,1,0:T(8,128)(2,1)S(1)} %collective-permute-done.12.refs_1_, bf16[2,2,256,256]{3,2,1,0:T(8,128)(2,1)S(1)} %pad_maximum_fusion.2.refs_2_, ...), custom_call_target="tpu_custom_call" | custom-call | tf_op jit(solution)/shard_map/place/pallas_call | solution.py:146
  101.1 0.5 collective-permute-start.21
  101.6 1.2 %collective-permute-done.21.refs_2_ = bf16[2,1,256,256]{3,2,1,0:T(8,128)(2,1)S(1)} collective-permute-done((bf16[2,1,256,256]{3,2,1,0:T(8,128)(2,1)S(1)}, bf16[2,1,256,256]{3,2,1,0:T(8,128)(2,1)S(1)}, u32[]{:S(2)}, u32[]{:S(2)}) %collective-permute-start.21) | collective-permute-done | bytes 262176 | tf_op jit(solution)/shard_map/ppermute | solution.py:176
  102.8 1.4 %place.3 = bf16[8,2,2,256,256]{4,3,2,1,0:T(8,128)(2,1)} custom-call(s32[2]{0:T(128)S(1)} %pad_add_fusion.where_ref, bf16[8,2,2,256,256]{4,3,2,1,0:T(8,128)(2,1)} %place.2.refs_0_, bf16[2,1,256,256]{3,2,1,0:T(8,128)(2,1)S(1)} %pad_maximum_fusion.3.refs_1_, bf16[2,1,256,256]{3,2,1,0:T(8,128)(2,1)S(1)} %collective-permute-done.21.refs_2_), custom_call_target="tpu_custom_call", output_to_operand_aliasing={{}: (1, {})} | custom-call | tf_op jit(solution)/shard_map/place/pallas_call | solution.py:146
  (28 shorter events, 0.2 us)
Async XLA Ops:
  0.6 7.8 %copy-start = (s32[512]{0:T(512)S(1)}, s32[512]{0:T(512)}, u32[]{:S(2)}) copy-start(s32[512]{0:T(512)} %param.11) | copy-start | bytes 6148
  1.6 5.1 %collective-permute-start = (bf16[2,256,256]{2,1,0:T(8,128)(2,1)S(1)}, bf16[2,256,256]{2,1,0:T(8,128)(2,1)S(1)}, u32[]{:S(2)}, u32[]{:S(2)}) collective-permute-start(bf16[2,256,256]{2,1,0:T(8,128)(2,1)S(1)} %dynamic-slice_bitcast_fusion.1), channel_id=1, source_target_pairs={{0,16},{16,0},{1,17},{17,1},{2,18},{18,2},{3,19},{19,3},{4,20},{20... | collective-permute-start | bytes 786440 | tf_op jit(solution)/shard_map/ppermute | solution.py:176
  8.4 13.7 %collective-permute-start.2 = (bf16[8,2,256,256]{3,2,1,0:T(8,128)(2,1)S(1)}, bf16[8,2,256,256]{3,2,1,0:T(8,128)(2,1)}, u32[]{:S(2)}, u32[]{:S(2)}) collective-permute-start(bf16[8,2,256,256]{3,2,1,0:T(8,128)(2,1)S(1)} %dynamic-slice_bitcast_fusion), channel_id=1, source_target_pairs={{0,16},{16,0},{1,17},{17,1},{2,18},{18,2},{3,19},{19,3},{4,20},{20... | collective-permute-start | bytes 6291464 | tf_op jit(solution)/shard_map/ppermute | solution.py:176
  10.2 11.8 %collective-permute-start.4 = (bf16[1,256,256]{2,1,0:T(8,128)(2,1)}, bf16[1,256,256]{2,1,0:T(8,128)(2,1)S(1)}, u32[]{:S(2)}, u32[]{:S(2)}) collective-permute-start(bf16[1,256,256]{2,1,0:T(8,128)(2,1)} %get-tuple-element.59), channel_id=1, source_target_pairs={{0,224},{32,0},{64,32},{96,64},{128,96},{160,128},{192,160},{224,1... | collective-permute-start | bytes 393224 | tf_op jit(solution)/shard_map/ppermute | solution.py:173
  15.3 6.8 %collective-permute-start.1 = (bf16[1,256,256]{2,1,0:T(8,128)(2,1)S(1)}, bf16[1,256,256]{2,1,0:T(8,128)(2,1)S(1)}, u32[]{:S(2)}, u32[]{:S(2)}) collective-permute-start(bf16[1,256,256]{2,1,0:T(8,128)(2,1)S(1)} %get-tuple-element.60), channel_id=1, source_target_pairs={{0,32},{32,64},{64,96},{96,128},{128,160},{160,192},{192,224},{224... | collective-permute-start | bytes 393224 | tf_op jit(solution)/shard_map/ppermute | solution.py:173
  15.3 22.2 %all-to-all-start = ((bf16[16,4,2,16,256]{4,3,2,1,0:T(8,128)(2,1)}), bf16[16,4,2,16,256]{4,3,2,1,0:T(8,128)(2,1)S(1)}, u32[]{:S(2)}, u32[]{:S(2)}) async-start(bf16[16,4,2,16,256]{4,3,2,1,0:T(8,128)(2,1)} %bitcast.23), calls=%async_computation | async-start | bytes 2097152 | tf_op jit(solution)/shard_map/all_to_all | solution.py:218
  23.6 8.0 %collective-permute-start.3 = (bf16[2,256,256]{2,1,0:T(8,128)(2,1)S(1)}, bf16[2,256,256]{2,1,0:T(8,128)(2,1)S(1)}, u32[]{:S(2)}, u32[]{:S(2)}) collective-permute-start(bf16[2,256,256]{2,1,0:T(8,128)(2,1)S(1)} %add_convert_fusion.6), channel_id=1, source_target_pairs={{0,32},{32,64},{64,96},{96,128},{128,160},{160,192},{192,224},{224... | collective-permute-start | bytes 786440 | tf_op jit(solution)/shard_map/ppermute | solution.py:173
  23.8 8.0 %collective-permute-start.6 = (bf16[2,256,256]{2,1,0:T(8,128)(2,1)S(1)}, bf16[2,256,256]{2,1,0:T(8,128)(2,1)S(1)}, u32[]{:S(2)}, u32[]{:S(2)}) collective-permute-start(bf16[2,256,256]{2,1,0:T(8,128)(2,1)S(1)} %add_convert_fusion.5), channel_id=1, source_target_pairs={{0,224},{32,0},{64,32},{96,64},{128,96},{160,128},{192,160},{224,1... | collective-permute-start | bytes 786440 | tf_op jit(solution)/shard_map/ppermute | solution.py:173
  31.7 12.5 %collective-permute-start.5 = (bf16[2,256,256]{2,1,0:T(8,128)(2,1)S(1)}, bf16[2,256,256]{2,1,0:T(8,128)(2,1)S(1)}, u32[]{:S(2)}, u32[]{:S(2)}) collective-permute-start(bf16[2,256,256]{2,1,0:T(8,128)(2,1)S(1)} %add_convert_fusion.4), channel_id=1, source_target_pairs={{0,32},{32,64},{64,96},{96,128},{128,160},{160,192},{192,224},{224... | collective-permute-start | bytes 786440 | tf_op jit(solution)/shard_map/ppermute | solution.py:173
  31.9 12.5 %collective-permute-start.8 = (bf16[2,256,256]{2,1,0:T(8,128)(2,1)S(1)}, bf16[2,256,256]{2,1,0:T(8,128)(2,1)S(1)}, u32[]{:S(2)}, u32[]{:S(2)}) collective-permute-start(bf16[2,256,256]{2,1,0:T(8,128)(2,1)S(1)} %add_convert_fusion.3), channel_id=1, source_target_pairs={{0,224},{32,0},{64,32},{96,64},{128,96},{160,128},{192,160},{224,1... | collective-permute-start | bytes 786440 | tf_op jit(solution)/shard_map/ppermute | solution.py:173
  38.9 13.0 %all-to-all-start.1 = ((bf16[16,2,2,16,256]{4,3,2,1,0:T(8,128)(2,1)}), bf16[16,2,2,16,256]{4,3,2,1,0:T(8,128)(2,1)S(1)}, u32[]{:S(2)}, u32[]{:S(2)}) async-start(bf16[16,2,2,16,256]{4,3,2,1,0:T(8,128)(2,1)} %bitcast.25), calls=%async_computation.1 | async-start | bytes 1048576 | tf_op jit(solution)/shard_map/all_to_all | solution.py:231
  44.2 8.8 %collective-permute-start.7 = (bf16[2,256,256]{2,1,0:T(8,128)(2,1)S(1)}, bf16[2,256,256]{2,1,0:T(8,128)(2,1)S(1)}, u32[]{:S(2)}, u32[]{:S(2)}) collective-permute-start(bf16[2,256,256]{2,1,0:T(8,128)(2,1)S(1)} %add_convert_fusion.2), channel_id=1, source_target_pairs={{0,32},{32,64},{64,96},{96,128},{128,160},{160,192},{192,224},{224... | collective-permute-start | bytes 786440 | tf_op jit(solution)/shard_map/ppermute | solution.py:173
  44.4 8.6 %collective-permute-start.9 = (bf16[2,256,256]{2,1,0:T(8,128)(2,1)S(1)}, bf16[2,256,256]{2,1,0:T(8,128)(2,1)S(1)}, u32[]{:S(2)}, u32[]{:S(2)}) collective-permute-start(bf16[2,256,256]{2,1,0:T(8,128)(2,1)S(1)} %add_convert_fusion.1), channel_id=1, source_target_pairs={{0,224},{32,0},{64,32},{96,64},{128,96},{160,128},{192,160},{224,1... | collective-permute-start | bytes 786440 | tf_op jit(solution)/shard_map/ppermute | solution.py:173
  54.2 7.4 %collective-permute-start.11 = (bf16[2,256,256]{2,1,0:T(8,128)(2,1)S(1)}, bf16[2,256,256]{2,1,0:T(8,128)(2,1)S(1)}, u32[]{:S(2)}, u32[]{:S(2)}) collective-permute-start(bf16[2,256,256]{2,1,0:T(8,128)(2,1)S(1)} %get-tuple-element.39), channel_id=1, source_target_pairs={{0,224},{32,0},{64,32},{96,64},{128,96},{160,128},{192,160},{224,1... | collective-permute-start | bytes 786440 | tf_op jit(solution)/shard_map/ppermute | solution.py:173
  56.6 8.0 %collective-permute-start.10 = (bf16[2,256,256]{2,1,0:T(8,128)(2,1)S(1)}, bf16[2,256,256]{2,1,0:T(8,128)(2,1)S(1)}, u32[]{:S(2)}, u32[]{:S(2)}) collective-permute-start(bf16[2,256,256]{2,1,0:T(8,128)(2,1)S(1)} %get-tuple-element.39), channel_id=1, source_target_pairs={{0,32},{32,64},{64,96},{96,128},{128,160},{160,192},{192,224},{224... | collective-permute-start | bytes 786440 | tf_op jit(solution)/shard_map/ppermute | solution.py:173
  56.6 12.3 %all-to-all-start.2 = ((bf16[16,2,16,256]{3,2,1,0:T(8,128)(2,1)}), bf16[16,2,16,256]{3,2,1,0:T(8,128)(2,1)S(1)}, u32[]{:S(2)}, u32[]{:S(2)}) async-start(bf16[16,2,16,256]{3,2,1,0:T(8,128)(2,1)} %get-tuple-element.38), calls=%async_computation.2 | async-start | bytes 524288 | tf_op jit(solution)/shard_map/all_to_all | solution.py:239
  61.6 12.5 %collective-permute-start.14 = (bf16[2,256,256]{2,1,0:T(8,128)(2,1)S(1)}, bf16[2,256,256]{2,1,0:T(8,128)(2,1)}, u32[]{:S(2)}, u32[]{:S(2)}) collective-permute-start(bf16[2,256,256]{2,1,0:T(8,128)(2,1)S(1)} %collective-permute-done.11), channel_id=1, source_target_pairs={{0,224},{32,0},{64,32},{96,64},{128,96},{160,128},{192,160},{224,1... | collective-permute-start | bytes 786440 | tf_op jit(solution)/shard_map/ppermute | solution.py:173
  64.5 9.5 %collective-permute-start.13 = (bf16[2,256,256]{2,1,0:T(8,128)(2,1)S(1)}, bf16[2,256,256]{2,1,0:T(8,128)(2,1)}, u32[]{:S(2)}, u32[]{:S(2)}) collective-permute-start(bf16[2,256,256]{2,1,0:T(8,128)(2,1)S(1)} %collective-permute-done.10), channel_id=1, source_target_pairs={{0,32},{32,64},{64,96},{96,128},{128,160},{160,192},{192,224},{224... | collective-permute-start | bytes 786440 | tf_op jit(solution)/shard_map/ppermute | solution.py:173
  70.4 14.5 %all-to-all-start.3 = ((bf16[16,4,16,256]{3,2,1,0:T(8,128)(2,1)}), bf16[16,4,16,256]{3,2,1,0:T(8,128)(2,1)S(1)}, u32[]{:S(2)}, u32[]{:S(2)}) async-start(bf16[16,4,16,256]{3,2,1,0:T(8,128)(2,1)} %bitcast.29), calls=%async_computation.3 | async-start | bytes 1048576 | tf_op jit(solution)/shard_map/all_to_all | solution.py:253
  74.1 10.8 %collective-permute-start.16 = (bf16[2,256,256]{2,1,0:T(8,128)(2,1)}, bf16[2,256,256]{2,1,0:T(8,128)(2,1)S(1)}, u32[]{:S(2)}, u32[]{:S(2)}) collective-permute-start(bf16[2,256,256]{2,1,0:T(8,128)(2,1)} %collective-permute-done.13), channel_id=1, source_target_pairs={{0,32},{32,64},{64,96},{96,128},{128,160},{160,192},{192,224},{224... | collective-permute-start | bytes 786440 | tf_op jit(solution)/shard_map/ppermute | solution.py:173
  74.2 10.7 %collective-permute-start.17 = (bf16[2,256,256]{2,1,0:T(8,128)(2,1)}, bf16[2,256,256]{2,1,0:T(8,128)(2,1)}, u32[]{:S(2)}, u32[]{:S(2)}) collective-permute-start(bf16[2,256,256]{2,1,0:T(8,128)(2,1)} %collective-permute-done.14), channel_id=1, source_target_pairs={{0,224},{32,0},{64,32},{96,64},{128,96},{160,128},{192,160},{224,1... | collective-permute-start | bytes 786440 | tf_op jit(solution)/shard_map/ppermute | solution.py:173
  76.9 21.6 %collective-permute-start.12 = (bf16[3,2,256,256]{3,2,1,0:T(8,128)(2,1)S(1)}, bf16[3,2,256,256]{3,2,1,0:T(8,128)(2,1)S(1)}, u32[]{:S(2)}, u32[]{:S(2)}) collective-permute-start(bf16[3,2,256,256]{3,2,1,0:T(8,128)(2,1)S(1)} %pad_maximum_fusion.1.refs_0_), channel_id=1, source_target_pairs={{0,16},{16,0},{1,17},{17,1},{2,18},{18,2},{3,19},{19,3},{4,20},{20... | collective-permute-start | bytes 2359304 | tf_op jit(solution)/shard_map/ppermute | solution.py:176
  84.8 13.7 %collective-permute-start.15 = (bf16[2,2,256,256]{3,2,1,0:T(8,128)(2,1)S(1)}, bf16[2,2,256,256]{3,2,1,0:T(8,128)(2,1)S(1)}, u32[]{:S(2)}, u32[]{:S(2)}) collective-permute-start(bf16[2,2,256,256]{3,2,1,0:T(8,128)(2,1)S(1)} %pad_maximum_fusion.2.refs_2_), channel_id=1, source_target_pairs={{0,16},{16,0},{1,17},{17,1},{2,18},{18,2},{3,19},{19,3},{4,20},{20... | collective-permute-start | bytes 1572872 | tf_op jit(solution)/shard_map/ppermute | solution.py:176
  85.9 12.6 %collective-permute-start.18 = (bf16[2,2,256,256]{3,2,1,0:T(8,128)(2,1)S(1)}, bf16[2,2,256,256]{3,2,1,0:T(8,128)(2,1)S(1)}, u32[]{:S(2)}, u32[]{:S(2)}) collective-permute-start(bf16[2,2,256,256]{3,2,1,0:T(8,128)(2,1)S(1)} %get-tuple-element.47.refs_4_), channel_id=1, source_target_pairs={{0,16},{16,0},{1,17},{17,1},{2,18},{18,2},{3,19},{19,3},{4,20},{20... | collective-permute-start | bytes 1572872 | tf_op jit(solution)/shard_map/ppermute | solution.py:176
  91.3 9.7 %collective-permute-start.19 = (bf16[1,256,256]{2,1,0:T(8,128)(2,1)S(1)}, bf16[1,256,256]{2,1,0:T(8,128)(2,1)S(1)}, u32[]{:S(2)}, u32[]{:S(2)}) collective-permute-start(bf16[1,256,256]{2,1,0:T(8,128)(2,1)S(1)} %get-tuple-element.48), channel_id=1, source_target_pairs={{0,32},{32,64},{64,96},{96,128},{128,160},{160,192},{192,224},{224... | collective-permute-start | bytes 393224 | tf_op jit(solution)/shard_map/ppermute | solution.py:173
  91.3 9.7 %collective-permute-start.20 = (bf16[1,256,256]{2,1,0:T(8,128)(2,1)S(1)}, bf16[1,256,256]{2,1,0:T(8,128)(2,1)S(1)}, u32[]{:S(2)}, u32[]{:S(2)}) collective-permute-start(bf16[1,256,256]{2,1,0:T(8,128)(2,1)S(1)} %get-tuple-element.49), channel_id=1, source_target_pairs={{0,224},{32,0},{64,32},{96,64},{128,96},{160,128},{192,160},{224,1... | collective-permute-start | bytes 393224 | tf_op jit(solution)/shard_map/ppermute | solution.py:173
  101.1 1.7 %collective-permute-start.21 = (bf16[2,1,256,256]{3,2,1,0:T(8,128)(2,1)S(1)}, bf16[2,1,256,256]{3,2,1,0:T(8,128)(2,1)S(1)}, u32[]{:S(2)}, u32[]{:S(2)}) collective-permute-start(bf16[2,1,256,256]{3,2,1,0:T(8,128)(2,1)S(1)} %pad_maximum_fusion.3.refs_1_), channel_id=1, source_target_pairs={{0,16},{16,0},{1,17},{17,1},{2,18},{18,2},{3,19},{19,3},{4,20},{20... | collective-permute-start | bytes 786440 | tf_op jit(solution)/shard_map/ppermute | solution.py:176

commit v6 on v5

--- a/solution.py
+++ b/solution.py
@@ -203,7 +203,7 @@
     theirs = lax.dynamic_slice(
         grads, (0, 1 - core, 0, 0, 0), (zs, 1, held, rows, cols)
     ).reshape(zs, held, rows, cols)
-    moving = rows_of(far, core)
+    moving = lax.optimization_barrier(rows_of(far, core))
     moving = [
         (moving[way : way + 1].astype(F32) + farthest[way : way + 1].astype(F32)).astype(BF16)
         for way in range(2)

time: 105 us -> 104 us (level)
  no operation moved by 1% of the time
where the time goes in v6:
time: 104 us; the launch traced here: 103 us
  starting transfers between devices  58.8 us (57%)
  waiting for transfers between devices  16.9 us (16%)
  Pallas kernels  13.1 us (13%)
  other arithmetic  9.22 us (9%)
  local copies, waits for them, and re-layouts  4.18 us (4%)
  between operations  1.22 us (1%)
    ppermute x16, starting transfers between devices, hop(): return lax.ppermute(value, 'z', ways[way])  23.4 us
    ppermute x6, starting transfers between devices, swap(): return lax.ppermute(value, 'core', [(0, 1), (1, 0)])  16.1 us
    all_to_all x1, starting transfers between devices, per_device(): spread = lax.all_to_all(spread, 'mp', 0, 0, tiled=True)  6.76 us
    add x4, other arithmetic, base(): value = mine.reshape(held, rows, cols).astype(F32) + given.astype(F32)  4.99 us
    all_to_all x1, starting transfers between devices, per_device(): arrived = lax.all_to_all(sliced, 'mp', 0, 0, tiled=True)  4.93 us
    all_to_all x1, waiting for transfers between devices, per_device(): roots = lax.all_to_all(wanted, 'mp', 0, 0, tiled=True)  4.79 us
    all_to_all x1, waiting for transfers between devices, per_device(): arrived = lax.all_to_all(sliced, 'mp', 0, 0, tiled=True)  4.28 us
    pallas_call x1, Pallas kernels, statistics(): pl.pallas_call(statistics_kernel, grid=(slots,), out_shape=(jax.ShapeDtyp...  4.19 us
  transfers between devices with their start and end apart: 26, of which 5 were waited for; matrix products, arithmetic and copies ran while one was open for 11% of the time, Pallas kernels for 10%

profile of v6, /device:TPU:1, one launch (start us, length us, event | category | flops | bytes accessed | tf_op | source)
XLA Modules:
  0.0 103.4 jit_solution(2489613027288562491)
XLA Ops:
  0.7 1.1 %dynamic-slice_bitcast_fusion.2 = (bf16[2,256,256]{2,1,0:T(8,128)(2,1)S(1)}, bf16[2,256,256]{2,1,0:T(8,128)(2,1)S(1)}) fusion(bf16[8,2,2,256,256]{4,3,2,1,0:T(8,128)(2,1)} %bitcast.80, s32[]{:T(128)S(6)} %select_n.100, s32[]{:T(128)S(6)} %select_n.101, s32[]{:T(128)S(6)} %select_n.102), kind=kLoop, calls=%fused_computation.22 | loop fusion | bytes 1048588 | tf_op jit(solution)/shard_map/reshape | solution.py:192
  1.7 3.3 %collective-permute-start = (bf16[2,256,256]{2,1,0:T(8,128)(2,1)S(1)}, bf16[2,256,256]{2,1,0:T(8,128)(2,1)S(1)}, u32[]{:S(2)}, u32[]{:S(2)}) collective-permute-start(bf16[2,256,256]{2,1,0:T(8,128)(2,1)S(1)} %get-tuple-element.60), channel_id=1, source_target_pairs={{0,16},{16,0},{1,17},{17,1},{2,18},{18,2},{3,19},{19,3},{4,20},{20... | collective-permute-start | bytes 786440 | tf_op jit(solution)/shard_map/ppermute | solution.py:176
  5.1 1.7 %dynamic-slice_bitcast_fusion = bf16[8,2,256,256]{3,2,1,0:T(8,128)(2,1)S(1)} fusion(bf16[8,2,2,256,256]{4,3,2,1,0:T(8,128)(2,1)} %bitcast.81, s32[]{:T(128)S(6)} %select_n.102), kind=kLoop, calls=%fused_computation | loop fusion | bytes 4194308 | tf_op jit(solution)/shard_map/reshape | solution.py:205
  6.8 0.0 collective-permute-done
  6.8 0.7 add_convert_fusion.7
  7.5 0.0 collective-permute-start.2
  7.6 0.1 reshape.108
  7.7 0.1 reshape.109
  7.8 0.2 convert_reduce_fusion
  8.0 1.3 %pad_maximum_fusion = bf16[4,2,16,16,256]{4,3,2,0,1:T(8,128)(2,1)S(1)} fusion(bf16[4,1,16,16,256]{4,3,2,0,1:T(8,128)(2,1)} %bitcast.88, bf16[4,1,16,16,256]{4,3,2,0,1:T(8,128)(2,1)} %bitcast.89), kind=kLoop, calls=%fused_computation.1 | loop fusion | flops 524288 | bytes 2097152 | tf_op jit(solution)/shard_map/stack | solution.py:214
  9.3 3.9 %collective-permute-start.4 = (bf16[1,256,256]{2,1,0:T(8,128)(2,1)}, bf16[1,256,256]{2,1,0:T(8,128)(2,1)S(1)}, u32[]{:S(2)}, u32[]{:S(2)}) collective-permute-start(bf16[1,256,256]{2,1,0:T(8,128)(2,1)} %get-tuple-element.61), channel_id=1, source_target_pairs={{0,224},{32,0},{64,32},{96,64},{128,96},{160,128},{192,160},{224,1... | collective-permute-start | bytes 393224 | tf_op jit(solution)/shard_map/ppermute | solution.py:173
  13.3 1.1 %copy.16 = bf16[4,2,16,16,256]{4,3,1,0,2:T(8,128)(2,1)} copy(bf16[4,2,16,16,256]{4,3,2,0,1:T(8,128)(2,1)S(1)} %pad_maximum_fusion) | data formatting | bytes 2097152 | tf_op jit(solution)/shard_map/stack | solution.py:214
  14.4 6.8 %all-to-all-start = ((bf16[16,4,2,16,256]{4,3,2,1,0:T(8,128)(2,1)}), bf16[16,4,2,16,256]{4,3,2,1,0:T(8,128)(2,1)S(1)}, u32[]{:S(2)}, u32[]{:S(2)}) async-start(bf16[16,4,2,16,256]{4,3,2,1,0:T(8,128)(2,1)} %bitcast.22), calls=%async_computation | async-start | bytes 2097152 | tf_op jit(solution)/shard_map/all_to_all | solution.py:218
  21.2 0.0 collective-permute-done.4
  21.2 0.0 collective-permute-done.1
  21.2 0.0 collective-permute-done.2
  21.2 1.3 %convert_add_fusion.5 = (f32[2,256,256]{2,1,0:T(8,128)S(1)}, f32[2,256,256]{2,1,0:T(8,128)S(1)}) fusion(bf16[8,2,256,256]{3,2,1,0:T(8,128)(2,1)} %collective-permute-done.2, s32[]{:T(128)S(6)} %select_n.109, bf16[8,2,2,256,256]{4,3,2,1,0:T(8,128)(2,1)} %bitcast.82, s32[]{:T(128)S(6)} %select_n.101, s32[]{:T(128)S(6)} %select_n.105), kind=kLoop, calls=%fused_computation.9 | loop fusion | flops 786432 | bytes 2097164 | tf_op jit(solution)/shard_map/add | solution.py:199
  22.6 0.1 add_convert_fusion.6
  22.7 0.1 collective-permute-start.3
  22.8 0.1 add_convert_fusion.5
  22.9 2.7 %collective-permute-start.6 = (bf16[2,256,256]{2,1,0:T(8,128)(2,1)S(1)}, bf16[2,256,256]{2,1,0:T(8,128)(2,1)S(1)}, u32[]{:S(2)}, u32[]{:S(2)}) collective-permute-start(bf16[2,256,256]{2,1,0:T(8,128)(2,1)S(1)} %add_convert_fusion.5), channel_id=1, source_target_pairs={{0,224},{32,0},{64,32},{96,64},{128,96},{160,128},{192,160},{224,1... | collective-permute-start | bytes 786440 | tf_op jit(solution)/shard_map/ppermute | solution.py:173
  25.7 1.3 %convert_add_fusion.3 = (f32[2,256,256]{2,1,0:T(8,128)S(1)}, f32[2,256,256]{2,1,0:T(8,128)S(1)}) fusion(bf16[8,2,256,256]{3,2,1,0:T(8,128)(2,1)} %collective-permute-done.2, s32[]{:T(128)S(6)} %select_n.113, bf16[8,2,2,256,256]{4,3,2,1,0:T(8,128)(2,1)} %bitcast.83, s32[]{:T(128)S(6)} %select_n.101, s32[]{:T(128)S(6)} %select_n.110), kind=kLoop, calls=%fused_computation.7 | loop fusion | flops 786432 | bytes 2097164 | tf_op jit(solution)/shard_map/add | solution.py:199
  27.0 3.8 %collective-permute-done.3 = bf16[2,256,256]{2,1,0:T(8,128)(2,1)S(1)} collective-permute-done((bf16[2,256,256]{2,1,0:T(8,128)(2,1)S(1)}, bf16[2,256,256]{2,1,0:T(8,128)(2,1)S(1)}, u32[]{:S(2)}, u32[]{:S(2)}) %collective-permute-start.3) | collective-permute-done | bytes 262176 | tf_op jit(solution)/shard_map/ppermute | solution.py:173
  30.7 0.1 add_convert_fusion.4
  30.8 0.1 collective-permute-start.5
  30.9 0.1 add_convert_fusion.3
  31.0 2.7 %collective-permute-start.8 = (bf16[2,256,256]{2,1,0:T(8,128)(2,1)S(1)}, bf16[2,256,256]{2,1,0:T(8,128)(2,1)S(1)}, u32[]{:S(2)}, u32[]{:S(2)}) collective-permute-start(bf16[2,256,256]{2,1,0:T(8,128)(2,1)S(1)} %add_convert_fusion.3), channel_id=1, source_target_pairs={{0,224},{32,0},{64,32},{96,64},{128,96},{160,128},{192,160},{224,1... | collective-permute-start | bytes 786440 | tf_op jit(solution)/shard_map/ppermute | solution.py:173
  33.7 2.9 %all-to-all-done = bf16[16,4,2,16,256]{4,3,2,1,0:T(8,128)(2,1)S(1)} async-done(((bf16[16,4,2,16,256]{4,3,2,1,0:T(8,128)(2,1)}), bf16[16,4,2,16,256]{4,3,2,1,0:T(8,128)(2,1)S(1)}, u32[]{:S(2)}, u32[]{:S(2)}) %all-to-all-start) | async-done | bytes 1048608 | tf_op jit(solution)/shard_map/all_to_all | solution.py:218
  36.6 1.4 %pick.2 = bf16[32,2,16,256]{3,2,1,0:T(8,128)(2,1)} custom-call(s32[32]{0:T(128)S(1)} %get-tuple-element.64.source_ref, bf16[64,2,16,256]{3,2,1,0:T(8,128)(2,1)S(1)} %bitcast.76), custom_call_target="tpu_custom_call" | custom-call | tf_op jit(solution)/shard_map/pick/pallas_call | solution.py:37
  38.0 3.9 %all-to-all-start.1 = ((bf16[16,2,2,16,256]{4,3,2,1,0:T(8,128)(2,1)}), bf16[16,2,2,16,256]{4,3,2,1,0:T(8,128)(2,1)S(1)}, u32[]{:S(2)}, u32[]{:S(2)}) async-start(bf16[16,2,2,16,256]{4,3,2,1,0:T(8,128)(2,1)} %bitcast.24), calls=%async_computation.1 | async-start | bytes 1048576 | tf_op jit(solution)/shard_map/all_to_all | solution.py:231
  42.0 1.3 %convert_add_fusion.1 = (f32[2,256,256]{2,1,0:T(8,128)S(1)}, f32[2,256,256]{2,1,0:T(8,128)S(1)}) fusion(bf16[8,2,256,256]{3,2,1,0:T(8,128)(2,1)} %collective-permute-done.2, s32[]{:T(128)S(6)} %select_n.116, bf16[8,2,2,256,256]{4,3,2,1,0:T(8,128)(2,1)} %bitcast.84, s32[]{:T(128)S(6)} %select_n.101, s32[]{:T(128)S(6)} %select_n.114), kind=kLoop, calls=%fused_computation.5 | loop fusion | flops 786432 | bytes 2097164 | tf_op jit(solution)/shard_map/add | solution.py:199
  43.3 0.0 collective-permute-done.5
  43.3 0.1 add_convert_fusion.2
  43.4 0.1 collective-permute-start.7
  43.5 0.1 add_convert_fusion.1
  43.5 2.7 %collective-permute-start.9 = (bf16[2,256,256]{2,1,0:T(8,128)(2,1)S(1)}, bf16[2,256,256]{2,1,0:T(8,128)(2,1)S(1)}, u32[]{:S(2)}, u32[]{:S(2)}) collective-permute-start(bf16[2,256,256]{2,1,0:T(8,128)(2,1)S(1)} %add_convert_fusion.1), channel_id=1, source_target_pairs={{0,224},{32,0},{64,32},{96,64},{128,96},{160,128},{192,160},{224,1... | collective-permute-start | bytes 786440 | tf_op jit(solution)/shard_map/ppermute | solution.py:173
  46.3 4.8 %all-to-all-done.1.root_ref = bf16[16,2,2,16,256]{4,3,2,1,0:T(8,128)(2,1)S(1)} async-done(((bf16[16,2,2,16,256]{4,3,2,1,0:T(8,128)(2,1)}), bf16[16,2,2,16,256]{4,3,2,1,0:T(8,128)(2,1)S(1)}, u32[]{:S(2)}, u32[]{:S(2)}) %all-to-all-start.1) | async-done | bytes 524320 | tf_op jit(solution)/shard_map/all_to_all | solution.py:231
  51.1 1.1 %convert_add_fusion = f32[2,256,256]{2,1,0:T(8,128)S(1)} fusion(bf16[8,2,256,256]{3,2,1,0:T(8,128)(2,1)} %collective-permute-done.2, s32[]{:T(128)S(6)} %select_n.118, bf16[8,2,2,256,256]{4,3,2,1,0:T(8,128)(2,1)} %bitcast.85, s32[]{:T(128)S(6)} %select_n.101), kind=kLoop, calls=%fused_computation.4 | loop fusion | flops 393216 | bytes 1048584 | tf_op jit(solution)/shard_map/add | solution.py:199
  52.1 0.0 collective-permute-done.7
  52.2 0.1 add_convert_fusion.grad_ref
  52.3 1.0 %precondition.1 = (bf16[2,256,256]{2,1,0:T(8,128)(2,1)S(1)}, bf16[16,2,16,256]{3,2,1,0:T(8,128)(2,1)}) custom-call(bf16[2,256,256]{2,1,0:T(8,128)(2,1)S(1)} %add_convert_fusion.grad_ref, bf16[16,2,2,16,256]{4,3,2,1,0:T(8,128)(2,1)S(1)} %all-to-all-done.1.root_ref), custom_call_target="tpu_custom_call" | custom-call | tf_op jit(solution)/shard_map/precondition/pallas_call | solution.py:60
  53.3 2.4 %collective-permute-start.11 = (bf16[2,256,256]{2,1,0:T(8,128)(2,1)S(1)}, bf16[2,256,256]{2,1,0:T(8,128)(2,1)S(1)}, u32[]{:S(2)}, u32[]{:S(2)}) collective-permute-start(bf16[2,256,256]{2,1,0:T(8,128)(2,1)S(1)} %get-tuple-element.39), channel_id=1, source_target_pairs={{0,224},{32,0},{64,32},{96,64},{128,96},{160,128},{192,160},{224,1... | collective-permute-start | bytes 786440 | tf_op jit(solution)/shard_map/ppermute | solution.py:173
  55.7 4.9 %all-to-all-start.2 = ((bf16[16,2,16,256]{3,2,1,0:T(8,128)(2,1)}), bf16[16,2,16,256]{3,2,1,0:T(8,128)(2,1)S(1)}, u32[]{:S(2)}, u32[]{:S(2)}) async-start(bf16[16,2,16,256]{3,2,1,0:T(8,128)(2,1)} %get-tuple-element.38), calls=%async_computation.2 | async-start | bytes 524288 | tf_op jit(solution)/shard_map/all_to_all | solution.py:239
  60.6 0.1 select_reduce_fusion
  60.7 0.0 collective-permute-done.11
  60.7 2.9 %collective-permute-start.14 = (bf16[2,256,256]{2,1,0:T(8,128)(2,1)S(1)}, bf16[2,256,256]{2,1,0:T(8,128)(2,1)}, u32[]{:S(2)}, u32[]{:S(2)}) collective-permute-start(bf16[2,256,256]{2,1,0:T(8,128)(2,1)S(1)} %collective-permute-done.11), channel_id=1, source_target_pairs={{0,224},{32,0},{64,32},{96,64},{128,96},{160,128},{192,160},{224,1... | collective-permute-start | bytes 786440 | tf_op jit(solution)/shard_map/ppermute | solution.py:173
  63.7 4.3 %all-to-all-done.2 = bf16[16,2,16,256]{3,2,1,0:T(8,128)(2,1)S(1)} async-done(((bf16[16,2,16,256]{3,2,1,0:T(8,128)(2,1)}), bf16[16,2,16,256]{3,2,1,0:T(8,128)(2,1)S(1)}, u32[]{:S(2)}, u32[]{:S(2)}) %all-to-all-start.2) | async-done | bytes 262176 | tf_op jit(solution)/shard_map/all_to_all | solution.py:239
  67.9 1.5 %pick.3 = bf16[64,16,256]{2,1,0:T(8,128)(2,1)} custom-call(s32[64]{0:T(128)S(1)} %broadcast_add_fusion.source_ref, bf16[32,16,256]{2,1,0:T(8,128)(2,1)S(1)} %bitcast.77), custom_call_target="tpu_custom_call" | custom-call | tf_op jit(solution)/shard_map/pick/pallas_call | solution.py:37
  69.5 3.7 %all-to-all-start.3 = ((bf16[16,4,16,256]{3,2,1,0:T(8,128)(2,1)}), bf16[16,4,16,256]{3,2,1,0:T(8,128)(2,1)S(1)}, u32[]{:S(2)}, u32[]{:S(2)}) async-start(bf16[16,4,16,256]{3,2,1,0:T(8,128)(2,1)} %bitcast.28), calls=%async_computation.3 | async-start | bytes 1048576 | tf_op jit(solution)/shard_map/all_to_all | solution.py:253
  73.2 0.1 collective-permute-start.16
  73.3 2.7 %collective-permute-start.17 = (bf16[2,256,256]{2,1,0:T(8,128)(2,1)}, bf16[2,256,256]{2,1,0:T(8,128)(2,1)}, u32[]{:S(2)}, u32[]{:S(2)}) collective-permute-start(bf16[2,256,256]{2,1,0:T(8,128)(2,1)} %collective-permute-done.14), channel_id=1, source_target_pairs={{0,224},{32,0},{64,32},{96,64},{128,96},{160,128},{192,160},{224,1... | collective-permute-start | bytes 786440 | tf_op jit(solution)/shard_map/ppermute | solution.py:173
  76.0 0.1 pad_maximum_fusion.1.refs_0_
  76.0 6.8 %collective-permute-start.12 = (bf16[3,2,256,256]{3,2,1,0:T(8,128)(2,1)S(1)}, bf16[3,2,256,256]{3,2,1,0:T(8,128)(2,1)S(1)}, u32[]{:S(2)}, u32[]{:S(2)}) collective-permute-start(bf16[3,2,256,256]{3,2,1,0:T(8,128)(2,1)S(1)} %pad_maximum_fusion.1.refs_0_), channel_id=1, source_target_pairs={{0,16},{16,0},{1,17},{17,1},{2,18},{18,2},{3,19},{19,3},{4,20},{20... | collective-permute-start | bytes 2359304 | tf_op jit(solution)/shard_map/ppermute | solution.py:176
  82.8 1.1 %pad_maximum_fusion.2.refs_2_ = bf16[2,2,256,256]{3,2,1,0:T(8,128)(2,1)S(1)} fusion(bf16[1,2,256,256]{3,2,1,0:T(8,128)(2,1)} %bitcast.35, bf16[1,2,256,256]{3,2,1,0:T(8,128)(2,1)} %bitcast.34), kind=kLoop, calls=%fused_computation.3 | loop fusion | flops 262144 | bytes 1048576 | tf_op jit(solution)/shard_map/stack | solution.py:263
  83.9 0.1 collective-permute-start.15
  84.0 1.0 part.1
  85.0 5.4 %collective-permute-start.18 = (bf16[2,2,256,256]{3,2,1,0:T(8,128)(2,1)S(1)}, bf16[2,2,256,256]{3,2,1,0:T(8,128)(2,1)S(1)}, u32[]{:S(2)}, u32[]{:S(2)}) collective-permute-start(bf16[2,2,256,256]{3,2,1,0:T(8,128)(2,1)S(1)} %get-tuple-element.47.refs_4_), channel_id=1, source_target_pairs={{0,16},{16,0},{1,17},{17,1},{2,18},{18,2},{3,19},{19,3},{4,20},{20... | collective-permute-start | bytes 1572872 | tf_op jit(solution)/shard_map/ppermute | solution.py:176
  90.4 3.0 %collective-permute-start.20 = (bf16[1,256,256]{2,1,0:T(8,128)(2,1)S(1)}, bf16[1,256,256]{2,1,0:T(8,128)(2,1)S(1)}, u32[]{:S(2)}, u32[]{:S(2)}) collective-permute-start(bf16[1,256,256]{2,1,0:T(8,128)(2,1)S(1)} %get-tuple-element.49), channel_id=1, source_target_pairs={{0,224},{32,0},{64,32},{96,64},{128,96},{160,128},{192,160},{224,1... | collective-permute-start | bytes 393224 | tf_op jit(solution)/shard_map/ppermute | solution.py:173
  93.4 0.1 pad_add_fusion.where_ref
  93.4 4.2 %statistics.1 = (f32[4,256,256]{2,1,0:T(8,128)}, f32[4,256,256]{2,1,0:T(8,128)}) custom-call(bf16[16,4,16,256]{3,2,1,0:T(8,128)(2,1)S(1)} %all-to-all-done.3.own_ref, f32[4,256,256]{2,1,0:T(8,128)} %bitcast.86, f32[4,256,256]{2,1,0:T(8,128)} %bitcast.87), custom_call_target="tpu_custom_call" | custom-call | tf_op jit(solution)/shard_map/statistics/pallas_call | solution.py:106
  97.6 2.5 %place.2.refs_0_ = bf16[8,2,2,256,256]{4,3,2,1,0:T(8,128)(2,1)} custom-call(s32[2]{0:T(128)S(1)} %pad_add_fusion.where_ref, bf16[3,2,256,256]{3,2,1,0:T(8,128)(2,1)S(1)} %pad_maximum_fusion.1.refs_0_, bf16[3,2,256,256]{3,2,1,0:T(8,128)(2,1)S(1)} %collective-permute-done.12.refs_1_, bf16[2,2,256,256]{3,2,1,0:T(8,128)(2,1)S(1)} %pad_maximum_fusion.2.refs_2_, ...), custom_call_target="tpu_custom_call" | custom-call | tf_op jit(solution)/shard_map/place/pallas_call | solution.py:146
  100.2 0.5 collective-permute-start.21
  100.7 1.2 %collective-permute-done.21.refs_2_ = bf16[2,1,256,256]{3,2,1,0:T(8,128)(2,1)S(1)} collective-permute-done((bf16[2,1,256,256]{3,2,1,0:T(8,128)(2,1)S(1)}, bf16[2,1,256,256]{3,2,1,0:T(8,128)(2,1)S(1)}, u32[]{:S(2)}, u32[]{:S(2)}) %collective-permute-start.21) | collective-permute-done | bytes 262176 | tf_op jit(solution)/shard_map/ppermute | solution.py:176
  101.9 1.4 %place.3 = bf16[8,2,2,256,256]{4,3,2,1,0:T(8,128)(2,1)} custom-call(s32[2]{0:T(128)S(1)} %pad_add_fusion.where_ref, bf16[8,2,2,256,256]{4,3,2,1,0:T(8,128)(2,1)} %place.2.refs_0_, bf16[2,1,256,256]{3,2,1,0:T(8,128)(2,1)S(1)} %pad_maximum_fusion.3.refs_1_, bf16[2,1,256,256]{3,2,1,0:T(8,128)(2,1)S(1)} %collective-permute-done.21.refs_2_), custom_call_target="tpu_custom_call", output_to_operand_aliasing={{}: (1, {})} | custom-call | tf_op jit(solution)/shard_map/place/pallas_call | solution.py:146
  (28 shorter events, 0.2 us)
Async XLA Ops:
  0.6 6.9 %copy-start = (s32[512]{0:T(512)S(1)}, s32[512]{0:T(512)}, u32[]{:S(2)}) copy-start(s32[512]{0:T(512)} %param.11) | copy-start | bytes 6148
  1.7 5.1 %collective-permute-start = (bf16[2,256,256]{2,1,0:T(8,128)(2,1)S(1)}, bf16[2,256,256]{2,1,0:T(8,128)(2,1)S(1)}, u32[]{:S(2)}, u32[]{:S(2)}) collective-permute-start(bf16[2,256,256]{2,1,0:T(8,128)(2,1)S(1)} %get-tuple-element.60), channel_id=1, source_target_pairs={{0,16},{16,0},{1,17},{17,1},{2,18},{18,2},{3,19},{19,3},{4,20},{20... | collective-permute-start | bytes 786440 | tf_op jit(solution)/shard_map/ppermute | solution.py:176
  7.5 13.7 %collective-permute-start.2 = (bf16[8,2,256,256]{3,2,1,0:T(8,128)(2,1)S(1)}, bf16[8,2,256,256]{3,2,1,0:T(8,128)(2,1)}, u32[]{:S(2)}, u32[]{:S(2)}) collective-permute-start(bf16[8,2,256,256]{3,2,1,0:T(8,128)(2,1)S(1)} %dynamic-slice_bitcast_fusion), channel_id=1, source_target_pairs={{0,16},{16,0},{1,17},{17,1},{2,18},{18,2},{3,19},{19,3},{4,20},{20... | collective-permute-start | bytes 6291464 | tf_op jit(solution)/shard_map/ppermute | solution.py:176
  9.3 11.8 %collective-permute-start.4 = (bf16[1,256,256]{2,1,0:T(8,128)(2,1)}, bf16[1,256,256]{2,1,0:T(8,128)(2,1)S(1)}, u32[]{:S(2)}, u32[]{:S(2)}) collective-permute-start(bf16[1,256,256]{2,1,0:T(8,128)(2,1)} %get-tuple-element.61), channel_id=1, source_target_pairs={{0,224},{32,0},{64,32},{96,64},{128,96},{160,128},{192,160},{224,1... | collective-permute-start | bytes 393224 | tf_op jit(solution)/shard_map/ppermute | solution.py:173
  14.4 6.8 %collective-permute-start.1 = (bf16[1,256,256]{2,1,0:T(8,128)(2,1)S(1)}, bf16[1,256,256]{2,1,0:T(8,128)(2,1)S(1)}, u32[]{:S(2)}, u32[]{:S(2)}) collective-permute-start(bf16[1,256,256]{2,1,0:T(8,128)(2,1)S(1)} %get-tuple-element.62), channel_id=1, source_target_pairs={{0,32},{32,64},{64,96},{96,128},{128,160},{160,192},{192,224},{224... | collective-permute-start | bytes 393224 | tf_op jit(solution)/shard_map/ppermute | solution.py:173
  14.4 22.2 %all-to-all-start = ((bf16[16,4,2,16,256]{4,3,2,1,0:T(8,128)(2,1)}), bf16[16,4,2,16,256]{4,3,2,1,0:T(8,128)(2,1)S(1)}, u32[]{:S(2)}, u32[]{:S(2)}) async-start(bf16[16,4,2,16,256]{4,3,2,1,0:T(8,128)(2,1)} %bitcast.22), calls=%async_computation | async-start | bytes 2097152 | tf_op jit(solution)/shard_map/all_to_all | solution.py:218
  22.7 8.0 %collective-permute-start.3 = (bf16[2,256,256]{2,1,0:T(8,128)(2,1)S(1)}, bf16[2,256,256]{2,1,0:T(8,128)(2,1)S(1)}, u32[]{:S(2)}, u32[]{:S(2)}) collective-permute-start(bf16[2,256,256]{2,1,0:T(8,128)(2,1)S(1)} %add_convert_fusion.6), channel_id=1, source_target_pairs={{0,32},{32,64},{64,96},{96,128},{128,160},{160,192},{192,224},{224... | collective-permute-start | bytes 786440 | tf_op jit(solution)/shard_map/ppermute | solution.py:173
  22.9 8.0 %collective-permute-start.6 = (bf16[2,256,256]{2,1,0:T(8,128)(2,1)S(1)}, bf16[2,256,256]{2,1,0:T(8,128)(2,1)S(1)}, u32[]{:S(2)}, u32[]{:S(2)}) collective-permute-start(bf16[2,256,256]{2,1,0:T(8,128)(2,1)S(1)} %add_convert_fusion.5), channel_id=1, source_target_pairs={{0,224},{32,0},{64,32},{96,64},{128,96},{160,128},{192,160},{224,1... | collective-permute-start | bytes 786440 | tf_op jit(solution)/shard_map/ppermute | solution.py:173
  30.8 12.5 %collective-permute-start.5 = (bf16[2,256,256]{2,1,0:T(8,128)(2,1)S(1)}, bf16[2,256,256]{2,1,0:T(8,128)(2,1)S(1)}, u32[]{:S(2)}, u32[]{:S(2)}) collective-permute-start(bf16[2,256,256]{2,1,0:T(8,128)(2,1)S(1)} %add_convert_fusion.4), channel_id=1, source_target_pairs={{0,32},{32,64},{64,96},{96,128},{128,160},{160,192},{192,224},{224... | collective-permute-start | bytes 786440 | tf_op jit(solution)/shard_map/ppermute | solution.py:173
  31.0 12.5 %collective-permute-start.8 = (bf16[2,256,256]{2,1,0:T(8,128)(2,1)S(1)}, bf16[2,256,256]{2,1,0:T(8,128)(2,1)S(1)}, u32[]{:S(2)}, u32[]{:S(2)}) collective-permute-start(bf16[2,256,256]{2,1,0:T(8,128)(2,1)S(1)} %add_convert_fusion.3), channel_id=1, source_target_pairs={{0,224},{32,0},{64,32},{96,64},{128,96},{160,128},{192,160},{224,1... | collective-permute-start | bytes 786440 | tf_op jit(solution)/shard_map/ppermute | solution.py:173
  38.0 13.0 %all-to-all-start.1 = ((bf16[16,2,2,16,256]{4,3,2,1,0:T(8,128)(2,1)}), bf16[16,2,2,16,256]{4,3,2,1,0:T(8,128)(2,1)S(1)}, u32[]{:S(2)}, u32[]{:S(2)}) async-start(bf16[16,2,2,16,256]{4,3,2,1,0:T(8,128)(2,1)} %bitcast.24), calls=%async_computation.1 | async-start | bytes 1048576 | tf_op jit(solution)/shard_map/all_to_all | solution.py:231
  43.4 8.8 %collective-permute-start.7 = (bf16[2,256,256]{2,1,0:T(8,128)(2,1)S(1)}, bf16[2,256,256]{2,1,0:T(8,128)(2,1)S(1)}, u32[]{:S(2)}, u32[]{:S(2)}) collective-permute-start(bf16[2,256,256]{2,1,0:T(8,128)(2,1)S(1)} %add_convert_fusion.2), channel_id=1, source_target_pairs={{0,32},{32,64},{64,96},{96,128},{128,160},{160,192},{192,224},{224... | collective-permute-start | bytes 786440 | tf_op jit(solution)/shard_map/ppermute | solution.py:173
  43.5 8.6 %collective-permute-start.9 = (bf16[2,256,256]{2,1,0:T(8,128)(2,1)S(1)}, bf16[2,256,256]{2,1,0:T(8,128)(2,1)S(1)}, u32[]{:S(2)}, u32[]{:S(2)}) collective-permute-start(bf16[2,256,256]{2,1,0:T(8,128)(2,1)S(1)} %add_convert_fusion.1), channel_id=1, source_target_pairs={{0,224},{32,0},{64,32},{96,64},{128,96},{160,128},{192,160},{224,1... | collective-permute-start | bytes 786440 | tf_op jit(solution)/shard_map/ppermute | solution.py:173
  53.3 7.4 %collective-permute-start.11 = (bf16[2,256,256]{2,1,0:T(8,128)(2,1)S(1)}, bf16[2,256,256]{2,1,0:T(8,128)(2,1)S(1)}, u32[]{:S(2)}, u32[]{:S(2)}) collective-permute-start(bf16[2,256,256]{2,1,0:T(8,128)(2,1)S(1)} %get-tuple-element.39), channel_id=1, source_target_pairs={{0,224},{32,0},{64,32},{96,64},{128,96},{160,128},{192,160},{224,1... | collective-permute-start | bytes 786440 | tf_op jit(solution)/shard_map/ppermute | solution.py:173
  55.7 8.0 %collective-permute-start.10 = (bf16[2,256,256]{2,1,0:T(8,128)(2,1)S(1)}, bf16[2,256,256]{2,1,0:T(8,128)(2,1)S(1)}, u32[]{:S(2)}, u32[]{:S(2)}) collective-permute-start(bf16[2,256,256]{2,1,0:T(8,128)(2,1)S(1)} %get-tuple-element.39), channel_id=1, source_target_pairs={{0,32},{32,64},{64,96},{96,128},{128,160},{160,192},{192,224},{224... | collective-permute-start | bytes 786440 | tf_op jit(solution)/shard_map/ppermute | solution.py:173
  55.7 12.3 %all-to-all-start.2 = ((bf16[16,2,16,256]{3,2,1,0:T(8,128)(2,1)}), bf16[16,2,16,256]{3,2,1,0:T(8,128)(2,1)S(1)}, u32[]{:S(2)}, u32[]{:S(2)}) async-start(bf16[16,2,16,256]{3,2,1,0:T(8,128)(2,1)} %get-tuple-element.38), calls=%async_computation.2 | async-start | bytes 524288 | tf_op jit(solution)/shard_map/all_to_all | solution.py:239
  60.7 12.5 %collective-permute-start.14 = (bf16[2,256,256]{2,1,0:T(8,128)(2,1)S(1)}, bf16[2,256,256]{2,1,0:T(8,128)(2,1)}, u32[]{:S(2)}, u32[]{:S(2)}) collective-permute-start(bf16[2,256,256]{2,1,0:T(8,128)(2,1)S(1)} %collective-permute-done.11), channel_id=1, source_target_pairs={{0,224},{32,0},{64,32},{96,64},{128,96},{160,128},{192,160},{224,1... | collective-permute-start | bytes 786440 | tf_op jit(solution)/shard_map/ppermute | solution.py:173
  63.7 9.5 %collective-permute-start.13 = (bf16[2,256,256]{2,1,0:T(8,128)(2,1)S(1)}, bf16[2,256,256]{2,1,0:T(8,128)(2,1)}, u32[]{:S(2)}, u32[]{:S(2)}) collective-permute-start(bf16[2,256,256]{2,1,0:T(8,128)(2,1)S(1)} %collective-permute-done.10), channel_id=1, source_target_pairs={{0,32},{32,64},{64,96},{96,128},{128,160},{160,192},{192,224},{224... | collective-permute-start | bytes 786440 | tf_op jit(solution)/shard_map/ppermute | solution.py:173
  69.5 14.5 %all-to-all-start.3 = ((bf16[16,4,16,256]{3,2,1,0:T(8,128)(2,1)}), bf16[16,4,16,256]{3,2,1,0:T(8,128)(2,1)S(1)}, u32[]{:S(2)}, u32[]{:S(2)}) async-start(bf16[16,4,16,256]{3,2,1,0:T(8,128)(2,1)} %bitcast.28), calls=%async_computation.3 | async-start | bytes 1048576 | tf_op jit(solution)/shard_map/all_to_all | solution.py:253
  73.2 10.8 %collective-permute-start.16 = (bf16[2,256,256]{2,1,0:T(8,128)(2,1)}, bf16[2,256,256]{2,1,0:T(8,128)(2,1)S(1)}, u32[]{:S(2)}, u32[]{:S(2)}) collective-permute-start(bf16[2,256,256]{2,1,0:T(8,128)(2,1)} %collective-permute-done.13), channel_id=1, source_target_pairs={{0,32},{32,64},{64,96},{96,128},{128,160},{160,192},{192,224},{224... | collective-permute-start | bytes 786440 | tf_op jit(solution)/shard_map/ppermute | solution.py:173
  73.3 10.7 %collective-permute-start.17 = (bf16[2,256,256]{2,1,0:T(8,128)(2,1)}, bf16[2,256,256]{2,1,0:T(8,128)(2,1)}, u32[]{:S(2)}, u32[]{:S(2)}) collective-permute-start(bf16[2,256,256]{2,1,0:T(8,128)(2,1)} %collective-permute-done.14), channel_id=1, source_target_pairs={{0,224},{32,0},{64,32},{96,64},{128,96},{160,128},{192,160},{224,1... | collective-permute-start | bytes 786440 | tf_op jit(solution)/shard_map/ppermute | solution.py:173
  76.0 21.6 %collective-permute-start.12 = (bf16[3,2,256,256]{3,2,1,0:T(8,128)(2,1)S(1)}, bf16[3,2,256,256]{3,2,1,0:T(8,128)(2,1)S(1)}, u32[]{:S(2)}, u32[]{:S(2)}) collective-permute-start(bf16[3,2,256,256]{3,2,1,0:T(8,128)(2,1)S(1)} %pad_maximum_fusion.1.refs_0_), channel_id=1, source_target_pairs={{0,16},{16,0},{1,17},{17,1},{2,18},{18,2},{3,19},{19,3},{4,20},{20... | collective-permute-start | bytes 2359304 | tf_op jit(solution)/shard_map/ppermute | solution.py:176
  83.9 13.7 %collective-permute-start.15 = (bf16[2,2,256,256]{3,2,1,0:T(8,128)(2,1)S(1)}, bf16[2,2,256,256]{3,2,1,0:T(8,128)(2,1)S(1)}, u32[]{:S(2)}, u32[]{:S(2)}) collective-permute-start(bf16[2,2,256,256]{3,2,1,0:T(8,128)(2,1)S(1)} %pad_maximum_fusion.2.refs_2_), channel_id=1, source_target_pairs={{0,16},{16,0},{1,17},{17,1},{2,18},{18,2},{3,19},{19,3},{4,20},{20... | collective-permute-start | bytes 1572872 | tf_op jit(solution)/shard_map/ppermute | solution.py:176
  85.0 12.6 %collective-permute-start.18 = (bf16[2,2,256,256]{3,2,1,0:T(8,128)(2,1)S(1)}, bf16[2,2,256,256]{3,2,1,0:T(8,128)(2,1)S(1)}, u32[]{:S(2)}, u32[]{:S(2)}) collective-permute-start(bf16[2,2,256,256]{3,2,1,0:T(8,128)(2,1)S(1)} %get-tuple-element.47.refs_4_), channel_id=1, source_target_pairs={{0,16},{16,0},{1,17},{17,1},{2,18},{18,2},{3,19},{19,3},{4,20},{20... | collective-permute-start | bytes 1572872 | tf_op jit(solution)/shard_map/ppermute | solution.py:176
  90.4 9.7 %collective-permute-start.19 = (bf16[1,256,256]{2,1,0:T(8,128)(2,1)S(1)}, bf16[1,256,256]{2,1,0:T(8,128)(2,1)S(1)}, u32[]{:S(2)}, u32[]{:S(2)}) collective-permute-start(bf16[1,256,256]{2,1,0:T(8,128)(2,1)S(1)} %get-tuple-element.48), channel_id=1, source_target_pairs={{0,32},{32,64},{64,96},{96,128},{128,160},{160,192},{192,224},{224... | collective-permute-start | bytes 393224 | tf_op jit(solution)/shard_map/ppermute | solution.py:173
  90.4 9.7 %collective-permute-start.20 = (bf16[1,256,256]{2,1,0:T(8,128)(2,1)S(1)}, bf16[1,256,256]{2,1,0:T(8,128)(2,1)S(1)}, u32[]{:S(2)}, u32[]{:S(2)}) collective-permute-start(bf16[1,256,256]{2,1,0:T(8,128)(2,1)S(1)} %get-tuple-element.49), channel_id=1, source_target_pairs={{0,224},{32,0},{64,32},{96,64},{128,96},{160,128},{192,160},{224,1... | collective-permute-start | bytes 393224 | tf_op jit(solution)/shard_map/ppermute | solution.py:173
  100.2 1.7 %collective-permute-start.21 = (bf16[2,1,256,256]{3,2,1,0:T(8,128)(2,1)S(1)}, bf16[2,1,256,256]{3,2,1,0:T(8,128)(2,1)S(1)}, u32[]{:S(2)}, u32[]{:S(2)}) collective-permute-start(bf16[2,1,256,256]{3,2,1,0:T(8,128)(2,1)S(1)} %pad_maximum_fusion.3.refs_1_), channel_id=1, source_target_pairs={{0,16},{16,0},{1,17},{17,1},{2,18},{18,2},{3,19},{19,3},{4,20},{20... | collective-permute-start | bytes 786440 | tf_op jit(solution)/shard_map/ppermute | solution.py:176

commit v7 on v6

--- a/solution.py
+++ b/solution.py
@@ -211,10 +211,9 @@
     theirs = swap(tie(theirs, *moving))
     came = [hop(moving[way], way) for way in range(2)]
 
-    spread = jnp.stack([left_root[0, 0], right_root[0, 0]], axis=1).reshape(
-        slots, 2, mp, piece, cols
-    )
-    spread = jnp.moveaxis(tie(spread, *moving), 2, 0)
+    both = tie((left_root[0, 0], right_root[0, 0]), *moving)
+    spread = jnp.stack(both, axis=1).reshape(slots, 2, mp, piece, cols)
+    spread = jnp.moveaxis(spread, 2, 0)
     spread = lax.all_to_all(spread, "mp", 0, 0, tiled=True)
 
     first = jnp.arange(held)[:, None, None]

time: 104 us -> 103 us (level)
    another operation x1 -> x0, other arithmetic: 1.31 us -> none  [per_device(): jnp.stack([left_root[0, 0], right_root[0, 0]], axis=1)]
    transpose x0 -> x1, other arithmetic: none -> 1.13 us  [per_device(): spread = jnp.moveaxis(spread, 2, 0)]
    another operation x1 -> x0, local copies, waits for them, and re-layouts: 1.12 us -> none  [per_device(): jnp.stack([left_root[0, 0], right_root[0, 0]], axis=1)]
  transfers between devices with their start and end apart: 26 -> 26, of which waited for: 5 -> 5; matrix products, arithmetic and copies ran while one was open for 11% -> 10% of each run, Pallas kernels for 10% -> 10%
where the time goes in v7:
time: 103 us; the launch traced here: 102 us
  starting transfers between devices  58.8 us (57%)
  waiting for transfers between devices  16.9 us (16%)
  Pallas kernels  13.1 us (13%)
  other arithmetic  9 us (9%)
  local copies, waits for them, and re-layouts  3.15 us (3%)
  between operations  1.33 us (1%)
    ppermute x16, starting transfers between devices, hop(): return lax.ppermute(value, 'z', ways[way])  23.4 us
    ppermute x6, starting transfers between devices, swap(): return lax.ppermute(value, 'core', [(0, 1), (1, 0)])  16.1 us
    all_to_all x1, starting transfers between devices, per_device(): spread = lax.all_to_all(spread, 'mp', 0, 0, tiled=True)  6.75 us
    add x4, other arithmetic, base(): value = mine.reshape(held, rows, cols).astype(F32) + given.astype(F32)  5 us
    all_to_all x1, starting transfers between devices, per_device(): arrived = lax.all_to_all(sliced, 'mp', 0, 0, tiled=True)  4.92 us
    all_to_all x1, waiting for transfers between devices, per_device(): roots = lax.all_to_all(wanted, 'mp', 0, 0, tiled=True)  4.8 us
    all_to_all x1, waiting for transfers between devices, per_device(): arrived = lax.all_to_all(sliced, 'mp', 0, 0, tiled=True)  4.28 us
    pallas_call x1, Pallas kernels, statistics(): pl.pallas_call(statistics_kernel, grid=(slots,), out_shape=(jax.ShapeDtyp...  4.19 us
  transfers between devices with their start and end apart: 26, of which 5 were waited for; matrix products, arithmetic and copies ran while one was open for 10% of the time, Pallas kernels for 10%

profile of v7, /device:TPU:1, one launch (start us, length us, event | category | flops | bytes accessed | tf_op | source)
XLA Modules:
  0.0 102.3 jit_solution(3284792561103581057)
XLA Ops:
  0.7 1.2 %dynamic-slice_bitcast_fusion.2 = (bf16[2,256,256]{2,1,0:T(8,128)(2,1)S(1)}, bf16[2,256,256]{2,1,0:T(8,128)(2,1)S(1)}) fusion(bf16[8,2,2,256,256]{4,3,2,1,0:T(8,128)(2,1)} %bitcast.83, s32[]{:T(128)S(6)} %select_n.100, s32[]{:T(128)S(6)} %select_n.101, s32[]{:T(128)S(6)} %select_n.102), kind=kLoop, calls=%fused_computation.23 | loop fusion | bytes 1048588 | tf_op jit(solution)/shard_map/reshape | solution.py:192
  1.8 3.3 %collective-permute-start = (bf16[2,256,256]{2,1,0:T(8,128)(2,1)S(1)}, bf16[2,256,256]{2,1,0:T(8,128)(2,1)S(1)}, u32[]{:S(2)}, u32[]{:S(2)}) collective-permute-start(bf16[2,256,256]{2,1,0:T(8,128)(2,1)S(1)} %get-tuple-element.62), channel_id=1, source_target_pairs={{0,16},{16,0},{1,17},{17,1},{2,18},{18,2},{3,19},{19,3},{4,20},{20... | collective-permute-start | bytes 786440 | tf_op jit(solution)/shard_map/ppermute | solution.py:176
  5.2 1.7 %dynamic-slice_bitcast_fusion = bf16[8,2,256,256]{3,2,1,0:T(8,128)(2,1)S(1)} fusion(bf16[8,2,2,256,256]{4,3,2,1,0:T(8,128)(2,1)} %bitcast.84, s32[]{:T(128)S(6)} %select_n.102), kind=kLoop, calls=%fused_computation | loop fusion | bytes 4194308 | tf_op jit(solution)/shard_map/reshape | solution.py:205
  6.9 0.7 add_convert_fusion.7
  7.6 0.0 collective-permute-start.2
  7.7 0.1 reshape.108
  7.8 0.1 reshape.109
  8.0 0.2 convert_reduce_fusion
  8.2 3.9 %collective-permute-start.4 = (bf16[1,256,256]{2,1,0:T(8,128)(2,1)}, bf16[1,256,256]{2,1,0:T(8,128)(2,1)S(1)}, u32[]{:S(2)}, u32[]{:S(2)}) collective-permute-start(bf16[1,256,256]{2,1,0:T(8,128)(2,1)} %get-tuple-element.63), channel_id=1, source_target_pairs={{0,224},{32,0},{64,32},{96,64},{128,96},{160,128},{192,160},{224,1... | collective-permute-start | bytes 393224 | tf_op jit(solution)/shard_map/ppermute | solution.py:173
  12.1 0.0 collective-permute-start.1
  12.1 1.1 %copy_bitcast_fusion = bf16[16,4,2,16,256]{4,3,2,1,0:T(8,128)(2,1)} fusion(bf16[4,1,16,16,256]{4,3,2,0,1:T(8,128)(2,1)S(1)} %bitcast.91, bf16[4,1,16,16,256]{4,3,2,0,1:T(8,128)(2,1)S(1)} %bitcast.92), kind=kLoop, calls=%fused_computation.2 | loop fusion | flops 524288 | bytes 2097152 | tf_op jit(solution)/shard_map/transpose | solution.py:216
  13.3 6.8 %all-to-all-start = ((bf16[16,4,2,16,256]{4,3,2,1,0:T(8,128)(2,1)}), bf16[16,4,2,16,256]{4,3,2,1,0:T(8,128)(2,1)S(1)}, u32[]{:S(2)}, u32[]{:S(2)}) async-start(bf16[16,4,2,16,256]{4,3,2,1,0:T(8,128)(2,1)} %copy_bitcast_fusion), calls=%async_computation | async-start | bytes 2097152 | tf_op jit(solution)/shard_map/all_to_all | solution.py:217
  20.0 0.0 collective-permute-done.4
  20.1 0.0 collective-permute-done.1
  20.1 0.0 collective-permute-done.2
  20.1 1.3 %convert_add_fusion.5 = (f32[2,256,256]{2,1,0:T(8,128)S(1)}, f32[2,256,256]{2,1,0:T(8,128)S(1)}) fusion(bf16[8,2,256,256]{3,2,1,0:T(8,128)(2,1)} %collective-permute-done.2, s32[]{:T(128)S(6)} %select_n.109, bf16[8,2,2,256,256]{4,3,2,1,0:T(8,128)(2,1)} %bitcast.85, s32[]{:T(128)S(6)} %select_n.101, s32[]{:T(128)S(6)} %select_n.105), kind=kLoop, calls=%fused_computation.10 | loop fusion | flops 786432 | bytes 2097164 | tf_op jit(solution)/shard_map/add | solution.py:199
  21.4 0.1 add_convert_fusion.6
  21.6 0.1 collective-permute-start.3
  21.7 0.1 add_convert_fusion.5
  21.8 2.7 %collective-permute-start.6 = (bf16[2,256,256]{2,1,0:T(8,128)(2,1)S(1)}, bf16[2,256,256]{2,1,0:T(8,128)(2,1)S(1)}, u32[]{:S(2)}, u32[]{:S(2)}) collective-permute-start(bf16[2,256,256]{2,1,0:T(8,128)(2,1)S(1)} %add_convert_fusion.5), channel_id=1, source_target_pairs={{0,224},{32,0},{64,32},{96,64},{128,96},{160,128},{192,160},{224,1... | collective-permute-start | bytes 786440 | tf_op jit(solution)/shard_map/ppermute | solution.py:173
  24.5 1.3 %convert_add_fusion.3 = (f32[2,256,256]{2,1,0:T(8,128)S(1)}, f32[2,256,256]{2,1,0:T(8,128)S(1)}) fusion(bf16[8,2,256,256]{3,2,1,0:T(8,128)(2,1)} %collective-permute-done.2, s32[]{:T(128)S(6)} %select_n.113, bf16[8,2,2,256,256]{4,3,2,1,0:T(8,128)(2,1)} %bitcast.86, s32[]{:T(128)S(6)} %select_n.101, s32[]{:T(128)S(6)} %select_n.110), kind=kLoop, calls=%fused_computation.8 | loop fusion | flops 786432 | bytes 2097164 | tf_op jit(solution)/shard_map/add | solution.py:199
  25.8 3.8 %collective-permute-done.3 = bf16[2,256,256]{2,1,0:T(8,128)(2,1)S(1)} collective-permute-done((bf16[2,256,256]{2,1,0:T(8,128)(2,1)S(1)}, bf16[2,256,256]{2,1,0:T(8,128)(2,1)S(1)}, u32[]{:S(2)}, u32[]{:S(2)}) %collective-permute-start.3) | collective-permute-done | bytes 262176 | tf_op jit(solution)/shard_map/ppermute | solution.py:173
  29.6 0.1 add_convert_fusion.4
  29.7 0.1 collective-permute-start.5
  29.8 0.1 add_convert_fusion.3
  29.8 2.7 %collective-permute-start.8 = (bf16[2,256,256]{2,1,0:T(8,128)(2,1)S(1)}, bf16[2,256,256]{2,1,0:T(8,128)(2,1)S(1)}, u32[]{:S(2)}, u32[]{:S(2)}) collective-permute-start(bf16[2,256,256]{2,1,0:T(8,128)(2,1)S(1)} %add_convert_fusion.3), channel_id=1, source_target_pairs={{0,224},{32,0},{64,32},{96,64},{128,96},{160,128},{192,160},{224,1... | collective-permute-start | bytes 786440 | tf_op jit(solution)/shard_map/ppermute | solution.py:173
  32.6 2.9 %all-to-all-done = bf16[16,4,2,16,256]{4,3,2,1,0:T(8,128)(2,1)S(1)} async-done(((bf16[16,4,2,16,256]{4,3,2,1,0:T(8,128)(2,1)}), bf16[16,4,2,16,256]{4,3,2,1,0:T(8,128)(2,1)S(1)}, u32[]{:S(2)}, u32[]{:S(2)}) %all-to-all-start) | async-done | bytes 1048608 | tf_op jit(solution)/shard_map/all_to_all | solution.py:217
  35.4 1.4 %pick.2 = bf16[32,2,16,256]{3,2,1,0:T(8,128)(2,1)} custom-call(s32[32]{0:T(128)S(1)} %get-tuple-element.66.source_ref, bf16[64,2,16,256]{3,2,1,0:T(8,128)(2,1)S(1)} %bitcast.79), custom_call_target="tpu_custom_call" | custom-call | tf_op jit(solution)/shard_map/pick/pallas_call | solution.py:37
  36.9 3.9 %all-to-all-start.1 = ((bf16[16,2,2,16,256]{4,3,2,1,0:T(8,128)(2,1)}), bf16[16,2,2,16,256]{4,3,2,1,0:T(8,128)(2,1)S(1)}, u32[]{:S(2)}, u32[]{:S(2)}) async-start(bf16[16,2,2,16,256]{4,3,2,1,0:T(8,128)(2,1)} %bitcast.26), calls=%async_computation.1 | async-start | bytes 1048576 | tf_op jit(solution)/shard_map/all_to_all | solution.py:230
  40.8 1.3 %convert_add_fusion.1 = (f32[2,256,256]{2,1,0:T(8,128)S(1)}, f32[2,256,256]{2,1,0:T(8,128)S(1)}) fusion(bf16[8,2,256,256]{3,2,1,0:T(8,128)(2,1)} %collective-permute-done.2, s32[]{:T(128)S(6)} %select_n.116, bf16[8,2,2,256,256]{4,3,2,1,0:T(8,128)(2,1)} %bitcast.87, s32[]{:T(128)S(6)} %select_n.101, s32[]{:T(128)S(6)} %select_n.114), kind=kLoop, calls=%fused_computation.6 | loop fusion | flops 786432 | bytes 2097164 | tf_op jit(solution)/shard_map/add | solution.py:199
  42.2 0.1 add_convert_fusion.2
  42.2 0.1 collective-permute-start.7
  42.3 0.1 add_convert_fusion.1
  42.4 2.7 %collective-permute-start.9 = (bf16[2,256,256]{2,1,0:T(8,128)(2,1)S(1)}, bf16[2,256,256]{2,1,0:T(8,128)(2,1)S(1)}, u32[]{:S(2)}, u32[]{:S(2)}) collective-permute-start(bf16[2,256,256]{2,1,0:T(8,128)(2,1)S(1)} %add_convert_fusion.1), channel_id=1, source_target_pairs={{0,224},{32,0},{64,32},{96,64},{128,96},{160,128},{192,160},{224,1... | collective-permute-start | bytes 786440 | tf_op jit(solution)/shard_map/ppermute | solution.py:173
  45.1 4.8 %all-to-all-done.1.root_ref = bf16[16,2,2,16,256]{4,3,2,1,0:T(8,128)(2,1)S(1)} async-done(((bf16[16,2,2,16,256]{4,3,2,1,0:T(8,128)(2,1)}), bf16[16,2,2,16,256]{4,3,2,1,0:T(8,128)(2,1)S(1)}, u32[]{:S(2)}, u32[]{:S(2)}) %all-to-all-start.1) | async-done | bytes 524320 | tf_op jit(solution)/shard_map/all_to_all | solution.py:230
  49.9 1.1 %convert_add_fusion = f32[2,256,256]{2,1,0:T(8,128)S(1)} fusion(bf16[8,2,256,256]{3,2,1,0:T(8,128)(2,1)} %collective-permute-done.2, s32[]{:T(128)S(6)} %select_n.118, bf16[8,2,2,256,256]{4,3,2,1,0:T(8,128)(2,1)} %bitcast.88, s32[]{:T(128)S(6)} %select_n.101), kind=kLoop, calls=%fused_computation.5 | loop fusion | flops 393216 | bytes 1048584 | tf_op jit(solution)/shard_map/add | solution.py:199
  51.0 0.0 collective-permute-done.7
  51.0 0.1 add_convert_fusion.grad_ref
  51.1 1.0 %precondition.1 = (bf16[2,256,256]{2,1,0:T(8,128)(2,1)S(1)}, bf16[16,2,16,256]{3,2,1,0:T(8,128)(2,1)}) custom-call(bf16[2,256,256]{2,1,0:T(8,128)(2,1)S(1)} %add_convert_fusion.grad_ref, bf16[16,2,2,16,256]{4,3,2,1,0:T(8,128)(2,1)S(1)} %all-to-all-done.1.root_ref), custom_call_target="tpu_custom_call" | custom-call | tf_op jit(solution)/shard_map/precondition/pallas_call | solution.py:60
  52.2 2.4 %collective-permute-start.11 = (bf16[2,256,256]{2,1,0:T(8,128)(2,1)S(1)}, bf16[2,256,256]{2,1,0:T(8,128)(2,1)S(1)}, u32[]{:S(2)}, u32[]{:S(2)}) collective-permute-start(bf16[2,256,256]{2,1,0:T(8,128)(2,1)S(1)} %get-tuple-element.41), channel_id=1, source_target_pairs={{0,224},{32,0},{64,32},{96,64},{128,96},{160,128},{192,160},{224,1... | collective-permute-start | bytes 786440 | tf_op jit(solution)/shard_map/ppermute | solution.py:173
  54.5 0.0 collective-permute-start.10
  54.5 4.9 %all-to-all-start.2 = ((bf16[16,2,16,256]{3,2,1,0:T(8,128)(2,1)}), bf16[16,2,16,256]{3,2,1,0:T(8,128)(2,1)S(1)}, u32[]{:S(2)}, u32[]{:S(2)}) async-start(bf16[16,2,16,256]{3,2,1,0:T(8,128)(2,1)} %get-tuple-element.40), calls=%async_computation.2 | async-start | bytes 524288 | tf_op jit(solution)/shard_map/all_to_all | solution.py:238
  59.5 0.1 select_reduce_fusion
  59.6 2.9 %collective-permute-start.14 = (bf16[2,256,256]{2,1,0:T(8,128)(2,1)S(1)}, bf16[2,256,256]{2,1,0:T(8,128)(2,1)}, u32[]{:S(2)}, u32[]{:S(2)}) collective-permute-start(bf16[2,256,256]{2,1,0:T(8,128)(2,1)S(1)} %collective-permute-done.11), channel_id=1, source_target_pairs={{0,224},{32,0},{64,32},{96,64},{128,96},{160,128},{192,160},{224,1... | collective-permute-start | bytes 786440 | tf_op jit(solution)/shard_map/ppermute | solution.py:173
  62.5 0.0 collective-permute-done.10
  62.5 0.0 collective-permute-start.13
  62.5 4.3 %all-to-all-done.2 = bf16[16,2,16,256]{3,2,1,0:T(8,128)(2,1)S(1)} async-done(((bf16[16,2,16,256]{3,2,1,0:T(8,128)(2,1)}), bf16[16,2,16,256]{3,2,1,0:T(8,128)(2,1)S(1)}, u32[]{:S(2)}, u32[]{:S(2)}) %all-to-all-start.2) | async-done | bytes 262176 | tf_op jit(solution)/shard_map/all_to_all | solution.py:238
  66.8 1.5 %pick.3 = bf16[64,16,256]{2,1,0:T(8,128)(2,1)} custom-call(s32[64]{0:T(128)S(1)} %broadcast_add_fusion.source_ref, bf16[32,16,256]{2,1,0:T(8,128)(2,1)S(1)} %bitcast.80), custom_call_target="tpu_custom_call" | custom-call | tf_op jit(solution)/shard_map/pick/pallas_call | solution.py:37
  68.3 3.7 %all-to-all-start.3 = ((bf16[16,4,16,256]{3,2,1,0:T(8,128)(2,1)}), bf16[16,4,16,256]{3,2,1,0:T(8,128)(2,1)S(1)}, u32[]{:S(2)}, u32[]{:S(2)}) async-start(bf16[16,4,16,256]{3,2,1,0:T(8,128)(2,1)} %bitcast.30), calls=%async_computation.3 | async-start | bytes 1048576 | tf_op jit(solution)/shard_map/all_to_all | solution.py:252
  72.0 0.1 collective-permute-start.16
  72.1 2.7 %collective-permute-start.17 = (bf16[2,256,256]{2,1,0:T(8,128)(2,1)}, bf16[2,256,256]{2,1,0:T(8,128)(2,1)}, u32[]{:S(2)}, u32[]{:S(2)}) collective-permute-start(bf16[2,256,256]{2,1,0:T(8,128)(2,1)} %collective-permute-done.14), channel_id=1, source_target_pairs={{0,224},{32,0},{64,32},{96,64},{128,96},{160,128},{192,160},{224,1... | collective-permute-start | bytes 786440 | tf_op jit(solution)/shard_map/ppermute | solution.py:173
  74.8 0.1 pad_maximum_fusion.1.refs_0_
  74.9 6.8 %collective-permute-start.12 = (bf16[3,2,256,256]{3,2,1,0:T(8,128)(2,1)S(1)}, bf16[3,2,256,256]{3,2,1,0:T(8,128)(2,1)S(1)}, u32[]{:S(2)}, u32[]{:S(2)}) collective-permute-start(bf16[3,2,256,256]{3,2,1,0:T(8,128)(2,1)S(1)} %pad_maximum_fusion.1.refs_0_), channel_id=1, source_target_pairs={{0,16},{16,0},{1,17},{17,1},{2,18},{18,2},{3,19},{19,3},{4,20},{20... | collective-permute-start | bytes 2359304 | tf_op jit(solution)/shard_map/ppermute | solution.py:176
  81.6 1.1 %pad_maximum_fusion.2.refs_2_ = bf16[2,2,256,256]{3,2,1,0:T(8,128)(2,1)S(1)} fusion(bf16[1,2,256,256]{3,2,1,0:T(8,128)(2,1)} %bitcast.37, bf16[1,2,256,256]{3,2,1,0:T(8,128)(2,1)} %bitcast.36), kind=kLoop, calls=%fused_computation.4 | loop fusion | flops 262144 | bytes 1048576 | tf_op jit(solution)/shard_map/stack | solution.py:262
  82.7 0.1 collective-permute-start.15
  82.9 1.0 part.1
  83.9 5.4 %collective-permute-start.18 = (bf16[2,2,256,256]{3,2,1,0:T(8,128)(2,1)S(1)}, bf16[2,2,256,256]{3,2,1,0:T(8,128)(2,1)S(1)}, u32[]{:S(2)}, u32[]{:S(2)}) collective-permute-start(bf16[2,2,256,256]{3,2,1,0:T(8,128)(2,1)S(1)} %get-tuple-element.49.refs_4_), channel_id=1, source_target_pairs={{0,16},{16,0},{1,17},{17,1},{2,18},{18,2},{3,19},{19,3},{4,20},{20... | collective-permute-start | bytes 1572872 | tf_op jit(solution)/shard_map/ppermute | solution.py:176
  89.2 3.0 %collective-permute-start.20 = (bf16[1,256,256]{2,1,0:T(8,128)(2,1)S(1)}, bf16[1,256,256]{2,1,0:T(8,128)(2,1)S(1)}, u32[]{:S(2)}, u32[]{:S(2)}) collective-permute-start(bf16[1,256,256]{2,1,0:T(8,128)(2,1)S(1)} %get-tuple-element.51), channel_id=1, source_target_pairs={{0,224},{32,0},{64,32},{96,64},{128,96},{160,128},{192,160},{224,1... | collective-permute-start | bytes 393224 | tf_op jit(solution)/shard_map/ppermute | solution.py:173
  92.2 0.1 pad_add_fusion.where_ref
  92.3 4.2 %statistics.1 = (f32[4,256,256]{2,1,0:T(8,128)}, f32[4,256,256]{2,1,0:T(8,128)}) custom-call(bf16[16,4,16,256]{3,2,1,0:T(8,128)(2,1)S(1)} %all-to-all-done.3.own_ref, f32[4,256,256]{2,1,0:T(8,128)} %bitcast.89, f32[4,256,256]{2,1,0:T(8,128)} %bitcast.90), custom_call_target="tpu_custom_call" | custom-call | tf_op jit(solution)/shard_map/statistics/pallas_call | solution.py:106
  96.5 2.5 %place.2.refs_0_ = bf16[8,2,2,256,256]{4,3,2,1,0:T(8,128)(2,1)} custom-call(s32[2]{0:T(128)S(1)} %pad_add_fusion.where_ref, bf16[3,2,256,256]{3,2,1,0:T(8,128)(2,1)S(1)} %pad_maximum_fusion.1.refs_0_, bf16[3,2,256,256]{3,2,1,0:T(8,128)(2,1)S(1)} %collective-permute-done.12.refs_1_, bf16[2,2,256,256]{3,2,1,0:T(8,128)(2,1)S(1)} %pad_maximum_fusion.2.refs_2_, ...), custom_call_target="tpu_custom_call" | custom-call | tf_op jit(solution)/shard_map/place/pallas_call | solution.py:146
  99.0 0.5 collective-permute-start.21
  99.6 1.2 %collective-permute-done.21.refs_2_ = bf16[2,1,256,256]{3,2,1,0:T(8,128)(2,1)S(1)} collective-permute-done((bf16[2,1,256,256]{3,2,1,0:T(8,128)(2,1)S(1)}, bf16[2,1,256,256]{3,2,1,0:T(8,128)(2,1)S(1)}, u32[]{:S(2)}, u32[]{:S(2)}) %collective-permute-start.21) | collective-permute-done | bytes 262176 | tf_op jit(solution)/shard_map/ppermute | solution.py:176
  100.7 1.4 %place.3 = bf16[8,2,2,256,256]{4,3,2,1,0:T(8,128)(2,1)} custom-call(s32[2]{0:T(128)S(1)} %pad_add_fusion.where_ref, bf16[8,2,2,256,256]{4,3,2,1,0:T(8,128)(2,1)} %place.2.refs_0_, bf16[2,1,256,256]{3,2,1,0:T(8,128)(2,1)S(1)} %pad_maximum_fusion.3.refs_1_, bf16[2,1,256,256]{3,2,1,0:T(8,128)(2,1)S(1)} %collective-permute-done.21.refs_2_), custom_call_target="tpu_custom_call", output_to_operand_aliasing={{}: (1, {})} | custom-call | tf_op jit(solution)/shard_map/place/pallas_call | solution.py:146
  (31 shorter events, 0.2 us)
Async XLA Ops:
  0.6 7.0 %copy-start.2 = (s32[512]{0:T(512)S(1)}, s32[512]{0:T(512)}, u32[]{:S(2)}) copy-start(s32[512]{0:T(512)} %param.11) | copy-start | bytes 6148
  0.6 11.5 %copy-start = (bf16[1,1,4,256,256]{4,3,2,1,0:T(8,128)(2,1)S(1)}, bf16[1,1,4,256,256]{4,3,2,1,0:T(8,128)(2,1)}, u32[]{:S(2)}) copy-start(bf16[1,1,4,256,256]{4,3,2,1,0:T(8,128)(2,1)} %param.10) | copy-start | bytes 1572868
  0.7 11.5 %copy-start.1 = (bf16[1,1,4,256,256]{4,3,2,1,0:T(8,128)(2,1)S(1)}, bf16[1,1,4,256,256]{4,3,2,1,0:T(8,128)(2,1)}, u32[]{:S(2)}) copy-start(bf16[1,1,4,256,256]{4,3,2,1,0:T(8,128)(2,1)} %param.9) | copy-start | bytes 1572868
  1.8 5.1 %collective-permute-start = (bf16[2,256,256]{2,1,0:T(8,128)(2,1)S(1)}, bf16[2,256,256]{2,1,0:T(8,128)(2,1)S(1)}, u32[]{:S(2)}, u32[]{:S(2)}) collective-permute-start(bf16[2,256,256]{2,1,0:T(8,128)(2,1)S(1)} %get-tuple-element.62), channel_id=1, source_target_pairs={{0,16},{16,0},{1,17},{17,1},{2,18},{18,2},{3,19},{19,3},{4,20},{20... | collective-permute-start | bytes 786440 | tf_op jit(solution)/shard_map/ppermute | solution.py:176
  7.6 12.5 %collective-permute-start.2 = (bf16[8,2,256,256]{3,2,1,0:T(8,128)(2,1)S(1)}, bf16[8,2,256,256]{3,2,1,0:T(8,128)(2,1)}, u32[]{:S(2)}, u32[]{:S(2)}) collective-permute-start(bf16[8,2,256,256]{3,2,1,0:T(8,128)(2,1)S(1)} %dynamic-slice_bitcast_fusion), channel_id=1, source_target_pairs={{0,16},{16,0},{1,17},{17,1},{2,18},{18,2},{3,19},{19,3},{4,20},{20... | collective-permute-start | bytes 6291464 | tf_op jit(solution)/shard_map/ppermute | solution.py:176
  8.2 11.8 %collective-permute-start.4 = (bf16[1,256,256]{2,1,0:T(8,128)(2,1)}, bf16[1,256,256]{2,1,0:T(8,128)(2,1)S(1)}, u32[]{:S(2)}, u32[]{:S(2)}) collective-permute-start(bf16[1,256,256]{2,1,0:T(8,128)(2,1)} %get-tuple-element.63), channel_id=1, source_target_pairs={{0,224},{32,0},{64,32},{96,64},{128,96},{160,128},{192,160},{224,1... | collective-permute-start | bytes 393224 | tf_op jit(solution)/shard_map/ppermute | solution.py:173
  12.1 8.0 %collective-permute-start.1 = (bf16[1,256,256]{2,1,0:T(8,128)(2,1)S(1)}, bf16[1,256,256]{2,1,0:T(8,128)(2,1)S(1)}, u32[]{:S(2)}, u32[]{:S(2)}) collective-permute-start(bf16[1,256,256]{2,1,0:T(8,128)(2,1)S(1)} %get-tuple-element.64), channel_id=1, source_target_pairs={{0,32},{32,64},{64,96},{96,128},{128,160},{160,192},{192,224},{224... | collective-permute-start | bytes 393224 | tf_op jit(solution)/shard_map/ppermute | solution.py:173
  13.3 22.2 %all-to-all-start = ((bf16[16,4,2,16,256]{4,3,2,1,0:T(8,128)(2,1)}), bf16[16,4,2,16,256]{4,3,2,1,0:T(8,128)(2,1)S(1)}, u32[]{:S(2)}, u32[]{:S(2)}) async-start(bf16[16,4,2,16,256]{4,3,2,1,0:T(8,128)(2,1)} %copy_bitcast_fusion), calls=%async_computation | async-start | bytes 2097152 | tf_op jit(solution)/shard_map/all_to_all | solution.py:217
  21.6 8.0 %collective-permute-start.3 = (bf16[2,256,256]{2,1,0:T(8,128)(2,1)S(1)}, bf16[2,256,256]{2,1,0:T(8,128)(2,1)S(1)}, u32[]{:S(2)}, u32[]{:S(2)}) collective-permute-start(bf16[2,256,256]{2,1,0:T(8,128)(2,1)S(1)} %add_convert_fusion.6), channel_id=1, source_target_pairs={{0,32},{32,64},{64,96},{96,128},{128,160},{160,192},{192,224},{224... | collective-permute-start | bytes 786440 | tf_op jit(solution)/shard_map/ppermute | solution.py:173
  21.8 8.0 %collective-permute-start.6 = (bf16[2,256,256]{2,1,0:T(8,128)(2,1)S(1)}, bf16[2,256,256]{2,1,0:T(8,128)(2,1)S(1)}, u32[]{:S(2)}, u32[]{:S(2)}) collective-permute-start(bf16[2,256,256]{2,1,0:T(8,128)(2,1)S(1)} %add_convert_fusion.5), channel_id=1, source_target_pairs={{0,224},{32,0},{64,32},{96,64},{128,96},{160,128},{192,160},{224,1... | collective-permute-start | bytes 786440 | tf_op jit(solution)/shard_map/ppermute | solution.py:173
  29.7 12.5 %collective-permute-start.5 = (bf16[2,256,256]{2,1,0:T(8,128)(2,1)S(1)}, bf16[2,256,256]{2,1,0:T(8,128)(2,1)S(1)}, u32[]{:S(2)}, u32[]{:S(2)}) collective-permute-start(bf16[2,256,256]{2,1,0:T(8,128)(2,1)S(1)} %add_convert_fusion.4), channel_id=1, source_target_pairs={{0,32},{32,64},{64,96},{96,128},{128,160},{160,192},{192,224},{224... | collective-permute-start | bytes 786440 | tf_op jit(solution)/shard_map/ppermute | solution.py:173
  29.8 12.5 %collective-permute-start.8 = (bf16[2,256,256]{2,1,0:T(8,128)(2,1)S(1)}, bf16[2,256,256]{2,1,0:T(8,128)(2,1)S(1)}, u32[]{:S(2)}, u32[]{:S(2)}) collective-permute-start(bf16[2,256,256]{2,1,0:T(8,128)(2,1)S(1)} %add_convert_fusion.3), channel_id=1, source_target_pairs={{0,224},{32,0},{64,32},{96,64},{128,96},{160,128},{192,160},{224,1... | collective-permute-start | bytes 786440 | tf_op jit(solution)/shard_map/ppermute | solution.py:173
  36.9 13.0 %all-to-all-start.1 = ((bf16[16,2,2,16,256]{4,3,2,1,0:T(8,128)(2,1)}), bf16[16,2,2,16,256]{4,3,2,1,0:T(8,128)(2,1)S(1)}, u32[]{:S(2)}, u32[]{:S(2)}) async-start(bf16[16,2,2,16,256]{4,3,2,1,0:T(8,128)(2,1)} %bitcast.26), calls=%async_computation.1 | async-start | bytes 1048576 | tf_op jit(solution)/shard_map/all_to_all | solution.py:230
  42.2 8.8 %collective-permute-start.7 = (bf16[2,256,256]{2,1,0:T(8,128)(2,1)S(1)}, bf16[2,256,256]{2,1,0:T(8,128)(2,1)S(1)}, u32[]{:S(2)}, u32[]{:S(2)}) collective-permute-start(bf16[2,256,256]{2,1,0:T(8,128)(2,1)S(1)} %add_convert_fusion.2), channel_id=1, source_target_pairs={{0,32},{32,64},{64,96},{96,128},{128,160},{160,192},{192,224},{224... | collective-permute-start | bytes 786440 | tf_op jit(solution)/shard_map/ppermute | solution.py:173
  42.4 8.6 %collective-permute-start.9 = (bf16[2,256,256]{2,1,0:T(8,128)(2,1)S(1)}, bf16[2,256,256]{2,1,0:T(8,128)(2,1)S(1)}, u32[]{:S(2)}, u32[]{:S(2)}) collective-permute-start(bf16[2,256,256]{2,1,0:T(8,128)(2,1)S(1)} %add_convert_fusion.1), channel_id=1, source_target_pairs={{0,224},{32,0},{64,32},{96,64},{128,96},{160,128},{192,160},{224,1... | collective-permute-start | bytes 786440 | tf_op jit(solution)/shard_map/ppermute | solution.py:173
  52.2 7.4 %collective-permute-start.11 = (bf16[2,256,256]{2,1,0:T(8,128)(2,1)S(1)}, bf16[2,256,256]{2,1,0:T(8,128)(2,1)S(1)}, u32[]{:S(2)}, u32[]{:S(2)}) collective-permute-start(bf16[2,256,256]{2,1,0:T(8,128)(2,1)S(1)} %get-tuple-element.41), channel_id=1, source_target_pairs={{0,224},{32,0},{64,32},{96,64},{128,96},{160,128},{192,160},{224,1... | collective-permute-start | bytes 786440 | tf_op jit(solution)/shard_map/ppermute | solution.py:173
  54.5 8.0 %collective-permute-start.10 = (bf16[2,256,256]{2,1,0:T(8,128)(2,1)S(1)}, bf16[2,256,256]{2,1,0:T(8,128)(2,1)S(1)}, u32[]{:S(2)}, u32[]{:S(2)}) collective-permute-start(bf16[2,256,256]{2,1,0:T(8,128)(2,1)S(1)} %get-tuple-element.41), channel_id=1, source_target_pairs={{0,32},{32,64},{64,96},{96,128},{128,160},{160,192},{192,224},{224... | collective-permute-start | bytes 786440 | tf_op jit(solution)/shard_map/ppermute | solution.py:173
  54.5 12.2 %all-to-all-start.2 = ((bf16[16,2,16,256]{3,2,1,0:T(8,128)(2,1)}), bf16[16,2,16,256]{3,2,1,0:T(8,128)(2,1)S(1)}, u32[]{:S(2)}, u32[]{:S(2)}) async-start(bf16[16,2,16,256]{3,2,1,0:T(8,128)(2,1)} %get-tuple-element.40), calls=%async_computation.2 | async-start | bytes 524288 | tf_op jit(solution)/shard_map/all_to_all | solution.py:238
  59.6 12.5 %collective-permute-start.14 = (bf16[2,256,256]{2,1,0:T(8,128)(2,1)S(1)}, bf16[2,256,256]{2,1,0:T(8,128)(2,1)}, u32[]{:S(2)}, u32[]{:S(2)}) collective-permute-start(bf16[2,256,256]{2,1,0:T(8,128)(2,1)S(1)} %collective-permute-done.11), channel_id=1, source_target_pairs={{0,224},{32,0},{64,32},{96,64},{128,96},{160,128},{192,160},{224,1... | collective-permute-start | bytes 786440 | tf_op jit(solution)/shard_map/ppermute | solution.py:173
  62.5 9.5 %collective-permute-start.13 = (bf16[2,256,256]{2,1,0:T(8,128)(2,1)S(1)}, bf16[2,256,256]{2,1,0:T(8,128)(2,1)}, u32[]{:S(2)}, u32[]{:S(2)}) collective-permute-start(bf16[2,256,256]{2,1,0:T(8,128)(2,1)S(1)} %collective-permute-done.10), channel_id=1, source_target_pairs={{0,32},{32,64},{64,96},{96,128},{128,160},{160,192},{192,224},{224... | collective-permute-start | bytes 786440 | tf_op jit(solution)/shard_map/ppermute | solution.py:173
  68.3 14.5 %all-to-all-start.3 = ((bf16[16,4,16,256]{3,2,1,0:T(8,128)(2,1)}), bf16[16,4,16,256]{3,2,1,0:T(8,128)(2,1)S(1)}, u32[]{:S(2)}, u32[]{:S(2)}) async-start(bf16[16,4,16,256]{3,2,1,0:T(8,128)(2,1)} %bitcast.30), calls=%async_computation.3 | async-start | bytes 1048576 | tf_op jit(solution)/shard_map/all_to_all | solution.py:252
  72.0 10.8 %collective-permute-start.16 = (bf16[2,256,256]{2,1,0:T(8,128)(2,1)}, bf16[2,256,256]{2,1,0:T(8,128)(2,1)S(1)}, u32[]{:S(2)}, u32[]{:S(2)}) collective-permute-start(bf16[2,256,256]{2,1,0:T(8,128)(2,1)} %collective-permute-done.13), channel_id=1, source_target_pairs={{0,32},{32,64},{64,96},{96,128},{128,160},{160,192},{192,224},{224... | collective-permute-start | bytes 786440 | tf_op jit(solution)/shard_map/ppermute | solution.py:173
  72.1 10.7 %collective-permute-start.17 = (bf16[2,256,256]{2,1,0:T(8,128)(2,1)}, bf16[2,256,256]{2,1,0:T(8,128)(2,1)}, u32[]{:S(2)}, u32[]{:S(2)}) collective-permute-start(bf16[2,256,256]{2,1,0:T(8,128)(2,1)} %collective-permute-done.14), channel_id=1, source_target_pairs={{0,224},{32,0},{64,32},{96,64},{128,96},{160,128},{192,160},{224,1... | collective-permute-start | bytes 786440 | tf_op jit(solution)/shard_map/ppermute | solution.py:173
  74.9 21.6 %collective-permute-start.12 = (bf16[3,2,256,256]{3,2,1,0:T(8,128)(2,1)S(1)}, bf16[3,2,256,256]{3,2,1,0:T(8,128)(2,1)S(1)}, u32[]{:S(2)}, u32[]{:S(2)}) collective-permute-start(bf16[3,2,256,256]{3,2,1,0:T(8,128)(2,1)S(1)} %pad_maximum_fusion.1.refs_0_), channel_id=1, source_target_pairs={{0,16},{16,0},{1,17},{17,1},{2,18},{18,2},{3,19},{19,3},{4,20},{20... | collective-permute-start | bytes 2359304 | tf_op jit(solution)/shard_map/ppermute | solution.py:176
  82.7 13.7 %collective-permute-start.15 = (bf16[2,2,256,256]{3,2,1,0:T(8,128)(2,1)S(1)}, bf16[2,2,256,256]{3,2,1,0:T(8,128)(2,1)S(1)}, u32[]{:S(2)}, u32[]{:S(2)}) collective-permute-start(bf16[2,2,256,256]{3,2,1,0:T(8,128)(2,1)S(1)} %pad_maximum_fusion.2.refs_2_), channel_id=1, source_target_pairs={{0,16},{16,0},{1,17},{17,1},{2,18},{18,2},{3,19},{19,3},{4,20},{20... | collective-permute-start | bytes 1572872 | tf_op jit(solution)/shard_map/ppermute | solution.py:176
  83.9 12.6 %collective-permute-start.18 = (bf16[2,2,256,256]{3,2,1,0:T(8,128)(2,1)S(1)}, bf16[2,2,256,256]{3,2,1,0:T(8,128)(2,1)S(1)}, u32[]{:S(2)}, u32[]{:S(2)}) collective-permute-start(bf16[2,2,256,256]{3,2,1,0:T(8,128)(2,1)S(1)} %get-tuple-element.49.refs_4_), channel_id=1, source_target_pairs={{0,16},{16,0},{1,17},{17,1},{2,18},{18,2},{3,19},{19,3},{4,20},{20... | collective-permute-start | bytes 1572872 | tf_op jit(solution)/shard_map/ppermute | solution.py:176
  89.2 9.7 %collective-permute-start.19 = (bf16[1,256,256]{2,1,0:T(8,128)(2,1)S(1)}, bf16[1,256,256]{2,1,0:T(8,128)(2,1)S(1)}, u32[]{:S(2)}, u32[]{:S(2)}) collective-permute-start(bf16[1,256,256]{2,1,0:T(8,128)(2,1)S(1)} %get-tuple-element.50), channel_id=1, source_target_pairs={{0,32},{32,64},{64,96},{96,128},{128,160},{160,192},{192,224},{224... | collective-permute-start | bytes 393224 | tf_op jit(solution)/shard_map/ppermute | solution.py:173
  89.2 9.7 %collective-permute-start.20 = (bf16[1,256,256]{2,1,0:T(8,128)(2,1)S(1)}, bf16[1,256,256]{2,1,0:T(8,128)(2,1)S(1)}, u32[]{:S(2)}, u32[]{:S(2)}) collective-permute-start(bf16[1,256,256]{2,1,0:T(8,128)(2,1)S(1)} %get-tuple-element.51), channel_id=1, source_target_pairs={{0,224},{32,0},{64,32},{96,64},{128,96},{160,128},{192,160},{224,1... | collective-permute-start | bytes 393224 | tf_op jit(solution)/shard_map/ppermute | solution.py:173
  99.0 1.7 %collective-permute-start.21 = (bf16[2,1,256,256]{3,2,1,0:T(8,128)(2,1)S(1)}, bf16[2,1,256,256]{3,2,1,0:T(8,128)(2,1)S(1)}, u32[]{:S(2)}, u32[]{:S(2)}) collective-permute-start(bf16[2,1,256,256]{3,2,1,0:T(8,128)(2,1)S(1)} %pad_maximum_fusion.3.refs_1_), channel_id=1, source_target_pairs={{0,16},{16,0},{1,17},{17,1},{2,18},{18,2},{3,19},{19,3},{4,20},{20... | collective-permute-start | bytes 786440 | tf_op jit(solution)/shard_map/ppermute | solution.py:176
